TPU v7x, 32 devices: a whole 2x2x4 slice. The times are simulated.
32 devices in a mesh: section: 4 (over x, core), expert: 8 (over z, y).
Axes of the slice: x: 2, y: 2, z: 4, core: 2. Of those that a mesh axis runs over, the one named last changes fastest.
Arguments:
- layer_input: bfloat16 [2, 4, 1024, 2048], P(None, 'section', 'expert'), may hold values from -48 to 48
- entering: bfloat16 [4, 1024, 2048], P('section', 'expert'), may hold values from -6 to 6
- fresh: bfloat16 [1, 1024, 2048], P(None, 'expert'), may hold values from -6 to 6
- routes: int32 [2, 4, 1024, 2], P(None, 'section', 'expert'), may hold values from 0 to 7, all different within a row; in each aligned block of 128 rows (0 to 127, 128 to 255, ..., all dimensions but the last counted through in order) at most 48 rows name the same one
- gate_weights: bfloat16 [2, 4, 1024, 2], P(None, 'section', 'expert'), may hold values from 0.019897461 to 0.5
- norm_gain: float32 [4, 2048], P('section'), may hold values from 0.3 to 3
- w_gate: bfloat16 [4, 8, 2048, 768], P('section', 'expert'), may hold values from -0.125 to 0.125
- w_up: bfloat16 [4, 8, 2048, 768], P('section', 'expert'), may hold values from -0.125 to 0.125
- w_down: bfloat16 [4, 8, 768, 2048], P('section', 'expert'), may hold values from -0.21875 to 0.21875
Outputs:
- produced: bfloat16 [2, 4, 1024, 2048], P(None, 'section', 'expert')
Inputs may be any that keep to these rules, and one draw needn't show every extreme that they name: `routes`: each row names 2 different experts; in each aligned block of 128 rows no expert is named more than 48 times, a bound that some block reaches.
All inputs are finite; a program needn't handle non-finite values.
Results may differ from a plain program's by a relative error of at most 0.0052.
Values may be sent and summed in bfloat16 or wider, within the bound.
No kernel may reach another device: no remote copies, remote signals or barrier semaphores. Data moves between devices by JAX's collectives and lax.ppermute only.
A program may use at most 128 MiB of HBM per device.

v0:
```python
import jax
import jax.numpy as jnp
from jax import lax
from jax.sharding import PartitionSpec as P

D = 2048
TOPK = 2
EXP_DEV = 1
TICKS = 2
TOK_DEV = 128


def from_behind(x, axis, by):
    length = lax.axis_size(axis)
    pairs = [(i, i + by) for i in range(length) if 0 <= i + by < length]
    return lax.ppermute(x, axis, pairs)


def contract_last(left, right):
    return lax.dot_general(
        left, right, (((1,), (1,)), ((), ())), preferred_element_type=jnp.float32
    )


def expert_backward(normed_rows, scaled_rows, gate_matrix, up_matrix, down_matrix):
    pre_gate = jnp.dot(normed_rows, gate_matrix, preferred_element_type=jnp.float32)
    pre_up = jnp.dot(normed_rows, up_matrix, preferred_element_type=jnp.float32)
    hidden_grad = contract_last(scaled_rows, down_matrix)
    sigmoid = jax.nn.sigmoid(pre_gate)
    gate_grad = (hidden_grad * pre_up * sigmoid * (1.0 + pre_gate * (1.0 - sigmoid))).astype(
        jnp.bfloat16
    )
    up_grad = (hidden_grad * pre_gate * sigmoid).astype(jnp.bfloat16)
    summed = contract_last(gate_grad, gate_matrix) + contract_last(up_grad, up_matrix)
    return summed.astype(jnp.bfloat16)


def expert_side(normed_in, grads_in, gates_in, w_gate, w_up, w_down):
    sources, local_count, slot_width, model_width = normed_in.shape
    normed_rows = normed_in[:, 0].reshape(-1, model_width)
    grad_rows = grads_in[:, 0].reshape(-1, model_width)
    gate_rows = gates_in[:, 0].reshape(-1)
    scaled_rows = (gate_rows.astype(jnp.float32)[:, None] * grad_rows.astype(jnp.float32)).astype(
        jnp.bfloat16
    )
    gate_matrix = w_gate[0, 0]
    up_matrix = w_up[0, 0]
    down_matrix = w_down[0, 0]
    result = expert_backward(normed_rows, scaled_rows, gate_matrix, up_matrix, down_matrix)
    outputs = [result.reshape(sources, slot_width, model_width)]
    return jnp.stack(outputs, axis=1)


def place_slots(values, slot_flat, devices_expert, slot_count):
    buffer = (
        jnp.zeros((devices_expert * EXP_DEV * slot_count,) + values.shape[1:], values.dtype)
        .at[slot_flat]
        .set(values)
    )
    return buffer.reshape((devices_expert, EXP_DEV, slot_count) + values.shape[1:])


def local(layer_input, entering, fresh, routes, gate_weights, norm_gain, w_gate, w_up, w_down):
    devices_expert = lax.axis_size("expert")
    experts_all = EXP_DEV * devices_expert
    slot_count = max(2, min(TOK_DEV, 3 * TOK_DEV * TOPK // (2 * experts_all)))
    section_last = lax.axis_size("section") - 1
    section_here = lax.axis_index("section")
    gain_row = norm_gain[0]
    token_of = jnp.arange(TOK_DEV * TOPK, dtype=jnp.int32) // TOPK
    expert_ids = jnp.arange(experts_all, dtype=jnp.int32)
    slot_table = []
    normed_table = []
    inverse_table = []
    for step_index in range(TICKS):
        flat_routes = routes[step_index, 0].reshape(-1)
        onehot = (flat_routes[:, None] == expert_ids[None, :]).astype(jnp.int32)
        earlier = jnp.cumsum(onehot, axis=0) - onehot
        rank_within = jnp.sum(earlier * onehot, axis=1)
        slot_table.append(flat_routes * slot_count + rank_within)
        xfloat = layer_input[step_index, 0].astype(jnp.float32)
        inverse = lax.rsqrt(jnp.mean(xfloat * xfloat, axis=1, keepdims=True) + 1e-05)
        inverse_table.append(inverse)
        normed_table.append((xfloat * inverse * gain_row).astype(jnp.bfloat16))
    results = []
    arrived = entering[0]
    for step_index in range(TICKS):
        if step_index == 0:
            incoming = entering[0]
        else:
            incoming = jnp.where(section_here == section_last, fresh[step_index - 1], arrived)
        slot_flat = slot_table[step_index]
        grads_packed = place_slots(incoming[token_of], slot_flat, devices_expert, slot_count)
        gates_packed = place_slots(
            gate_weights[step_index, 0].reshape(-1), slot_flat, devices_expert, slot_count
        )
        normed_packed = place_slots(
            normed_table[step_index][token_of], slot_flat, devices_expert, slot_count
        )
        computed = expert_side(
            lax.all_to_all(normed_packed, "expert", split_axis=0, concat_axis=0, tiled=True),
            lax.all_to_all(grads_packed, "expert", split_axis=0, concat_axis=0, tiled=True),
            lax.all_to_all(gates_packed, "expert", split_axis=0, concat_axis=0, tiled=True),
            w_gate,
            w_up,
            w_down,
        )
        returned = lax.all_to_all(computed, "expert", split_axis=0, concat_axis=0, tiled=True)
        picked = jnp.take(returned.reshape(experts_all * slot_count, D), slot_flat, axis=0)
        normed_grad = jnp.sum(picked.reshape(TOK_DEV, TOPK, D).astype(jnp.float32), axis=1)
        xfloat = layer_input[step_index, 0].astype(jnp.float32)
        inverse = inverse_table[step_index]
        weighted = gain_row * normed_grad
        project = jnp.mean(xfloat * weighted, axis=1, keepdims=True)
        result = (
            incoming.astype(jnp.float32) + inverse * weighted - xfloat * inverse**3 * project
        ).astype(jnp.bfloat16)
        results.append(result)
        if step_index + 1 < TICKS:
            arrived = from_behind(result, "section", -1)
    return jnp.stack(results, axis=0)[:, None]


def solution(mesh):
    in_specs = (
        P(None, "section", "expert", None),
        P("section", "expert", None),
        P(None, "expert", None),
        P(None, "section", "expert", None),
        P(None, "section", "expert", None),
        P("section", None),
        P("section", "expert", None, None),
        P("section", "expert", None, None),
        P("section", "expert", None, None),
    )
    out_specs = P(None, "section", "expert", None)
    return jax.shard_map(local, mesh=mesh, in_specs=in_specs, out_specs=out_specs, check_vma=False)
```

profile of v0, /device:TPU:0, one launch (start us, length us, event | category | flops | bytes accessed | tf_op | source)
XLA Modules:
  0.0 361.7 jit_solution(16599872276799323001)
XLA Ops:
  6.3 7.3 %all-to-all-start = ((bf16[8,1,48]{2,1,0:T(2,128)(2,1)}), bf16[8,1,48]{2,1,0:T(2,128)(2,1)S(1)}, u32[]{:S(2)}, u32[]{:S(2)}) async-start(bf16[8,1,48]{2,1,0:T(2,128)(2,1)} %reshape.466), calls=%async_computation | async-start | bytes 8192 | tf_op jit(solution)/shard_map/all_to_all | solution.py:103
  16.9 6.8 %scatter_custom_fusion.2 = bf16[384,2048]{1,0:T(8,128)(2,1)} fusion(s32[256]{0:T(256)S(1)} %bitcast.196, bf16[128,2048]{1,0:T(8,128)(2,1)} %fusion.54, s32[1024]{0:T(1024)S(1)} %pad_clamp_fusion.2, bf16[]{:T(256)} %constant.52.clone.1), kind=kCustom, calls=%fused_computation.86 | custom fusion | bytes 1573376 | tf_op jit(solution)/shard_map/scatter | solution.py:58
  23.7 6.2 %all-to-all-start.2 = ((bf16[8,1,48,2048]{3,2,1,0:T(8,128)(2,1)}), bf16[8,1,48,2048]{3,2,1,0:T(8,128)(2,1)}, u32[]{:S(2)}, u32[]{:S(2)}) async-start(bf16[8,1,48,2048]{3,2,1,0:T(8,128)(2,1)} %bitcast.176), calls=%async_computation.2 | async-start | bytes 3145728 | tf_op jit(solution)/shard_map/all_to_all | solution.py:101
  29.9 6.9 %scatter_custom_fusion.1 = bf16[384,2048]{1,0:T(8,128)(2,1)} fusion(s32[256]{0:T(256)S(1)} %bitcast.197, bf16[128,2048]{1,0:T(8,128)(2,1)} %bitcast.177, s32[1024]{0:T(1024)S(1)} %pad_clamp_fusion.2, bf16[]{:T(256)} %constant.52.clone.1), kind=kCustom, calls=%fused_computation.88 | custom fusion | bytes 1573376 | tf_op jit(solution)/shard_map/scatter | solution.py:58
  36.9 29.6 %all-to-all-done.2 = bf16[8,1,48,2048]{3,2,1,0:T(8,128)(2,1)} async-done(((bf16[8,1,48,2048]{3,2,1,0:T(8,128)(2,1)}), bf16[8,1,48,2048]{3,2,1,0:T(8,128)(2,1)}, u32[]{:S(2)}, u32[]{:S(2)}) %all-to-all-start.2) | async-done | bytes 1572896 | tf_op jit(solution)/shard_map/all_to_all | solution.py:101
  70.7 4.8 %fusion.6 = f32[384,768]{1,0:T(8,128)} fusion(bf16[384,2048]{1,0:T(8,128)(2,1)} %bitcast.13, bf16[1,1,2048,768]{3,2,1,0:T(8,128)(2,1)} %param.17), kind=kOutput, calls=%fused_computation.18 | convolution fusion | flops 1207959552 | bytes 5898240 | tf_op jit(solution)/shard_map/dot_general | solution.py:26
  75.5 31.8 %all-to-all-done.1 = bf16[8,1,48,2048]{3,2,1,0:T(8,128)(2,1)} async-done(((bf16[8,1,48,2048]{3,2,1,0:T(8,128)(2,1)}), bf16[8,1,48,2048]{3,2,1,0:T(8,128)(2,1)}, u32[]{:S(2)}, u32[]{:S(2)}) %all-to-all-start.1) | async-done | bytes 1572896 | tf_op jit(solution)/shard_map/all_to_all | solution.py:102
  112.2 7.8 %fusion.4 = f32[384,2048]{1,0:T(8,128)} fusion(bf16[1,1,2048,768]{3,2,1,0:T(8,128)(2,1)} %param.17, f32[384,768]{1,0:T(8,128)} %fusion.18, bf16[384,2048]{1,0:T(8,128)(2,1)} %bitcast.13, bf16[1,1,2048,768]{3,2,1,0:T(8,128)(2,1)S(1)} %copy-done, f32[384,768]{1,0:T(8,128)} %fusion.6), kind=kOutput, calls=%fused_computation.16 | convolution fusion | flops 2418868224 | bytes 13369344 | tf_op jit(solution)/shard_map/dot_general | solution.py:20
  120.0 5.2 %add_convert_fusion.1 = bf16[384,2048]{1,0:T(8,128)(2,1)} fusion(f32[384,2048]{1,0:T(8,128)} %fusion.4, bf16[1,1,2048,768]{3,2,1,0:T(8,128)(2,1)S(1)} %copy-done, f32[384,768]{1,0:T(8,128)} %fusion.18, f32[384,768]{1,0:T(8,128)} %fusion.6), kind=kOutput, calls=%fused_computation.34 | convolution fusion | flops 1211301888 | bytes 10223616 | tf_op jit(solution)/shard_map/dot_general | solution.py:20
  134.3 31.9 %all-to-all-done.3 = bf16[8,1,48,2048]{3,2,1,0:T(8,128)(2,1)} async-done(((bf16[8,1,48,2048]{3,2,1,0:T(8,128)(2,1)}), bf16[8,1,48,2048]{3,2,1,0:T(8,128)(2,1)}, u32[]{:S(2)}, u32[]{:S(2)}) %all-to-all-start.3) | async-done | bytes 1572896 | tf_op jit(solution)/shard_map/all_to_all | solution.py:108
  170.2 4.9 %gather_fusion = bf16[256,2048]{1,0:T(8,128)(2,1)} fusion(bf16[384,2048]{1,0:T(8,128)(2,1)} %bitcast.18, s32[1024]{0:T(1024)S(1)} %pad_clamp_fusion.1), kind=kCustom, calls=%fused_computation.clone | custom fusion | bytes 2098176 | tf_op jit(solution)/shard_map/jit(_take)/gather | solution.py:109
  181.4 5.1 %reduce_sum.81 = f32[128,2048]{1,0:T(8,128)} reduce(f32[128,2,2048]{2,1,0:T(2,128)} %reshape.359, f32[]{:T(128)} %constant.49.clone.1), dimensions={1}, to_apply=%region_7.9 | reduce | flops 262144 | bytes 3145732 | tf_op jit(solution)/shard_map/reduce_sum | solution.py:110
  191.2 6.8 %scatter_custom_fusion.5 = bf16[384,2048]{1,0:T(8,128)(2,1)} fusion(s32[256]{0:T(256)S(1)} %bitcast.193, bf16[128,2048]{1,0:T(8,128)(2,1)} %get-tuple-element.12, s32[1024]{0:T(1024)S(1)} %pad_clamp_fusion.2, bf16[]{:T(256)} %constant.52.clone.1), kind=kCustom, calls=%fused_computation.82 | custom fusion | bytes 1573376 | tf_op jit(solution)/shard_map/scatter | solution.py:58
  198.0 6.0 %all-to-all-start.6 = ((bf16[8,1,48,2048]{3,2,1,0:T(8,128)(2,1)}), bf16[8,1,48,2048]{3,2,1,0:T(8,128)(2,1)}, u32[]{:S(2)}, u32[]{:S(2)}) async-start(bf16[8,1,48,2048]{3,2,1,0:T(8,128)(2,1)} %bitcast.173), calls=%async_computation.6 | async-start | bytes 3145728 | tf_op jit(solution)/shard_map/all_to_all | solution.py:101
  210.2 6.9 %scatter_custom_fusion.4 = bf16[384,2048]{1,0:T(8,128)(2,1)} fusion(s32[256]{0:T(256)S(1)} %bitcast.194, bf16[128,2048]{1,0:T(8,128)(2,1)} %bitcast_select_fusion, s32[1024]{0:T(1024)S(1)} %pad_clamp_fusion.2, bf16[]{:T(256)} %constant.52.clone.1), kind=kCustom, calls=%fused_computation.84 | custom fusion | bytes 1573376 | tf_op jit(solution)/shard_map/scatter | solution.py:58
  217.1 23.7 %all-to-all-done.6 = bf16[8,1,48,2048]{3,2,1,0:T(8,128)(2,1)} async-done(((bf16[8,1,48,2048]{3,2,1,0:T(8,128)(2,1)}), bf16[8,1,48,2048]{3,2,1,0:T(8,128)(2,1)}, u32[]{:S(2)}, u32[]{:S(2)}) %all-to-all-start.6) | async-done | bytes 1572896 | tf_op jit(solution)/shard_map/all_to_all | solution.py:101
  245.1 4.8 %fusion.2 = f32[384,768]{1,0:T(8,128)} fusion(bf16[384,2048]{1,0:T(8,128)(2,1)} %bitcast.32, bf16[1,1,2048,768]{3,2,1,0:T(8,128)(2,1)} %param.17), kind=kOutput, calls=%fused_computation.14 | convolution fusion | flops 1207959552 | bytes 5898240 | tf_op jit(solution)/shard_map/dot_general | solution.py:26
  249.9 31.8 %all-to-all-done.5 = bf16[8,1,48,2048]{3,2,1,0:T(8,128)(2,1)} async-done(((bf16[8,1,48,2048]{3,2,1,0:T(8,128)(2,1)}), bf16[8,1,48,2048]{3,2,1,0:T(8,128)(2,1)}, u32[]{:S(2)}, u32[]{:S(2)}) %all-to-all-start.5) | async-done | bytes 1572896 | tf_op jit(solution)/shard_map/all_to_all | solution.py:102
  286.5 7.8 %fusion = f32[384,2048]{1,0:T(8,128)} fusion(bf16[1,1,2048,768]{3,2,1,0:T(8,128)(2,1)} %param.17, f32[384,768]{1,0:T(8,128)} %fusion.16, bf16[384,2048]{1,0:T(8,128)(2,1)} %bitcast.32, bf16[1,1,2048,768]{3,2,1,0:T(8,128)(2,1)S(1)} %copy-done, f32[384,768]{1,0:T(8,128)} %fusion.2), kind=kOutput, calls=%fused_computation.12 | convolution fusion | flops 2418868224 | bytes 13369344 | tf_op jit(solution)/shard_map/dot_general | solution.py:20
  294.3 5.2 %add_convert_fusion = bf16[384,2048]{1,0:T(8,128)(2,1)} fusion(f32[384,2048]{1,0:T(8,128)} %fusion, bf16[1,1,2048,768]{3,2,1,0:T(8,128)(2,1)S(1)} %copy-done, f32[384,768]{1,0:T(8,128)} %fusion.16, f32[384,768]{1,0:T(8,128)} %fusion.2), kind=kOutput, calls=%fused_computation.32 | convolution fusion | flops 1211301888 | bytes 10223616 | tf_op jit(solution)/shard_map/dot_general | solution.py:20
  299.5 4.5 %all-to-all-start.7 = ((bf16[8,1,48,2048]{3,2,1,0:T(8,128)(2,1)}), bf16[8,1,48,2048]{3,2,1,0:T(8,128)(2,1)}, u32[]{:S(2)}, u32[]{:S(2)}) async-start(bf16[8,1,48,2048]{3,2,1,0:T(8,128)(2,1)} %bitcast.179), calls=%async_computation.7 | async-start | bytes 3145728 | tf_op jit(solution)/shard_map/all_to_all | solution.py:108
  306.8 33.8 %all-to-all-done.7 = bf16[8,1,48,2048]{3,2,1,0:T(8,128)(2,1)} async-done(((bf16[8,1,48,2048]{3,2,1,0:T(8,128)(2,1)}), bf16[8,1,48,2048]{3,2,1,0:T(8,128)(2,1)}, u32[]{:S(2)}, u32[]{:S(2)}) %all-to-all-start.7) | async-done | bytes 1572896 | tf_op jit(solution)/shard_map/all_to_all | solution.py:108
  340.7 4.9 %gather_fusion.1 = bf16[256,2048]{1,0:T(8,128)(2,1)} fusion(bf16[384,2048]{1,0:T(8,128)(2,1)} %bitcast.35, s32[1024]{0:T(1024)S(1)} %pad_clamp_fusion), kind=kCustom, calls=%fused_computation.1.clone | custom fusion | bytes 2098176 | tf_op jit(solution)/shard_map/jit(_take)/gather | solution.py:109
  351.8 5.1 %reduce_sum.87 = f32[128,2048]{1,0:T(8,128)} reduce(f32[128,2,2048]{2,1,0:T(2,128)} %reshape.363, f32[]{:T(128)} %constant.49.clone.1), dimensions={1}, to_apply=%region_16.18 | reduce | flops 262144 | bytes 3145732 | tf_op jit(solution)/shard_map/reduce_sum | solution.py:110
  (88 shorter events, 71.5 us)
Async XLA Ops:
  0.0 112.2 %copy-start = (bf16[1,1,2048,768]{3,2,1,0:T(8,128)(2,1)S(1)}, bf16[1,1,2048,768]{3,2,1,0:T(8,128)(2,1)}, u32[]{:S(2)}) copy-start(bf16[1,1,2048,768]{3,2,1,0:T(8,128)(2,1)} %param.18) | copy-start | bytes 9437188
  6.3 17.4 %all-to-all-start = ((bf16[8,1,48]{2,1,0:T(2,128)(2,1)}), bf16[8,1,48]{2,1,0:T(2,128)(2,1)S(1)}, u32[]{:S(2)}, u32[]{:S(2)}) async-start(bf16[8,1,48]{2,1,0:T(2,128)(2,1)} %reshape.466), calls=%async_computation | async-start | bytes 8192 | tf_op jit(solution)/shard_map/all_to_all | solution.py:103
  23.7 42.7 %all-to-all-start.2 = ((bf16[8,1,48,2048]{3,2,1,0:T(8,128)(2,1)}), bf16[8,1,48,2048]{3,2,1,0:T(8,128)(2,1)}, u32[]{:S(2)}, u32[]{:S(2)}) async-start(bf16[8,1,48,2048]{3,2,1,0:T(8,128)(2,1)} %bitcast.176), calls=%async_computation.2 | async-start | bytes 3145728 | tf_op jit(solution)/shard_map/all_to_all | solution.py:101
  66.4 40.9 %all-to-all-start.1 = ((bf16[8,1,48,2048]{3,2,1,0:T(8,128)(2,1)}), bf16[8,1,48,2048]{3,2,1,0:T(8,128)(2,1)}, u32[]{:S(2)}, u32[]{:S(2)}) async-start(bf16[8,1,48,2048]{3,2,1,0:T(8,128)(2,1)} %bitcast.175), calls=%async_computation.1 | async-start | bytes 3145728 | tf_op jit(solution)/shard_map/all_to_all | solution.py:102
  107.4 2.4 copy-start.7
  125.2 40.9 %all-to-all-start.3 = ((bf16[8,1,48,2048]{3,2,1,0:T(8,128)(2,1)}), bf16[8,1,48,2048]{3,2,1,0:T(8,128)(2,1)}, u32[]{:S(2)}, u32[]{:S(2)}) async-start(bf16[8,1,48,2048]{3,2,1,0:T(8,128)(2,1)} %bitcast.178), calls=%async_computation.3 | async-start | bytes 3145728 | tf_op jit(solution)/shard_map/all_to_all | solution.py:108
  166.1 31.9 %all-to-all-start.4 = ((bf16[8,1,48]{2,1,0:T(2,128)(2,1)}), bf16[8,1,48]{2,1,0:T(2,128)(2,1)S(1)}, u32[]{:S(2)}, u32[]{:S(2)}) async-start(bf16[8,1,48]{2,1,0:T(2,128)(2,1)} %reshape.467), calls=%async_computation.4 | async-start | bytes 8192 | tf_op jit(solution)/shard_map/all_to_all | solution.py:103
  181.4 5.1 %copy-start.6 = (f32[1,2048]{1,0:T(1,128)S(1)}, f32[1,2048]{1,0:T(1,128)}, u32[]{:S(2)}) copy-start(f32[1,2048]{1,0:T(1,128)} %param.16) | copy-start | bytes 24580
  186.5 2.0 copy-start.1
  186.5 2.2 copy-start.3
  198.0 42.7 %all-to-all-start.6 = ((bf16[8,1,48,2048]{3,2,1,0:T(8,128)(2,1)}), bf16[8,1,48,2048]{3,2,1,0:T(8,128)(2,1)}, u32[]{:S(2)}, u32[]{:S(2)}) async-start(bf16[8,1,48,2048]{3,2,1,0:T(8,128)(2,1)} %bitcast.173), calls=%async_computation.6 | async-start | bytes 3145728 | tf_op jit(solution)/shard_map/all_to_all | solution.py:101
  204.0 4.1 %collective-permute-start = (bf16[128,2048]{1,0:T(8,128)(2,1)}, bf16[128,2048]{1,0:T(8,128)(2,1)}, u32[]{:S(2)}, u32[]{:S(2)}) collective-permute-start(bf16[128,2048]{1,0:T(8,128)(2,1)} %get-tuple-element.13), channel_id=1, source_target_pairs={{8,0},{16,8},{24,16},{9,1},{17,9},{25,17},{10,2},{18,10},{26,18},{... | collective-permute-start | bytes 1572872 | tf_op jit(solution)/shard_map/ppermute | solution.py:16
  240.7 40.9 %all-to-all-start.5 = ((bf16[8,1,48,2048]{3,2,1,0:T(8,128)(2,1)}), bf16[8,1,48,2048]{3,2,1,0:T(8,128)(2,1)}, u32[]{:S(2)}, u32[]{:S(2)}) async-start(bf16[8,1,48,2048]{3,2,1,0:T(8,128)(2,1)} %bitcast.174), calls=%async_computation.5 | async-start | bytes 3145728 | tf_op jit(solution)/shard_map/all_to_all | solution.py:102
  281.7 2.4 copy-start.8
  299.5 41.1 %all-to-all-start.7 = ((bf16[8,1,48,2048]{3,2,1,0:T(8,128)(2,1)}), bf16[8,1,48,2048]{3,2,1,0:T(8,128)(2,1)}, u32[]{:S(2)}, u32[]{:S(2)}) async-start(bf16[8,1,48,2048]{3,2,1,0:T(8,128)(2,1)} %bitcast.179), calls=%async_computation.7 | async-start | bytes 3145728 | tf_op jit(solution)/shard_map/all_to_all | solution.py:108
  356.9 1.7 copy-start.2
  356.9 1.8 copy-start.4
  358.6 1.8 copy-start.5
where the time goes:
time: 369 us; the launch traced here: 362 us
  waiting for transfers between devices  185 us (50%)
  local copies, waits for them, and re-layouts  54.1 us (15%)
  starting transfers between devices  42.4 us (11%)
  matrix products  40.5 us (11%)
  other arithmetic  38.9 us (11%)
    all_to_all x2, waiting for transfers between devices, local(): lax.all_to_all(computed, 'expert', split_axis=0, concat_axis=0, tiled=True)  65.7 us
    all_to_all x2, waiting for transfers between devices, local(): lax.all_to_all(grads_packed, 'expert', split_axis=0, concat_axis=0, tiled...  63.7 us
    all_to_all x2, waiting for transfers between devices, local(): lax.all_to_all(normed_packed, 'expert', split_axis=0, concat_axis=0, tile...  53.2 us
    scatter x6, local copies, waits for them, and re-layouts, place_slots(): buffer = jnp.zeros((devices_expert * EXP_DEV * slot_count,) + values.shap...  31.7 us
    dot_general x6, matrix products, contract_last(): lax.dot_general(left, right, (((1,), (1,)), ((), ())), preferred_element_...  30.9 us
    all_to_all x2, starting transfers between devices, local(): lax.all_to_all(normed_packed, 'expert', split_axis=0, concat_axis=0, tile...  12.2 us
    all_to_all x2, starting transfers between devices, local(): lax.all_to_all(gates_packed, 'expert', split_axis=0, concat_axis=0, tiled...  11.4 us
    reduce_sum x2, other arithmetic, local(): jnp.sum(picked.reshape(TOK_DEV, TOPK, D).astype(jnp.float32), axis=1)  10.2 us
  transfers between devices with their start and end apart: 9, of which 7 were waited for; matrix products, arithmetic and copies ran while one was open for 20% of the time, Pallas kernels for 0%

commit v1 on v0

v1 whole, which is shorter than its diff:
```python
import jax
import jax.numpy as jnp
from jax import lax
from jax.sharding import Mesh, PartitionSpec as P

TICKS = 2
TOPK = 2
BOTH = ("quad", "half")


def contract_last(left, right):
    return lax.dot_general(
        left, right, (((1,), (1,)), ((), ())), preferred_element_type=jnp.float32
    )


def after(value, *others):
    return lax.optimization_barrier((value,) + others)[0]


def swap(value):
    return lax.ppermute(value, "half", [(0, 1), (1, 0)])


def positions(routes, quads, slots):
    tokens, topk = routes.shape
    experts = 2 * quads
    flat = routes.reshape(-1)
    onehot = (flat[:, None] == jnp.arange(experts, dtype=jnp.int32)[None, :]).astype(jnp.bfloat16)
    count = flat.shape[0]
    row = lax.broadcasted_iota(jnp.int32, (count, count), 0)
    col = lax.broadcasted_iota(jnp.int32, (count, count), 1)
    earlier = jnp.dot(
        (col < row).astype(jnp.bfloat16), onehot, preferred_element_type=jnp.float32
    )
    rank = jnp.sum(earlier * onehot.astype(jnp.float32), axis=1).astype(jnp.int32)
    place = ((flat % quads) * 2 + flat // quads) * slots + rank
    return place.reshape(tokens, topk)


def select(place, slot_of):
    hit = place[:, 0][None, :] == slot_of[:, None]
    for k in range(1, TOPK):
        hit = hit | (place[:, k][None, :] == slot_of[:, None])
    return hit.astype(jnp.bfloat16)


def gate_of(place, gates, slot_of):
    total = jnp.zeros(slot_of.shape, jnp.float32)
    for k in range(TOPK):
        hit = place[:, k][None, :] == slot_of[:, None]
        total = total + jnp.sum(jnp.where(hit, gates[:, k].astype(jnp.float32)[None, :], 0.0), axis=1)
    return total


def local(layer_input, entering, fresh, routes, gate_weights, norm_gain, w_gate, w_up, w_down):
    quads = lax.axis_size("quad")
    experts = 2 * quads
    tokens, width = layer_input.shape[2], layer_input.shape[3]
    slots = max(2, min(tokens, 3 * tokens * TOPK // (2 * experts)))
    rows = experts * slots
    half_here = lax.axis_index("half")
    section_here = lax.axis_index("section")
    section_last = lax.axis_size("section") - 1
    gain = norm_gain[0]
    gate_matrix, up_matrix, down_matrix = w_gate[0, 0], w_up[0, 0], w_down[0, 0]

    def norm(t):
        xfloat = layer_input[t, 0].astype(jnp.float32)
        inverse = lax.rsqrt(jnp.mean(xfloat * xfloat, axis=1, keepdims=True) + 1e-05)
        return (xfloat * inverse * gain).astype(jnp.bfloat16), inverse

    def incoming_pack(values, place, gates):
        slot_of = jnp.arange(rows, dtype=jnp.int32)
        packed = jnp.dot(select(place, slot_of), values, preferred_element_type=jnp.float32)
        return (packed * gate_of(place, gates, slot_of)[:, None]).astype(jnp.bfloat16)

    index = jnp.arange(rows, dtype=jnp.int32)
    source_half = (index // slots) % 2
    own_row = source_half == half_here
    wanted = (index // (2 * slots) * 2 + half_here) * slots + index % slots

    def pair_select(own_place, mirror_place):
        own = select(own_place, jnp.where(own_row, wanted, -1))
        mirror = select(mirror_place, jnp.where(own_row, -1, wanted))
        return jnp.concatenate([own, mirror], axis=1)

    def pair_gate(own_place, own_gates, mirror_place, mirror_gates):
        own = gate_of(own_place, own_gates, jnp.where(own_row, wanted, -1))
        mirror = gate_of(mirror_place, mirror_gates, jnp.where(own_row, -1, wanted))
        return own + mirror

    def quad_exchange(packed):
        return lax.all_to_all(
            packed.reshape(quads, 2 * slots, width), "quad", split_axis=0, concat_axis=0, tiled=True
        ).reshape(rows, width)

    def full_exchange(packed):
        return lax.all_to_all(
            packed.reshape(experts, slots, width), BOTH, split_axis=0, concat_axis=0, tiled=True
        ).reshape(rows, width)

    def hidden(normed_rows):
        pre_gate = jnp.dot(normed_rows, gate_matrix, preferred_element_type=jnp.float32)
        pre_up = jnp.dot(normed_rows, up_matrix, preferred_element_type=jnp.float32)
        return pre_gate, pre_up

    def backward(pre_gate, pre_up, hidden_grad):
        sigmoid = jax.nn.sigmoid(pre_gate)
        gate_grad = (
            hidden_grad * pre_up * sigmoid * (1.0 + pre_gate * (1.0 - sigmoid))
        ).astype(jnp.bfloat16)
        up_grad = (hidden_grad * pre_gate * sigmoid).astype(jnp.bfloat16)
        summed = contract_last(gate_grad, gate_matrix) + contract_last(up_grad, up_matrix)
        return summed.astype(jnp.bfloat16)

    def combine(t, incoming, returned, place, inverse):
        chosen = select(place, jnp.arange(rows, dtype=jnp.int32))
        normed_grad = lax.dot_general(
            chosen, returned, (((0,), (0,)), ((), ())), preferred_element_type=jnp.float32
        )
        xfloat = layer_input[t, 0].astype(jnp.float32)
        weighted = gain * normed_grad
        project = jnp.mean(xfloat * weighted, axis=1, keepdims=True)
        return (
            incoming.astype(jnp.float32) + inverse * weighted - xfloat * inverse**3 * project
        ).astype(jnp.bfloat16)

    place = [positions(routes[t, 0], quads, slots) for t in range(TICKS)]
    gates = [gate_weights[t, 0] for t in range(TICKS)]

    grad_mirror = swap(entering[0])
    place_mirror = swap(jnp.stack(place, axis=0))
    gates_mirror = swap(gates[0])
    normed0, inverse0 = norm(0)
    normed1, inverse1 = norm(1)
    normed0_mirror = swap(after(normed0, grad_mirror))
    normed1_mirror = swap(after(normed1, normed0_mirror))

    pair0 = pair_select(place[0], place_mirror[0])
    pair1 = pair_select(place[1], place_mirror[1])
    scale0 = pair_gate(place[0], gates[0], place_mirror[0], gates_mirror)

    both = jnp.concatenate([entering[0], grad_mirror], axis=0)
    packed = jnp.dot(pair0, both, preferred_element_type=jnp.float32)
    scaled0 = quad_exchange((packed * scale0[:, None]).astype(jnp.bfloat16))
    hidden_grad0 = contract_last(scaled0, down_matrix)

    both = jnp.concatenate([normed0, normed0_mirror], axis=0)
    rows0 = quad_exchange(jnp.dot(pair0, both, preferred_element_type=jnp.bfloat16))
    pre_gate0, pre_up0 = hidden(rows0)
    computed0 = backward(pre_gate0, pre_up0, hidden_grad0)
    returned0 = full_exchange(computed0)

    both = jnp.concatenate([normed1, normed1_mirror], axis=0)
    packed1 = jnp.dot(pair1, both, preferred_element_type=jnp.bfloat16)
    rows1 = quad_exchange(after(packed1, returned0))
    result0 = combine(0, entering[0], returned0, place[0], inverse0)

    length = section_last + 1
    arrived = lax.ppermute(result0, "section", [(i, i - 1) for i in range(1, length)])
    incoming = jnp.where(section_here == section_last, fresh[0], arrived)
    scaled1 = full_exchange(incoming_pack(incoming, place[1], gates[1]))
    pre_gate1, pre_up1 = hidden(rows1)
    computed1 = backward(pre_gate1, pre_up1, contract_last(scaled1, down_matrix))
    returned1 = full_exchange(computed1)
    result1 = combine(1, incoming, returned1, place[1], inverse1)
    return jnp.stack([result0, result1], axis=0)[:, None]


def solution(mesh):
    sections, experts = mesh.shape["section"], mesh.shape["expert"]
    split = Mesh(mesh.devices.reshape(sections, 2, experts // 2), ("section", "half", "quad"))
    expert = ("half", "quad")
    in_specs = (
        P(None, "section", expert, None),
        P("section", expert, None),
        P(None, expert, None),
        P(None, "section", expert, None),
        P(None, "section", expert, None),
        P("section", None),
        P("section", expert, None, None),
        P("section", expert, None, None),
        P("section", expert, None, None),
    )
    out_specs = P(None, "section", expert, None)
    return jax.shard_map(local, mesh=split, in_specs=in_specs, out_specs=out_specs, check_vma=False)
```

time: 369 us -> 308 us (0.83); the launches traced: 362 us -> 308 us
  blocking collectives: 0 us -> 83.2 us
  waiting for transfers between devices: 185 us -> 128 us
  local copies, waits for them, and re-layouts: 54.1 us -> 3.75 us
  other arithmetic: 38.9 us -> 7.74 us
  matrix products: 40.5 us -> 53.9 us
  starting transfers between devices: 42.4 us -> 30.5 us
    all_to_all x8 -> x4, waiting for transfers between devices: 183 us -> 56.7 us  [the longest x1 29.4 us: full_exchange(): lax.all_to_all(packed.reshape(experts, slots, width), BOTH, split_axis=0,...]
    all_to_all x0 -> x2, blocking collectives: none -> 83.2 us  [full_exchange(): lax.all_to_all(packed.reshape(experts, slots, width), BOTH, split_axis=0,...]
    ppermute x1 -> x6, waiting for transfers between devices: 2.67 us -> 71.5 us  [the longest x5 69.1 us: swap(): return lax.ppermute(value, 'half', [(0, 1), (1, 0)])]
    scatter x6 -> x0, local copies, waits for them, and re-layouts: 31.7 us -> none  [place_slots(): buffer = jnp.zeros((devices_expert * EXP_DEV * slot_count,) + values.shap...]
    all_to_all x8 -> x4, starting transfers between devices: 41 us -> 20.1 us  [the longest x3 15.8 us: quad_exchange(): lax.all_to_all(packed.reshape(quads, 2 * slots, width), 'quad', split_axi...]
    convert_element_type x11 -> x6, other arithmetic: 16.6 us -> 2.46 us  [the longest x2 2.44 us: norm(): return ((xfloat * inverse * gain).astype(jnp.bfloat16), inverse)]
    reduce_sum x7 -> x5, other arithmetic: 15.3 us -> 2.05 us  [the longest x1 1.23 us: norm(): jnp.mean(xfloat * xfloat, axis=1, keepdims=True) + 1e-05]
    dot_general x2 -> x10, matrix products: 9.6 us -> 20.5 us  [the longest x2 9.57 us: hidden(): jnp.dot(normed_rows, gate_matrix, preferred_element_type=jnp.float32)]
  transfers between devices with their start and end apart: 9 -> 10, of which waited for: 7 -> 9; matrix products, arithmetic and copies ran while one was open for 20% -> 7% of each run, Pallas kernels for 0% -> 0%
where the time goes in v1:
time: 308 us
  waiting for transfers between devices  128 us (42%)
  blocking collectives  83.2 us (27%)
  matrix products  53.9 us (18%)
  starting transfers between devices  30.5 us (10%)
  other arithmetic  7.74 us (3%)
  local copies, waits for them, and re-layouts  3.75 us (1%)
    all_to_all x2, blocking collectives, full_exchange(): lax.all_to_all(packed.reshape(experts, slots, width), BOTH, split_axis=0,...  83.2 us
    ppermute x5, waiting for transfers between devices, swap(): return lax.ppermute(value, 'half', [(0, 1), (1, 0)])  69.1 us
    dot_general x6, matrix products, contract_last(): lax.dot_general(left, right, (((1,), (1,)), ((), ())), preferred_element_...  33.4 us
    all_to_all x1, waiting for transfers between devices, full_exchange(): lax.all_to_all(packed.reshape(experts, slots, width), BOTH, split_axis=0,...  29.4 us
    all_to_all x3, waiting for transfers between devices, quad_exchange(): lax.all_to_all(packed.reshape(quads, 2 * slots, width), 'quad', split_axi...  27.3 us
    all_to_all x3, starting transfers between devices, quad_exchange(): lax.all_to_all(packed.reshape(quads, 2 * slots, width), 'quad', split_axi...  15.8 us
    dot_general x2, matrix products, hidden(): jnp.dot(normed_rows, gate_matrix, preferred_element_type=jnp.float32)  9.57 us
    ppermute x5, starting transfers between devices, swap(): return lax.ppermute(value, 'half', [(0, 1), (1, 0)])  8.93 us
  transfers between devices with their start and end apart: 10, of which 9 were waited for; matrix products, arithmetic and copies ran while one was open for 7% of the time, Pallas kernels for 0%

profile of v1, /device:TPU:0, one launch (start us, length us, event | category | flops | bytes accessed | tf_op | source)
XLA Modules:
  0.0 307.6 jit_solution(10301642479717798831)
XLA Ops:
  0.8 4.1 %collective-permute-start.2 = (bf16[128,2]{0,1:T(2,128)(2,1)S(1)}, bf16[128,2]{0,1:T(2,128)(2,1)S(1)}, u32[]{:S(2)}, u32[]{:S(2)}) collective-permute-start(bf16[128,2]{0,1:T(2,128)(2,1)S(1)} %get-tuple-element.35), channel_id=1, source_target_pairs={{0,4},{4,0},{1,5},{5,1},{2,6},{6,2},{3,7},{7,3},{8,12},{12,8},{9,1... | collective-permute-start | bytes 1544 | tf_op jit(solution)/shard_map/ppermute | solution.py:22
  11.2 11.6 %collective-permute-done = s32[2,128,2]{1,2,0:T(2,128)S(1)} collective-permute-done((s32[2,128,2]{1,2,0:T(2,128)S(1)}, s32[2,128,2]{1,2,0:T(2,128)S(1)}, u32[]{:S(2)}, u32[]{:S(2)}) %collective-permute-start) | collective-permute-done | bytes 2080 | tf_op jit(solution)/shard_map/ppermute | solution.py:22
  23.3 9.9 %collective-permute-done.1 = bf16[128,2048]{1,0:T(8,128)(2,1)} collective-permute-done((bf16[128,2048]{1,0:T(8,128)(2,1)}, bf16[128,2048]{1,0:T(8,128)(2,1)}, u32[]{:S(2)}, u32[]{:S(2)}) %collective-permute-start.1) | collective-permute-done | bytes 524320 | tf_op jit(solution)/shard_map/ppermute | solution.py:22
  33.2 2.9 multiply_convert_fusion.1
  36.1 4.5 %all-to-all-start = ((bf16[4,96,2048]{2,1,0:T(8,128)(2,1)}), bf16[4,96,2048]{2,1,0:T(8,128)(2,1)}, u32[]{:S(2)}, u32[]{:S(2)}) async-start(bf16[4,96,2048]{2,1,0:T(8,128)(2,1)} %bitcast.216), calls=%async_computation | async-start | bytes 3145728 | tf_op jit(solution)/shard_map/all_to_all | solution.py:94
  44.9 23.5 %collective-permute-done.3 = bf16[128,2048]{1,0:T(8,128)(2,1)S(1)} collective-permute-done((bf16[128,2048]{1,0:T(8,128)(2,1)S(1)}, bf16[128,2048]{1,0:T(8,128)(2,1)S(1)}, u32[]{:S(2)}, u32[]{:S(2)}) %collective-permute-start.3) | collective-permute-done | bytes 524320 | tf_op jit(solution)/shard_map/ppermute | solution.py:22
  70.7 7.0 %all-to-all-start.1 = ((bf16[4,96,2048]{2,1,0:T(8,128)(2,1)}), bf16[4,96,2048]{2,1,0:T(8,128)(2,1)}, u32[]{:S(2)}, u32[]{:S(2)}) async-start(bf16[4,96,2048]{2,1,0:T(8,128)(2,1)} %bitcast.217), calls=%async_computation.1 | async-start | bytes 3145728 | tf_op jit(solution)/shard_map/all_to_all | solution.py:94
  77.7 4.8 %fusion.18 = f32[384,768]{1,0:T(8,128)} fusion(bf16[384,2048]{1,0:T(8,128)(2,1)} %bitcast.15, bf16[1,1,768,2048]{3,2,1,0:T(8,128)(2,1)} %param.17), kind=kOutput, calls=%fused_computation.18 | convolution fusion | flops 1207959552 | bytes 5898240 | tf_op jit(solution)/shard_map/dot_general | solution.py:12
  82.5 14.7 %all-to-all-done.1 = bf16[4,96,2048]{2,1,0:T(8,128)(2,1)} async-done(((bf16[4,96,2048]{2,1,0:T(8,128)(2,1)}), bf16[4,96,2048]{2,1,0:T(8,128)(2,1)}, u32[]{:S(2)}, u32[]{:S(2)}) %all-to-all-start.1) | async-done | bytes 1572896 | tf_op jit(solution)/shard_map/all_to_all | solution.py:94
  97.2 4.8 %fusion.6 = f32[384,768]{1,0:T(8,128)} fusion(bf16[384,2048]{1,0:T(8,128)(2,1)} %bitcast.19, bf16[1,1,2048,768]{3,2,1,0:T(8,128)(2,1)} %param.15), kind=kOutput, calls=%fused_computation.6 | convolution fusion | flops 1207959552 | bytes 5898240 | tf_op jit(solution)/shard_map/dot_general | solution.py:104
  102.0 7.8 %fusion.4 = f32[384,2048]{1,0:T(8,128)} fusion(bf16[1,1,2048,768]{3,2,1,0:T(8,128)(2,1)} %param.15, f32[384,768]{1,0:T(8,128)} %fusion.18, bf16[384,2048]{1,0:T(8,128)(2,1)} %bitcast.19, bf16[1,1,2048,768]{3,2,1,0:T(8,128)(2,1)S(1)} %copy-done, f32[384,768]{1,0:T(8,128)} %fusion.6), kind=kOutput, calls=%fused_computation.4 | convolution fusion | flops 2418868224 | bytes 13369344 | tf_op jit(solution)/shard_map/dot_general | solution.py:12
  109.8 4.0 %add_convert_fusion.1 = bf16[384,2048]{1,0:T(8,128)(2,1)S(1)} fusion(f32[384,2048]{1,0:T(8,128)} %fusion.4, bf16[1,1,2048,768]{3,2,1,0:T(8,128)(2,1)S(1)} %copy-done, f32[384,768]{1,0:T(8,128)} %fusion.18, f32[384,768]{1,0:T(8,128)} %fusion.6), kind=kOutput, calls=%fused_computation.22 | convolution fusion | flops 1211301888 | bytes 10223616 | tf_op jit(solution)/shard_map/dot_general | solution.py:12
  113.9 39.7 %all_to_all.30 = bf16[8,48,2048]{2,1,0:T(8,128)(2,1)S(1)} all-to-all(bf16[8,48,2048]{2,1,0:T(8,128)(2,1)S(1)} %bitcast.219), channel_id=1, replica_groups=mesh['section'=4,'half'=2,'quad'=4] {'quad','half'}, dimensions={0} | all-to-all | bytes 3145728 | tf_op jit(solution)/shard_map/all_to_all | solution.py:99
  155.9 24.1 %collective-permute-done.5 = bf16[128,2048]{1,0:T(8,128)(2,1)S(1)} collective-permute-done((bf16[128,2048]{1,0:T(8,128)(2,1)S(1)}, bf16[128,2048]{1,0:T(8,128)(2,1)S(1)}, u32[]{:S(2)}, u32[]{:S(2)}) %collective-permute-start.5) | collective-permute-done | bytes 524320 | tf_op jit(solution)/shard_map/ppermute | solution.py:22
  181.8 4.3 %all-to-all-start.4 = ((bf16[4,96,2048]{2,1,0:T(8,128)(2,1)}), bf16[4,96,2048]{2,1,0:T(8,128)(2,1)}, u32[]{:S(2)}, u32[]{:S(2)}) async-start(bf16[4,96,2048]{2,1,0:T(8,128)(2,1)} %bitcast.215), calls=%async_computation.4 | async-start | bytes 3145728 | tf_op jit(solution)/shard_map/all_to_all | solution.py:94
  190.3 2.9 multiply_convert_fusion
  193.2 12.0 %all-to-all-done.4 = bf16[4,96,2048]{2,1,0:T(8,128)(2,1)} async-done(((bf16[4,96,2048]{2,1,0:T(8,128)(2,1)}), bf16[4,96,2048]{2,1,0:T(8,128)(2,1)}, u32[]{:S(2)}, u32[]{:S(2)}) %all-to-all-start.4) | async-done | bytes 1572896 | tf_op jit(solution)/shard_map/all_to_all | solution.py:94
  205.2 4.3 %all-to-all-start.3 = ((bf16[8,48,2048]{2,1,0:T(8,128)(2,1)}), bf16[8,48,2048]{2,1,0:T(8,128)(2,1)}, u32[]{:S(2)}, u32[]{:S(2)}) async-start(bf16[8,48,2048]{2,1,0:T(8,128)(2,1)} %bitcast.212), calls=%async_computation.3 | async-start | bytes 3145728 | tf_op jit(solution)/shard_map/all_to_all | solution.py:99
  209.5 4.8 %fusion.2 = f32[384,768]{1,0:T(8,128)} fusion(bf16[384,2048]{1,0:T(8,128)(2,1)} %bitcast.38, bf16[1,1,2048,768]{3,2,1,0:T(8,128)(2,1)} %param.15), kind=kOutput, calls=%fused_computation.2 | convolution fusion | flops 1207959552 | bytes 5898240 | tf_op jit(solution)/shard_map/dot_general | solution.py:104
  214.3 29.4 %all-to-all-done.3 = bf16[8,48,2048]{2,1,0:T(8,128)(2,1)} async-done(((bf16[8,48,2048]{2,1,0:T(8,128)(2,1)}), bf16[8,48,2048]{2,1,0:T(8,128)(2,1)}, u32[]{:S(2)}, u32[]{:S(2)}) %all-to-all-start.3) | async-done | bytes 1572896 | tf_op jit(solution)/shard_map/all_to_all | solution.py:99
  243.7 4.8 %fusion.16 = f32[384,768]{1,0:T(8,128)} fusion(bf16[384,2048]{1,0:T(8,128)(2,1)} %bitcast.32, bf16[1,1,768,2048]{3,2,1,0:T(8,128)(2,1)} %param.17), kind=kOutput, calls=%fused_computation.16 | convolution fusion | flops 1207959552 | bytes 5898240 | tf_op jit(solution)/shard_map/dot_general | solution.py:12
  248.5 7.8 %fusion = f32[384,2048]{1,0:T(8,128)} fusion(bf16[1,1,2048,768]{3,2,1,0:T(8,128)(2,1)} %param.15, f32[384,768]{1,0:T(8,128)} %fusion.16, bf16[384,2048]{1,0:T(8,128)(2,1)} %bitcast.38, bf16[1,1,2048,768]{3,2,1,0:T(8,128)(2,1)S(1)} %copy-done, f32[384,768]{1,0:T(8,128)} %fusion.2), kind=kOutput, calls=%fused_computation | convolution fusion | flops 2418868224 | bytes 13369344 | tf_op jit(solution)/shard_map/dot_general | solution.py:12
  256.3 4.0 %add_convert_fusion = bf16[384,2048]{1,0:T(8,128)(2,1)S(1)} fusion(f32[384,2048]{1,0:T(8,128)} %fusion, bf16[1,1,2048,768]{3,2,1,0:T(8,128)(2,1)S(1)} %copy-done, f32[384,768]{1,0:T(8,128)} %fusion.16, f32[384,768]{1,0:T(8,128)} %fusion.2), kind=kOutput, calls=%fused_computation.20 | convolution fusion | flops 1211301888 | bytes 10223616 | tf_op jit(solution)/shard_map/dot_general | solution.py:12
  260.4 43.5 %all_to_all.31 = bf16[8,48,2048]{2,1,0:T(8,128)(2,1)S(1)} all-to-all(bf16[8,48,2048]{2,1,0:T(8,128)(2,1)S(1)} %bitcast.220), channel_id=1, replica_groups=mesh['section'=4,'half'=2,'quad'=4] {'quad','half'}, dimensions={0} | all-to-all | bytes 3145728 | tf_op jit(solution)/shard_map/all_to_all | solution.py:99
  (72 shorter events, 25.9 us)
Async XLA Ops:
  0.0 102.0 %copy-start = (bf16[1,1,2048,768]{3,2,1,0:T(8,128)(2,1)S(1)}, bf16[1,1,2048,768]{3,2,1,0:T(8,128)(2,1)}, u32[]{:S(2)}) copy-start(bf16[1,1,2048,768]{3,2,1,0:T(8,128)(2,1)} %param.16) | copy-start | bytes 9437188
  0.8 10.4 %collective-permute-start.2 = (bf16[128,2]{0,1:T(2,128)(2,1)S(1)}, bf16[128,2]{0,1:T(2,128)(2,1)S(1)}, u32[]{:S(2)}, u32[]{:S(2)}) collective-permute-start(bf16[128,2]{0,1:T(2,128)(2,1)S(1)} %get-tuple-element.35), channel_id=1, source_target_pairs={{0,4},{4,0},{1,5},{5,1},{2,6},{6,2},{3,7},{7,3},{8,12},{12,8},{9,1... | collective-permute-start | bytes 1544 | tf_op jit(solution)/shard_map/ppermute | solution.py:22
  7.1 15.8 %collective-permute-start = (s32[2,128,2]{1,2,0:T(2,128)S(1)}, s32[2,128,2]{1,2,0:T(2,128)S(1)}, u32[]{:S(2)}, u32[]{:S(2)}) collective-permute-start(s32[2,128,2]{1,2,0:T(2,128)S(1)} %pad_add_fusion.3), channel_id=1, source_target_pairs={{0,4},{4,0},{1,5},{5,1},{2,6},{6,2},{3,7},{7,3},{8,12},{12,8},{9,1... | collective-permute-start | bytes 6152 | tf_op jit(solution)/shard_map/ppermute | solution.py:22
  7.3 25.9 %collective-permute-start.1 = (bf16[128,2048]{1,0:T(8,128)(2,1)}, bf16[128,2048]{1,0:T(8,128)(2,1)}, u32[]{:S(2)}, u32[]{:S(2)}) collective-permute-start(bf16[128,2048]{1,0:T(8,128)(2,1)} %bitcast.221), channel_id=1, source_target_pairs={{0,4},{4,0},{1,5},{5,1},{2,6},{6,2},{3,7},{7,3},{8,12},{12,8},{9,1... | collective-permute-start | bytes 1572872 | tf_op jit(solution)/shard_map/ppermute | solution.py:22
  36.1 5.7 %copy-start.6 = (f32[1,2048]{1,0:T(1,128)S(1)}, f32[1,2048]{1,0:T(1,128)}, u32[]{:S(2)}) copy-start(f32[1,2048]{1,0:T(1,128)} %param.14) | copy-start | bytes 24580
  36.1 34.6 %all-to-all-start = ((bf16[4,96,2048]{2,1,0:T(8,128)(2,1)}), bf16[4,96,2048]{2,1,0:T(8,128)(2,1)}, u32[]{:S(2)}, u32[]{:S(2)}) async-start(bf16[4,96,2048]{2,1,0:T(8,128)(2,1)} %bitcast.216), calls=%async_computation | async-start | bytes 3145728 | tf_op jit(solution)/shard_map/all_to_all | solution.py:94
  43.1 25.3 %collective-permute-start.3 = (bf16[128,2048]{1,0:T(8,128)(2,1)S(1)}, bf16[128,2048]{1,0:T(8,128)(2,1)S(1)}, u32[]{:S(2)}, u32[]{:S(2)}) collective-permute-start(bf16[128,2048]{1,0:T(8,128)(2,1)S(1)} %fusion.52), channel_id=1, source_target_pairs={{0,4},{4,0},{1,5},{5,1},{2,6},{6,2},{3,7},{7,3},{8,12},{12,8},{9,1... | collective-permute-start | bytes 1572872 | tf_op jit(solution)/shard_map/ppermute | solution.py:22
  70.7 26.5 %all-to-all-start.1 = ((bf16[4,96,2048]{2,1,0:T(8,128)(2,1)}), bf16[4,96,2048]{2,1,0:T(8,128)(2,1)}, u32[]{:S(2)}, u32[]{:S(2)}) async-start(bf16[4,96,2048]{2,1,0:T(8,128)(2,1)} %bitcast.217), calls=%async_computation.1 | async-start | bytes 3145728 | tf_op jit(solution)/shard_map/all_to_all | solution.py:94
  113.9 39.7 %copy-start.1 = (bf16[2,1,128,2048]{3,2,1,0:T(8,128)(2,1)S(1)}, bf16[2,1,128,2048]{3,2,1,0:T(8,128)(2,1)}, u32[]{:S(2)}) copy-start(bf16[2,1,128,2048]{3,2,1,0:T(8,128)(2,1)} %param.9) | copy-start | bytes 3145732
  153.6 1.0 copy-start.5
  155.8 24.2 %collective-permute-start.5 = (bf16[128,2048]{1,0:T(8,128)(2,1)S(1)}, bf16[128,2048]{1,0:T(8,128)(2,1)S(1)}, u32[]{:S(2)}, u32[]{:S(2)}) collective-permute-start(bf16[128,2048]{1,0:T(8,128)(2,1)S(1)} %get-tuple-element.9), channel_id=1, source_target_pairs={{0,4},{4,0},{1,5},{5,1},{2,6},{6,2},{3,7},{7,3},{8,12},{12,8},{9,1... | collective-permute-start | bytes 1572872 | tf_op jit(solution)/shard_map/ppermute | solution.py:22
  181.8 23.4 %all-to-all-start.4 = ((bf16[4,96,2048]{2,1,0:T(8,128)(2,1)}), bf16[4,96,2048]{2,1,0:T(8,128)(2,1)}, u32[]{:S(2)}, u32[]{:S(2)}) async-start(bf16[4,96,2048]{2,1,0:T(8,128)(2,1)} %bitcast.215), calls=%async_computation.4 | async-start | bytes 3145728 | tf_op jit(solution)/shard_map/all_to_all | solution.py:94
  186.1 4.1 %collective-permute-start.4 = (bf16[128,2048]{1,0:T(8,128)(2,1)}, bf16[128,2048]{1,0:T(8,128)(2,1)}, u32[]{:S(2)}, u32[]{:S(2)}) collective-permute-start(bf16[128,2048]{1,0:T(8,128)(2,1)} %get-tuple-element.22), channel_id=1, source_target_pairs={{8,0},{16,8},{24,16},{9,1},{17,9},{25,17},{10,2},{18,10},{26,18},{... | collective-permute-start | bytes 1572872 | tf_op jit(solution)/shard_map/ppermute | solution.py:161
  205.2 38.5 %all-to-all-start.3 = ((bf16[8,48,2048]{2,1,0:T(8,128)(2,1)}), bf16[8,48,2048]{2,1,0:T(8,128)(2,1)}, u32[]{:S(2)}, u32[]{:S(2)}) async-start(bf16[8,48,2048]{2,1,0:T(8,128)(2,1)} %bitcast.212), calls=%async_computation.3 | async-start | bytes 3145728 | tf_op jit(solution)/shard_map/all_to_all | solution.py:99
  260.4 43.6 %copy-start.2 = (bf16[2,1,128,2048]{3,2,1,0:T(8,128)(2,1)S(1)}, bf16[2,1,128,2048]{3,2,1,0:T(8,128)(2,1)}, u32[]{:S(2)}) copy-start(bf16[2,1,128,2048]{3,2,1,0:T(8,128)(2,1)} %param.9) | copy-start | bytes 3145732
  303.9 1.0 copy-start.4
  305.0 1.5 copy-start.3

commit v2 on v1

--- a/solution.py
+++ b/solution.py
@@ -1,6 +1,10 @@
+import functools
+
 import jax
 import jax.numpy as jnp
 from jax import lax
+from jax.experimental import pallas as pl
+from jax.experimental.pallas import tpu as pltpu
 from jax.sharding import Mesh, PartitionSpec as P
 
 TICKS = 2
@@ -12,6 +16,96 @@
     return lax.dot_general(
         left, right, (((1,), (1,)), ((), ())), preferred_element_type=jnp.float32
     )
+
+
+def piece(size, want):
+    return want if size % want == 0 else size
+
+
+def pre_kernel(rows_ref, gate_ref, up_ref, pre_gate_ref, pre_up_ref):
+    rows = rows_ref[...]
+    pre_gate_ref[...] = jnp.dot(rows, gate_ref[...], preferred_element_type=jnp.float32)
+    pre_up_ref[...] = jnp.dot(rows, up_ref[...], preferred_element_type=jnp.float32)
+
+
+def pre_activations(rows, gate_matrix, up_matrix):
+    count, width = rows.shape
+    hidden = gate_matrix.shape[1]
+    part = piece(hidden, 256)
+    weight = pl.BlockSpec((width, part), lambda i: (0, i))
+    out = pl.BlockSpec((count, part), lambda i: (0, i))
+    return pl.pallas_call(
+        pre_kernel,
+        grid=(hidden // part,),
+        in_specs=[pl.BlockSpec((count, width), lambda i: (0, 0)), weight, weight],
+        out_specs=[out, out],
+        out_shape=[jax.ShapeDtypeStruct((count, hidden), jnp.float32)] * 2,
+        compiler_params=pltpu.CompilerParams(vmem_limit_bytes=24 * 2**20),
+        cost_estimate=pl.CostEstimate(
+            flops=4 * count * width * hidden,
+            bytes_accessed=4 * width * hidden + 2 * count * width + 8 * count * hidden,
+            transcendentals=0,
+        ),
+        name="pre_activations",
+    )(rows, gate_matrix, up_matrix)
+
+
+def backward_kernel(
+    parts, scaled_ref, pre_gate_ref, pre_up_ref, down_ref, gate_ref, up_ref, out_ref, gate_grad, up_grad
+):
+    step = pl.program_id(0)
+
+    @pl.when(step < parts)
+    def _():
+        hidden_grad = contract_last(scaled_ref[...], down_ref[...])
+        pre_gate = pre_gate_ref[...]
+        sigmoid = 1.0 / (1.0 + jnp.exp(-pre_gate))
+        both = hidden_grad * sigmoid
+        gate_grad[step] = (both * pre_up_ref[...] * (1.0 + pre_gate * (1.0 - sigmoid))).astype(
+            jnp.bfloat16
+        )
+        up_grad[step] = (both * pre_gate).astype(jnp.bfloat16)
+
+    @pl.when(step >= parts)
+    def _():
+        part = gate_grad.shape[2]
+        total = jnp.zeros(out_ref.shape, jnp.float32)
+        for k in range(parts):
+            columns = slice(k * part, (k + 1) * part)
+            total += contract_last(gate_grad[k], gate_ref[:, columns])
+            total += contract_last(up_grad[k], up_ref[:, columns])
+        out_ref[...] = total.astype(out_ref.dtype)
+
+
+def expert_backward(scaled, pre_gate, pre_up, gate_matrix, up_matrix, down_matrix):
+    count, width = scaled.shape
+    hidden = gate_matrix.shape[1]
+    part, column = piece(hidden, 256), piece(width, 256)
+    parts, columns = hidden // part, width // column
+    early = lambda i: (0, jnp.minimum(i, parts - 1))
+    late = lambda i: (jnp.maximum(i - parts, 0), 0)
+    return pl.pallas_call(
+        functools.partial(backward_kernel, parts),
+        grid=(parts + columns,),
+        in_specs=[
+            pl.BlockSpec((count, width), lambda i: (0, 0)),
+            pl.BlockSpec((count, part), early),
+            pl.BlockSpec((count, part), early),
+            pl.BlockSpec((part, width), lambda i: (jnp.minimum(i, parts - 1), 0)),
+            pl.BlockSpec((column, hidden), late),
+            pl.BlockSpec((column, hidden), late),
+        ],
+        out_specs=pl.BlockSpec((count, column), lambda i: (0, jnp.maximum(i - parts, 0))),
+        out_shape=jax.ShapeDtypeStruct((count, width), jnp.bfloat16),
+        scratch_shapes=[pltpu.VMEM((parts, count, part), jnp.bfloat16)] * 2,
+        compiler_params=pltpu.CompilerParams(vmem_limit_bytes=24 * 2**20),
+        cost_estimate=pl.CostEstimate(
+            flops=6 * count * width * hidden,
+            bytes_accessed=6 * width * hidden + 4 * count * width + 8 * count * hidden,
+            transcendentals=count * hidden,
+        ),
+        name="expert_backward",
+    )(scaled, pre_gate, pre_up, down_matrix, gate_matrix, up_matrix)
 
 
 def after(value, *others):
@@ -90,29 +184,13 @@
         mirror = gate_of(mirror_place, mirror_gates, jnp.where(own_row, -1, wanted))
         return own + mirror
 
-    def quad_exchange(packed):
+    def exchange(packed, axes):
         return lax.all_to_all(
-            packed.reshape(quads, 2 * slots, width), "quad", split_axis=0, concat_axis=0, tiled=True
-        ).reshape(rows, width)
-
-    def full_exchange(packed):
-        return lax.all_to_all(
-            packed.reshape(experts, slots, width), BOTH, split_axis=0, concat_axis=0, tiled=True
-        ).reshape(rows, width)
-
-    def hidden(normed_rows):
-        pre_gate = jnp.dot(normed_rows, gate_matrix, preferred_element_type=jnp.float32)
-        pre_up = jnp.dot(normed_rows, up_matrix, preferred_element_type=jnp.float32)
-        return pre_gate, pre_up
-
-    def backward(pre_gate, pre_up, hidden_grad):
-        sigmoid = jax.nn.sigmoid(pre_gate)
-        gate_grad = (
-            hidden_grad * pre_up * sigmoid * (1.0 + pre_gate * (1.0 - sigmoid))
-        ).astype(jnp.bfloat16)
-        up_grad = (hidden_grad * pre_gate * sigmoid).astype(jnp.bfloat16)
-        summed = contract_last(gate_grad, gate_matrix) + contract_last(up_grad, up_matrix)
-        return summed.astype(jnp.bfloat16)
+            packed.reshape(lax.axis_size(axes), -1, width), axes, split_axis=0, concat_axis=0, tiled=True
+        )
+
+    def place_rows(chosen, values):
+        return jnp.dot(chosen, values, preferred_element_type=jnp.bfloat16)
 
     def combine(t, incoming, returned, place, inverse):
         chosen = select(place, jnp.arange(rows, dtype=jnp.int32))
@@ -137,33 +215,39 @@
     normed0_mirror = swap(after(normed0, grad_mirror))
     normed1_mirror = swap(after(normed1, normed0_mirror))
 
+    half_index = jnp.arange(quads * slots, dtype=jnp.int32)
+    half_wanted = (half_index // slots * 2 + half_here) * slots + half_index % slots
+    rows1_own = exchange(place_rows(select(place[1], half_wanted), normed1), "quad")
+
     pair0 = pair_select(place[0], place_mirror[0])
-    pair1 = pair_select(place[1], place_mirror[1])
     scale0 = pair_gate(place[0], gates[0], place_mirror[0], gates_mirror)
 
     both = jnp.concatenate([entering[0], grad_mirror], axis=0)
     packed = jnp.dot(pair0, both, preferred_element_type=jnp.float32)
-    scaled0 = quad_exchange((packed * scale0[:, None]).astype(jnp.bfloat16))
-    hidden_grad0 = contract_last(scaled0, down_matrix)
+    packed = (packed * scale0[:, None]).astype(jnp.bfloat16)
+    scaled0 = exchange(after(packed, rows1_own), "quad").reshape(rows, width)
 
     both = jnp.concatenate([normed0, normed0_mirror], axis=0)
-    rows0 = quad_exchange(jnp.dot(pair0, both, preferred_element_type=jnp.bfloat16))
-    pre_gate0, pre_up0 = hidden(rows0)
-    computed0 = backward(pre_gate0, pre_up0, hidden_grad0)
-    returned0 = full_exchange(computed0)
-
-    both = jnp.concatenate([normed1, normed1_mirror], axis=0)
-    packed1 = jnp.dot(pair1, both, preferred_element_type=jnp.bfloat16)
-    rows1 = quad_exchange(after(packed1, returned0))
+    rows0 = exchange(after(place_rows(pair0, both), scaled0), "quad").reshape(rows, width)
+    pre_gate0, pre_up0 = pre_activations(after(rows0, normed1_mirror), gate_matrix, up_matrix)
+    computed0 = expert_backward(scaled0, pre_gate0, pre_up0, gate_matrix, up_matrix, down_matrix)
+    packed1 = place_rows(select(place_mirror[1], half_wanted), normed1_mirror)
+    returned0 = exchange(computed0, BOTH).reshape(rows, width)
+    rows1_mirror = exchange(after(packed1, returned0), "quad")
     result0 = combine(0, entering[0], returned0, place[0], inverse0)
 
     length = section_last + 1
     arrived = lax.ppermute(result0, "section", [(i, i - 1) for i in range(1, length)])
     incoming = jnp.where(section_here == section_last, fresh[0], arrived)
-    scaled1 = full_exchange(incoming_pack(incoming, place[1], gates[1]))
-    pre_gate1, pre_up1 = hidden(rows1)
-    computed1 = backward(pre_gate1, pre_up1, contract_last(scaled1, down_matrix))
-    returned1 = full_exchange(computed1)
+    scaled1 = after(incoming_pack(incoming, place[1], gates[1]), rows1_mirror)
+    scaled1 = exchange(scaled1, BOTH).reshape(rows, width)
+    first = half_here == 0
+    rows1 = jnp.stack(
+        [jnp.where(first, rows1_own, rows1_mirror), jnp.where(first, rows1_mirror, rows1_own)], axis=1
+    ).reshape(rows, width)
+    pre_gate1, pre_up1 = pre_activations(rows1, gate_matrix, up_matrix)
+    computed1 = expert_backward(scaled1, pre_gate1, pre_up1, gate_matrix, up_matrix, down_matrix)
+    returned1 = exchange(computed1, BOTH).reshape(rows, width)
     result1 = combine(1, incoming, returned1, place[1], inverse1)
     return jnp.stack([result0, result1], axis=0)[:, None]
 

time: 308 us -> 287 us (0.932)
  matrix products: 53.9 us -> 15 us
  blocking collectives: 83.2 us -> 45.4 us
  Pallas kernels: 0 us -> 23 us
  local copies, waits for them, and re-layouts: 3.75 us -> 18.9 us
  starting transfers between devices: 30.5 us -> 39.4 us
  waiting for transfers between devices: 128 us -> 133 us
    dot_general x10 -> x3, matrix products: 46.4 us -> 5.39 us  [place_rows(): return jnp.dot(chosen, values, preferred_element_type=jnp.bfloat16)]
    all_to_all x2 -> x1, blocking collectives: 83.2 us -> 45.4 us  [exchange(): lax.all_to_all(packed.reshape(lax.axis_size(axes), -1, width), axes, spli...]
    pallas_call x0 -> x4, Pallas kernels: none -> 23 us  [the longest x2 14.5 us: expert_backward(): pl.pallas_call(functools.partial(backward_kernel, parts), grid=(parts + c...]
    unnamed x16 -> x40, local copies, waits for them, and re-layouts: 1.06 us -> 16 us
    all_to_all x4 -> x6, starting transfers between devices: 20.1 us -> 28.5 us  [exchange(): lax.all_to_all(packed.reshape(lax.axis_size(axes), -1, width), axes, spli...]
    all_to_all x4 -> x6, waiting for transfers between devices: 56.7 us -> 62.8 us  [exchange(): lax.all_to_all(packed.reshape(lax.axis_size(axes), -1, width), axes, spli...]
  transfers between devices with their start and end apart: 10 -> 12, of which waited for: 9 -> 11; matrix products, arithmetic and copies ran while one was open for 7% -> 7% of each run, Pallas kernels for 0% -> 1%
where the time goes in v2:
time: 287 us; the launch traced here: 285 us
  waiting for transfers between devices  133 us (46%)
  blocking collectives  45.4 us (16%)
  starting transfers between devices  39.4 us (14%)
  Pallas kernels  23 us (8%)
  local copies, waits for them, and re-layouts  18.9 us (7%)
  matrix products  15 us (5%)
  other arithmetic  10.6 us (4%)
    ppermute x5, waiting for transfers between devices, swap(): return lax.ppermute(value, 'half', [(0, 1), (1, 0)])  67.3 us
    all_to_all x6, waiting for transfers between devices, exchange(): lax.all_to_all(packed.reshape(lax.axis_size(axes), -1, width), axes, spli...  62.8 us
    all_to_all x1, blocking collectives, exchange(): lax.all_to_all(packed.reshape(lax.axis_size(axes), -1, width), axes, spli...  45.4 us
    all_to_all x6, starting transfers between devices, exchange(): lax.all_to_all(packed.reshape(lax.axis_size(axes), -1, width), axes, spli...  28.5 us
    unnamed x40, local copies, waits for them, and re-layouts  16 us
    pallas_call x2, Pallas kernels, expert_backward(): pl.pallas_call(functools.partial(backward_kernel, parts), grid=(parts + c...  14.5 us
    ppermute x5, starting transfers between devices, swap(): return lax.ppermute(value, 'half', [(0, 1), (1, 0)])  9.65 us
    pallas_call x2, Pallas kernels, pre_activations(): pl.pallas_call(pre_kernel, grid=(hidden // part,), in_specs=[pl.BlockSpec...  8.51 us
  transfers between devices with their start and end apart: 12, of which 11 were waited for; matrix products, arithmetic and copies ran while one was open for 7% of the time, Pallas kernels for 1%

profile of v2, /device:TPU:0, one launch (start us, length us, event | category | flops | bytes accessed | tf_op | source)
XLA Modules:
  0.0 285.5 jit_solution(7753422801034949347)
XLA Ops:
  2.3 4.1 %collective-permute-start = (s32[2,128,2]{1,2,0:T(2,128)S(1)}, s32[2,128,2]{1,2,0:T(2,128)S(1)}, u32[]{:S(2)}, u32[]{:S(2)}) collective-permute-start(s32[2,128,2]{1,2,0:T(2,128)S(1)} %pad_add_fusion.3), channel_id=1, source_target_pairs={{0,4},{4,0},{1,5},{5,1},{2,6},{6,2},{3,7},{7,3},{8,12},{12,8},{9,1... | collective-permute-start | bytes 6152 | tf_op jit(solution)/shard_map/ppermute | solution.py:116
  7.1 2.9 %collective-permute-start.1 = (bf16[128,2048]{1,0:T(8,128)(2,1)}, bf16[128,2048]{1,0:T(8,128)(2,1)}, u32[]{:S(2)}, u32[]{:S(2)}) collective-permute-start(bf16[128,2048]{1,0:T(8,128)(2,1)} %bitcast.211), channel_id=1, source_target_pairs={{0,4},{4,0},{1,5},{5,1},{2,6},{6,2},{3,7},{7,3},{8,12},{12,8},{9,1... | collective-permute-start | bytes 1572872 | tf_op jit(solution)/shard_map/ppermute | solution.py:116
  12.1 3.8 %all-to-all-start = ((bf16[4,48,2048]{2,1,0:T(8,128)(2,1)}), bf16[4,48,2048]{2,1,0:T(8,128)(2,1)S(1)}, u32[]{:S(2)}, u32[]{:S(2)}) async-start(bf16[4,48,2048]{2,1,0:T(8,128)(2,1)} %fusion.30), calls=%async_computation | async-start | bytes 1572864 | tf_op jit(solution)/shard_map/all_to_all | solution.py:188
  16.7 4.5 %collective-permute-done.2 = bf16[128,2]{0,1:T(2,128)(2,1)S(1)} collective-permute-done((bf16[128,2]{0,1:T(2,128)(2,1)S(1)}, bf16[128,2]{0,1:T(2,128)(2,1)S(1)}, u32[]{:S(2)}, u32[]{:S(2)}) %collective-permute-start.2) | collective-permute-done | bytes 544 | tf_op jit(solution)/shard_map/ppermute | solution.py:116
  21.6 11.4 %collective-permute-done.1 = bf16[128,2048]{1,0:T(8,128)(2,1)} collective-permute-done((bf16[128,2048]{1,0:T(8,128)(2,1)}, bf16[128,2048]{1,0:T(8,128)(2,1)}, u32[]{:S(2)}, u32[]{:S(2)}) %collective-permute-start.1) | collective-permute-done | bytes 524320 | tf_op jit(solution)/shard_map/ppermute | solution.py:116
  33.1 2.8 multiply_convert_fusion.1
  36.9 3.6 %all-to-all-start.1 = ((bf16[4,96,2048]{2,1,0:T(8,128)(2,1)}), bf16[4,96,2048]{2,1,0:T(8,128)(2,1)S(1)}, u32[]{:S(2)}, u32[]{:S(2)}) async-start(bf16[4,96,2048]{2,1,0:T(8,128)(2,1)} %bitcast.209), calls=%async_computation.1 | async-start | bytes 3145728 | tf_op jit(solution)/shard_map/all_to_all | solution.py:188
  44.1 24.1 %collective-permute-done.3 = bf16[128,2048]{1,0:T(8,128)(2,1)S(1)} collective-permute-done((bf16[128,2048]{1,0:T(8,128)(2,1)S(1)}, bf16[128,2048]{1,0:T(8,128)(2,1)S(1)}, u32[]{:S(2)}, u32[]{:S(2)}) %collective-permute-start.3) | collective-permute-done | bytes 524320 | tf_op jit(solution)/shard_map/ppermute | solution.py:116
  71.5 7.5 %all-to-all-start.2 = ((bf16[4,96,2048]{2,1,0:T(8,128)(2,1)}), bf16[4,96,2048]{2,1,0:T(8,128)(2,1)}, u32[]{:S(2)}, u32[]{:S(2)}) async-start(bf16[4,96,2048]{2,1,0:T(8,128)(2,1)} %bitcast.210), calls=%async_computation.2 | async-start | bytes 3145728 | tf_op jit(solution)/shard_map/all_to_all | solution.py:188
  79.0 27.4 %collective-permute-done.4 = bf16[128,2048]{1,0:T(8,128)(2,1)} collective-permute-done((bf16[128,2048]{1,0:T(8,128)(2,1)}, bf16[128,2048]{1,0:T(8,128)(2,1)}, u32[]{:S(2)}, u32[]{:S(2)}) %collective-permute-start.4) | collective-permute-done | bytes 524320 | tf_op jit(solution)/shard_map/ppermute | solution.py:116
  106.4 2.8 all-to-all-done.2
  111.2 5.0 %pre_activations.2 = (f32[384,768]{1,0:T(8,128)S(1)}, f32[384,768]{1,0:T(8,128)S(1)}) custom-call(bf16[384,2048]{1,0:T(8,128)(2,1)} %bitcast.22.rows_ref, bf16[2048,768]{1,0:T(8,128)(2,1)S(1)} %bitcast.192, bf16[2048,768]{1,0:T(8,128)(2,1)S(1)} %bitcast.196), custom_call_target="tpu_custom_call" | custom-call | flops 2415919104 | bytes 10223616 | tf_op jit(solution)/shard_map/pre_activations/pallas_call | solution.py:37
  116.2 6.6 %expert_backward.2 = bf16[384,2048]{1,0:T(8,128)(2,1)S(1)} custom-call(bf16[384,2048]{1,0:T(8,128)(2,1)S(1)} %bitcast.202, f32[384,768]{1,0:T(8,128)S(1)} %get-tuple-element.21.pre_gate_ref, f32[384,768]{1,0:T(8,128)S(1)} %get-tuple-element.22.pre_up_ref, bf16[768,2048]{1,0:T(8,128)(2,1)S(1)} %bitcast.200, bf16[2048,768]{1,0:T(8,128)(2,1)S(1)} %bitcast.193, ...), custom_call_target="tpu_custom_call" | custom-call | flops 3623878656 | bytes 14942208 | tf_op jit(solution)/shard_map/expert_backward/pallas_call | solution.py:87
  123.9 4.3 %all-to-all-start.3 = ((bf16[8,48,2048]{2,1,0:T(8,128)(2,1)}), bf16[8,48,2048]{2,1,0:T(8,128)(2,1)}, u32[]{:S(2)}, u32[]{:S(2)}) async-start(bf16[8,48,2048]{2,1,0:T(8,128)(2,1)} %bitcast.203), calls=%async_computation.3 | async-start | bytes 3145728 | tf_op jit(solution)/shard_map/all_to_all | solution.py:188
  130.6 32.6 %all-to-all-done.3 = bf16[8,48,2048]{2,1,0:T(8,128)(2,1)} async-done(((bf16[8,48,2048]{2,1,0:T(8,128)(2,1)}), bf16[8,48,2048]{2,1,0:T(8,128)(2,1)}, u32[]{:S(2)}, u32[]{:S(2)}) %all-to-all-start.3) | async-done | bytes 1572896 | tf_op jit(solution)/shard_map/all_to_all | solution.py:188
  163.1 3.0 %fusion.21 = (f32[128]{0:T(128)S(1)}, f32[128,2048]{1,0:T(8,128)}) fusion(bf16[2,1,128,2048]{3,2,1,0:T(8,128)(2,1)} %param.9, bf16[384,2048]{1,0:T(8,128)(2,1)} %bitcast.27, s32[128]{0:T(128)S(1)} %get-tuple-element.29, s32[128]{0:T(128)S(1)} %get-tuple-element.30, f32[2048]{0:T(1024)S(1)} %bitcast.215), kind=kOutput, calls=%fused_computation.34 | convolution fusion | flops 202522496 | bytes 3155456 | tf_op jit(solution)/shard_map/dot_general | solution.py:197
  166.1 5.0 %all-to-all-start.4 = ((bf16[4,48,2048]{2,1,0:T(8,128)(2,1)}), bf16[4,48,2048]{2,1,0:T(8,128)(2,1)}, u32[]{:S(2)}, u32[]{:S(2)}) async-start(bf16[4,48,2048]{2,1,0:T(8,128)(2,1)} %bitcast.208), calls=%async_computation.4 | async-start | bytes 1572864 | tf_op jit(solution)/shard_map/all_to_all | solution.py:188
  171.1 2.7 fusion.20
  178.0 2.9 %multiply_convert_fusion = bf16[384,2048]{1,0:T(8,128)(2,1)} fusion(f32[384]{0:T(512)S(1)} %add.290, bf16[128,2048]{1,0:T(8,128)(2,1)} %collective-permute-done.5, bf16[1,128,2048]{2,1,0:T(8,128)(2,1)} %param.11, pred[]{:T(512)S(6)} %eq.160, s32[128]{0:T(128)S(1)} %get-tuple-element.31, s32[128]{0:T(128)S(1)} %get-tuple-element.32), kind=kOutput, calls=%fused_computation | convolution fusion | flops 203309056 | bytes 2624001 | tf_op jit(solution)/shard_map/dot_general | solution.py:169
  182.8 4.3 %all-to-all-start.5 = ((bf16[8,48,2048]{2,1,0:T(8,128)(2,1)}), bf16[8,48,2048]{2,1,0:T(8,128)(2,1)}, u32[]{:S(2)}, u32[]{:S(2)}) async-start(bf16[8,48,2048]{2,1,0:T(8,128)(2,1)} %bitcast.206), calls=%async_computation.5 | async-start | bytes 3145728 | tf_op jit(solution)/shard_map/all_to_all | solution.py:188
  190.6 3.5 %pre_activations.3 = (f32[384,768]{1,0:T(8,128)S(1)}, f32[384,768]{1,0:T(8,128)S(1)}) custom-call(bf16[384,2048]{1,0:T(8,128)(2,1)S(1)} %bitcast.205, bf16[2048,768]{1,0:T(8,128)(2,1)S(1)} %bitcast.194, bf16[2048,768]{1,0:T(8,128)(2,1)S(1)} %bitcast.198), custom_call_target="tpu_custom_call" | custom-call | flops 2415919104 | bytes 10223616 | tf_op jit(solution)/shard_map/pre_activations/pallas_call | solution.py:37
  196.2 24.9 %all-to-all-done.5 = bf16[8,48,2048]{2,1,0:T(8,128)(2,1)} async-done(((bf16[8,48,2048]{2,1,0:T(8,128)(2,1)}), bf16[8,48,2048]{2,1,0:T(8,128)(2,1)}, u32[]{:S(2)}, u32[]{:S(2)}) %all-to-all-start.5) | async-done | bytes 1572896 | tf_op jit(solution)/shard_map/all_to_all | solution.py:188
  227.4 7.9 %expert_backward.3 = bf16[384,2048]{1,0:T(8,128)(2,1)S(1)} custom-call(bf16[384,2048]{1,0:T(8,128)(2,1)} %bitcast.38.scaled_ref, f32[384,768]{1,0:T(8,128)S(1)} %copy-done.10, f32[384,768]{1,0:T(8,128)S(1)} %copy-done.12, bf16[768,2048]{1,0:T(8,128)(2,1)S(1)} %bitcast.201, bf16[2048,768]{1,0:T(8,128)(2,1)S(1)} %bitcast.195, bf16[2048,768]{1,0:T(8,128)(2,1)S(1)} %bitcast.199), custom_call_target="tpu_custom_call" | custom-call | flops 3623878656 | bytes 14942208 | tf_op jit(solution)/shard_map/expert_backward/pallas_call | solution.py:87
  235.4 45.4 %all_to_all.35 = bf16[8,48,2048]{2,1,0:T(8,128)(2,1)S(1)} all-to-all(bf16[8,48,2048]{2,1,0:T(8,128)(2,1)S(1)} %bitcast.204), channel_id=1, replica_groups=mesh['section'=4,'half'=2,'quad'=4] {'quad','half'}, dimensions={0} | all-to-all | bytes 3145728 | tf_op jit(solution)/shard_map/all_to_all | solution.py:188
  (100 shorter events, 42.1 us)
Async XLA Ops:
  0.0 10.4 %copy-start.13 = (bf16[2,1,128,2048]{3,2,1,0:T(8,128)(2,1)S(1)}, bf16[2,1,128,2048]{3,2,1,0:T(8,128)(2,1)}, u32[]{:S(2)}) copy-start(bf16[2,1,128,2048]{3,2,1,0:T(8,128)(2,1)} %param.9) | copy-start | bytes 3145732
  0.0 10.8 %copy-start.18 = (f32[1,2048]{1,0:T(1,128)S(1)}, f32[1,2048]{1,0:T(1,128)}, u32[]{:S(2)}) copy-start(f32[1,2048]{1,0:T(1,128)} %param.14) | copy-start | bytes 24580
  2.3 18.9 %collective-permute-start = (s32[2,128,2]{1,2,0:T(2,128)S(1)}, s32[2,128,2]{1,2,0:T(2,128)S(1)}, u32[]{:S(2)}, u32[]{:S(2)}) collective-permute-start(s32[2,128,2]{1,2,0:T(2,128)S(1)} %pad_add_fusion.3), channel_id=1, source_target_pairs={{0,4},{4,0},{1,5},{5,1},{2,6},{6,2},{3,7},{7,3},{8,12},{12,8},{9,1... | collective-permute-start | bytes 6152 | tf_op jit(solution)/shard_map/ppermute | solution.py:116
  7.1 14.1 %collective-permute-start.2 = (bf16[128,2]{0,1:T(2,128)(2,1)S(1)}, bf16[128,2]{0,1:T(2,128)(2,1)S(1)}, u32[]{:S(2)}, u32[]{:S(2)}) collective-permute-start(bf16[128,2]{0,1:T(2,128)(2,1)S(1)} %get-tuple-element.49), channel_id=1, source_target_pairs={{0,4},{4,0},{1,5},{5,1},{2,6},{6,2},{3,7},{7,3},{8,12},{12,8},{9,1... | collective-permute-start | bytes 1544 | tf_op jit(solution)/shard_map/ppermute | solution.py:116
  7.1 26.0 %collective-permute-start.1 = (bf16[128,2048]{1,0:T(8,128)(2,1)}, bf16[128,2048]{1,0:T(8,128)(2,1)}, u32[]{:S(2)}, u32[]{:S(2)}) collective-permute-start(bf16[128,2048]{1,0:T(8,128)(2,1)} %bitcast.211), channel_id=1, source_target_pairs={{0,4},{4,0},{1,5},{5,1},{2,6},{6,2},{3,7},{7,3},{8,12},{12,8},{9,1... | collective-permute-start | bytes 1572872 | tf_op jit(solution)/shard_map/ppermute | solution.py:116
  10.8 22.3 %copy-start.17 = (bf16[1,128,2048]{2,1,0:T(8,128)(2,1)S(1)}, bf16[1,128,2048]{2,1,0:T(8,128)(2,1)}, u32[]{:S(2)}) copy-start(bf16[1,128,2048]{2,1,0:T(8,128)(2,1)} %param.10) | copy-start | bytes 1572868
  12.1 23.9 %all-to-all-start = ((bf16[4,48,2048]{2,1,0:T(8,128)(2,1)}), bf16[4,48,2048]{2,1,0:T(8,128)(2,1)S(1)}, u32[]{:S(2)}, u32[]{:S(2)}) async-start(bf16[4,48,2048]{2,1,0:T(8,128)(2,1)} %fusion.30), calls=%async_computation | async-start | bytes 1572864 | tf_op jit(solution)/shard_map/all_to_all | solution.py:188
  36.9 33.4 %all-to-all-start.1 = ((bf16[4,96,2048]{2,1,0:T(8,128)(2,1)}), bf16[4,96,2048]{2,1,0:T(8,128)(2,1)S(1)}, u32[]{:S(2)}, u32[]{:S(2)}) async-start(bf16[4,96,2048]{2,1,0:T(8,128)(2,1)} %bitcast.209), calls=%async_computation.1 | async-start | bytes 3145728 | tf_op jit(solution)/shard_map/all_to_all | solution.py:188
  41.5 26.6 %collective-permute-start.3 = (bf16[128,2048]{1,0:T(8,128)(2,1)S(1)}, bf16[128,2048]{1,0:T(8,128)(2,1)S(1)}, u32[]{:S(2)}, u32[]{:S(2)}) collective-permute-start(bf16[128,2048]{1,0:T(8,128)(2,1)S(1)} %get-tuple-element.17), channel_id=1, source_target_pairs={{0,4},{4,0},{1,5},{5,1},{2,6},{6,2},{3,7},{7,3},{8,12},{12,8},{9,1... | collective-permute-start | bytes 1572872 | tf_op jit(solution)/shard_map/ppermute | solution.py:116
  71.5 37.8 %copy-start = (bf16[1,1,2048,768]{3,2,1,0:T(8,128)(2,1)S(1)}, bf16[1,1,2048,768]{3,2,1,0:T(8,128)(2,1)}, u32[]{:S(2)}) copy-start(bf16[1,1,2048,768]{3,2,1,0:T(8,128)(2,1)} %param.15) | copy-start | bytes 9437188
  71.5 37.8 %all-to-all-start.2 = ((bf16[4,96,2048]{2,1,0:T(8,128)(2,1)}), bf16[4,96,2048]{2,1,0:T(8,128)(2,1)}, u32[]{:S(2)}, u32[]{:S(2)}) async-start(bf16[4,96,2048]{2,1,0:T(8,128)(2,1)} %bitcast.210), calls=%async_computation.2 | async-start | bytes 3145728 | tf_op jit(solution)/shard_map/all_to_all | solution.py:188
  79.0 27.4 %collective-permute-start.4 = (bf16[128,2048]{1,0:T(8,128)(2,1)}, bf16[128,2048]{1,0:T(8,128)(2,1)}, u32[]{:S(2)}, u32[]{:S(2)}) collective-permute-start(bf16[128,2048]{1,0:T(8,128)(2,1)} %get-tuple-element.19), channel_id=1, source_target_pairs={{0,4},{4,0},{1,5},{5,1},{2,6},{6,2},{3,7},{7,3},{8,12},{12,8},{9,1... | collective-permute-start | bytes 1572872 | tf_op jit(solution)/shard_map/ppermute | solution.py:116
  109.3 1.9 copy-start.1
  111.2 5.0 %copy-start.4 = (bf16[1,1,768,2048]{3,2,1,0:T(8,128)(2,1)S(1)}, bf16[1,1,768,2048]{3,2,1,0:T(8,128)(2,1)}, u32[]{:S(2)}) copy-start(bf16[1,1,768,2048]{3,2,1,0:T(8,128)(2,1)} %param.17) | copy-start | bytes 9437188
  111.2 5.0 %copy-start.7 = (bf16[4,96,2048]{2,1,0:T(8,128)(2,1)S(1)}, bf16[4,96,2048]{2,1,0:T(8,128)(2,1)}, u32[]{:S(2)}) copy-start(bf16[4,96,2048]{2,1,0:T(8,128)(2,1)} %copy-done.6) | copy-start | bytes 4718596
  123.9 39.2 %all-to-all-start.3 = ((bf16[8,48,2048]{2,1,0:T(8,128)(2,1)}), bf16[8,48,2048]{2,1,0:T(8,128)(2,1)}, u32[]{:S(2)}, u32[]{:S(2)}) async-start(bf16[8,48,2048]{2,1,0:T(8,128)(2,1)} %bitcast.203), calls=%async_computation.3 | async-start | bytes 3145728 | tf_op jit(solution)/shard_map/all_to_all | solution.py:188
  166.1 16.6 %all-to-all-start.4 = ((bf16[4,48,2048]{2,1,0:T(8,128)(2,1)}), bf16[4,48,2048]{2,1,0:T(8,128)(2,1)}, u32[]{:S(2)}, u32[]{:S(2)}) async-start(bf16[4,48,2048]{2,1,0:T(8,128)(2,1)} %bitcast.208), calls=%async_computation.4 | async-start | bytes 1572864 | tf_op jit(solution)/shard_map/all_to_all | solution.py:188
  173.8 4.1 %collective-permute-start.5 = (bf16[128,2048]{1,0:T(8,128)(2,1)}, bf16[128,2048]{1,0:T(8,128)(2,1)}, u32[]{:S(2)}, u32[]{:S(2)}) collective-permute-start(bf16[128,2048]{1,0:T(8,128)(2,1)} %fusion.20), channel_id=1, source_target_pairs={{8,0},{16,8},{24,16},{9,1},{17,9},{25,17},{10,2},{18,10},{26,18},{... | collective-permute-start | bytes 1572872 | tf_op jit(solution)/shard_map/ppermute | solution.py:240
  182.8 38.4 %all-to-all-start.5 = ((bf16[8,48,2048]{2,1,0:T(8,128)(2,1)}), bf16[8,48,2048]{2,1,0:T(8,128)(2,1)}, u32[]{:S(2)}, u32[]{:S(2)}) async-start(bf16[8,48,2048]{2,1,0:T(8,128)(2,1)} %bitcast.206), calls=%async_computation.5 | async-start | bytes 3145728 | tf_op jit(solution)/shard_map/all_to_all | solution.py:188
  188.7 1.9 copy-start.2
  221.1 1.9 copy-start.3
  223.0 1.9 copy-start.5
  226.2 1.3 copy-start.12
  235.4 45.5 %copy-start.14 = (bf16[2,1,128,2048]{3,2,1,0:T(8,128)(2,1)S(1)}, bf16[2,1,128,2048]{3,2,1,0:T(8,128)(2,1)}, u32[]{:S(2)}) copy-start(bf16[2,1,128,2048]{3,2,1,0:T(8,128)(2,1)} %param.9) | copy-start | bytes 3145732
  (7 other events, 7.6 us)

commit v3 on v0

v3 whole, which is shorter than its diff:
```python
import functools

import jax
import jax.numpy as jnp
from jax import lax
from jax.experimental import pallas as pl
from jax.experimental.pallas import tpu as pltpu
from jax.sharding import PartitionSpec as P

TICKS = 2
TOPK = 2
SUBLANES = 16

VMEM_WHOLE = pl.BlockSpec(memory_space=pltpu.VMEM)


def piece(size, want):
    return want if size % want == 0 else size


def contract_last(left, right):
    return lax.dot_general(
        left, right, (((1,), (1,)), ((), ())), preferred_element_type=jnp.float32
    )


def params(limit=16):
    return pltpu.CompilerParams(vmem_limit_bytes=limit * 2**20)


def aligned(slots):
    return slots % SUBLANES == 0


def slab_shapes(slabs, slots, width):
    if aligned(slots):
        return [jax.ShapeDtypeStruct((slots, width), jnp.bfloat16)] * slabs
    return [jax.ShapeDtypeStruct((slabs * slots, width), jnp.bfloat16)]


def to_slabs(outs, slabs, slots):
    if aligned(slots):
        return list(outs)
    return [outs[0][k * slots : (k + 1) * slots] for k in range(slabs)]


def from_slabs(slabs):
    if aligned(slabs[0].shape[0]):
        return list(slabs)
    return [jnp.concatenate(slabs, axis=0)]


def store_slabs(value, refs, columns):
    rows = refs[0].shape[0]
    for k, ref in enumerate(refs):
        ref[:, columns] = value[k * rows : (k + 1) * rows].astype(ref.dtype)


def gather_slabs(refs, rows_ref):
    start = 0
    for ref in refs:
        rows_ref[start : start + ref.shape[0], :] = ref[...]
        start += ref.shape[0]


def slot_hits(info_ref, first, rows, base):
    slot = lax.broadcasted_iota(jnp.int32, (rows, info_ref.shape[1]), 0) + base
    return [slot == info_ref[first + k : first + k + 1, :].astype(jnp.int32) for k in range(TOPK)]


def one_hot(hits):
    total = jnp.where(hits[0], 1.0, 0.0)
    for hit in hits[1:]:
        total = total + jnp.where(hit, 1.0, 0.0)
    return total.astype(jnp.bfloat16)


def slot_gates(hits, info_ref, first):
    total = jnp.zeros((hits[0].shape[0], 1), jnp.float32)
    for k, hit in enumerate(hits):
        gates = info_ref[first + k : first + k + 1, :]
        total = total + jnp.sum(jnp.where(hit, gates, 0.0), axis=1, keepdims=True)
    return total


def inverse_of(x_ref):
    xfloat = x_ref[...].astype(jnp.float32)
    return lax.rsqrt(jnp.mean(xfloat * xfloat, axis=1, keepdims=True) + 1e-05)


def whole(shape):
    return pl.BlockSpec(shape, lambda *_: (0,) * len(shape))


def pack_normed_kernel(rows, first, base, info_ref, x_ref, gain_ref, *outs):
    chosen = one_hot(slot_hits(info_ref, first, rows, base))
    inverse = inverse_of(x_ref)
    width = x_ref.shape[1]
    part = piece(width, 512)
    for start in range(0, width, part):
        columns = slice(start, start + part)
        normed = (x_ref[:, columns].astype(jnp.float32) * inverse * gain_ref[:, columns]).astype(
            jnp.bfloat16
        )
        store_slabs(jnp.dot(chosen, normed, preferred_element_type=jnp.float32), outs, columns)


def pack_scaled_kernel(rows, first, base, info_ref, values_ref, *outs):
    hits = slot_hits(info_ref, first, rows, base)
    chosen = one_hot(hits)
    gates = slot_gates(hits, info_ref, 2 * TOPK + first)
    width = values_ref.shape[1]
    part = piece(width, 512)
    for start in range(0, width, part):
        columns = slice(start, start + part)
        packed = jnp.dot(chosen, values_ref[:, columns], preferred_element_type=jnp.float32)
        store_slabs(packed * gates, outs, columns)


def call_pack(kernel, slabs, slots, first, base, arrays):
    width = arrays[1].shape[1]
    rows = slabs * slots
    outs = pl.pallas_call(
        functools.partial(kernel, rows, first, base),
        in_specs=[whole(a.shape) for a in arrays],
        out_specs=[whole(s.shape) for s in slab_shapes(slabs, slots, width)],
        out_shape=slab_shapes(slabs, slots, width),
        grid=(1,),
        compiler_params=params(),
        cost_estimate=pl.CostEstimate(
            flops=2 * rows * arrays[1].shape[0] * width,
            bytes_accessed=2 * rows * width + 2 * arrays[1].size,
            transcendentals=0,
        ),
    )(*arrays)
    return to_slabs(outs, slabs, slots)


def resident(value):
    return pltpu.with_memory_space_constraint(value, pltpu.VMEM)


def pre_kernel(part, *refs):
    *slabs, gate_ref, up_ref, pre_gate_ref, pre_up_ref, rows_ref = refs
    gather_slabs(slabs, rows_ref)
    for start in range(0, gate_ref.shape[1], part):
        columns = slice(start, start + part)
        rows = rows_ref[...]
        pre_gate_ref[:, columns] = jnp.dot(rows, gate_ref[:, columns], preferred_element_type=jnp.float32)
        pre_up_ref[:, columns] = jnp.dot(rows, up_ref[:, columns], preferred_element_type=jnp.float32)


def pre_activations(slabs, gate_matrix, up_matrix):
    slabs = from_slabs(slabs)
    count, width = sum(s.shape[0] for s in slabs), slabs[0].shape[1]
    hidden = gate_matrix.shape[1]
    return pl.pallas_call(
        functools.partial(pre_kernel, piece(hidden, 256)),
        in_specs=[VMEM_WHOLE] * (len(slabs) + 2),
        out_specs=[VMEM_WHOLE] * 2,
        out_shape=[jax.ShapeDtypeStruct((count, hidden), jnp.float32)] * 2,
        scratch_shapes=[pltpu.VMEM((count, width), jnp.bfloat16)],
        compiler_params=params(16),
        cost_estimate=pl.CostEstimate(
            flops=4 * count * width * hidden,
            bytes_accessed=4 * width * hidden + 2 * count * width + 8 * count * hidden,
            transcendentals=0,
        ),
        name="pre_activations",
    )(*slabs, resident(gate_matrix), resident(up_matrix))


def backward_kernel(part, column, count_in, *refs):
    slabs, refs = refs[:count_in], refs[count_in:]
    pre_gate_ref, pre_up_ref, down_ref, gate_ref, up_ref, *outs = refs
    *outs, rows_ref, gate_grad, up_grad = outs
    gather_slabs(slabs, rows_ref)
    for start in range(0, gate_ref.shape[1], part):
        columns = slice(start, start + part)
        hidden_grad = contract_last(rows_ref[...], down_ref[columns, :])
        pre_gate = pre_gate_ref[:, columns]
        sigmoid = 1.0 / (1.0 + jnp.exp(-pre_gate))
        both = hidden_grad * sigmoid
        gate_grad[:, columns] = (
            both * pre_up_ref[:, columns] * (1.0 + pre_gate * (1.0 - sigmoid))
        ).astype(jnp.bfloat16)
        up_grad[:, columns] = (both * pre_gate).astype(jnp.bfloat16)
    for start in range(0, gate_ref.shape[0], column):
        chosen = slice(start, start + column)
        total = contract_last(gate_grad[...], gate_ref[chosen, :]) + contract_last(
            up_grad[...], up_ref[chosen, :]
        )
        store_slabs(total, outs, chosen)


def expert_backward(slabs, slots, pre_gate, pre_up, gate_matrix, up_matrix, down_matrix):
    number = len(slabs)
    slabs = from_slabs(slabs)
    count, width = sum(s.shape[0] for s in slabs), slabs[0].shape[1]
    hidden = gate_matrix.shape[1]
    shapes = slab_shapes(number, slots, width)
    outs = pl.pallas_call(
        functools.partial(backward_kernel, piece(hidden, 256), piece(width, 256), len(slabs)),
        in_specs=[VMEM_WHOLE] * (len(slabs) + 5),
        out_specs=[VMEM_WHOLE] * len(shapes),
        out_shape=shapes,
        scratch_shapes=[pltpu.VMEM((count, width), jnp.bfloat16)]
        + [pltpu.VMEM((count, hidden), jnp.bfloat16)] * 2,
        compiler_params=params(16),
        cost_estimate=pl.CostEstimate(
            flops=6 * count * width * hidden,
            bytes_accessed=6 * width * hidden + 4 * count * width + 8 * count * hidden,
            transcendentals=count * hidden,
        ),
        name="expert_backward",
    )(*slabs, pre_gate, pre_up, resident(down_matrix), resident(gate_matrix), resident(up_matrix))
    return to_slabs(outs, number, slots)


def combined(slabs, info_ref, first, x_ref, incoming_of, gain_ref, rows_ref, weighted_ref, put):
    gather_slabs(slabs, rows_ref)
    rows, width = rows_ref.shape
    chosen = one_hot(slot_hits(info_ref, first, rows, 0))
    inverse = inverse_of(x_ref)
    part = piece(width, 512)
    project = None
    for start in range(0, width, part):
        columns = slice(start, start + part)
        normed_grad = lax.dot_general(
            chosen, rows_ref[:, columns], (((0,), (0,)), ((), ())), preferred_element_type=jnp.float32
        )
        weighted = gain_ref[:, columns] * normed_grad
        weighted_ref[:, columns] = weighted
        term = jnp.sum(x_ref[:, columns].astype(jnp.float32) * weighted, axis=1, keepdims=True)
        project = term if project is None else project + term
    factor = inverse * inverse * inverse * (project / width)
    for start in range(0, width, part):
        columns = slice(start, start + part)
        put(
            columns,
            (
                incoming_of(columns).astype(jnp.float32)
                + inverse * weighted_ref[:, columns]
                - x_ref[:, columns].astype(jnp.float32) * factor
            ).astype(jnp.bfloat16),
        )


def relay_kernel(count_in, *refs):
    slabs, refs = refs[:count_in], refs[count_in:]
    flag_ref, info_ref, next_ref, x_ref, incoming_ref, fresh_ref, gain_ref, result_ref, *outs = refs
    *outs, rows_ref, weighted_ref = outs
    rows = rows_ref.shape[0]
    hits = slot_hits(next_ref, TOPK, rows, 0)
    chosen = one_hot(hits)
    gates = slot_gates(hits, next_ref, 3 * TOPK)
    takes_fresh = flag_ref[0] == 0

    def put(columns, value):
        result_ref[:, columns] = value
        passed = jnp.where(takes_fresh, fresh_ref[:, columns], value)
        store_slabs(jnp.dot(chosen, passed, preferred_element_type=jnp.float32) * gates, outs, columns)

    combined(slabs, info_ref, 0, x_ref, lambda c: incoming_ref[:, c], gain_ref, rows_ref, weighted_ref, put)


def final_kernel(count_in, *refs):
    slabs, refs = refs[:count_in], refs[count_in:]
    flag_ref, info_ref, x_ref, arrived_ref, fresh_ref, gain_ref, result_ref, out_ref = refs[:8]
    rows_ref, weighted_ref = refs[8:]
    out_ref[0] = result_ref[...]
    takes_fresh = flag_ref[1] == 0

    def put(columns, value):
        out_ref[1, :, columns] = value

    def incoming_of(columns):
        return jnp.where(takes_fresh, fresh_ref[:, columns], arrived_ref[:, columns])

    combined(slabs, info_ref, TOPK, x_ref, incoming_of, gain_ref, rows_ref, weighted_ref, put)


def call_combine(kernel, slabs, arrays, shapes):
    slabs = from_slabs(slabs)
    count, width = sum(s.shape[0] for s in slabs), slabs[0].shape[1]
    tokens = arrays[-1].shape[0]
    specs = [whole(s.shape) for s in slabs] + [pl.BlockSpec(memory_space=pltpu.SMEM)]
    return pl.pallas_call(
        functools.partial(kernel, len(slabs)),
        in_specs=specs + [whole(a.shape) for a in arrays[1:]],
        out_specs=[whole(s.shape) for s in shapes],
        out_shape=shapes,
        grid=(1,),
        scratch_shapes=[
            pltpu.VMEM((count, width), jnp.bfloat16),
            pltpu.VMEM((shapes[0].shape[-2], width), jnp.float32),
        ],
        compiler_params=params(),
        cost_estimate=pl.CostEstimate(
            flops=4 * count * tokens * width, bytes_accessed=4 * count * width, transcendentals=0
        ),
    )(*slabs, *arrays)


def local(layer_input, entering, fresh, routes, gate_weights, norm_gain, w_gate, w_up, w_down):
    experts = lax.axis_size("expert")
    sections = lax.axis_size("section")
    tokens, width = layer_input.shape[2], layer_input.shape[3]
    slots = max(2, min(tokens, 3 * tokens * TOPK // (2 * experts)))
    half = experts // 2
    here = lax.axis_index("expert")
    section_here = lax.axis_index("section")
    gate_matrix, up_matrix, down_matrix = w_gate[0, 0], w_up[0, 0], w_down[0, 0]
    layer_rows = [layer_input[t, 0] for t in range(TICKS)]
    token_rows = jax.ShapeDtypeStruct((tokens, width), jnp.bfloat16)

    def across(value, k):
        return lax.ppermute(value, "expert", [(i, i ^ k) for i in range(experts)])

    def deal(slabs):
        return [slabs[0]] + [across(slabs[k], k) for k in range(1, len(slabs))]

    def previous(value, k):
        pairs = [
            (s * experts + i, (s - 1) % sections * experts + (i ^ k))
            for s in range(sections)
            for i in range(experts)
        ]
        return lax.ppermute(value, ("section", "expert"), pairs)

    grad_mirror = across(entering[0], half)

    chosen = routes[:, 0].transpose(0, 2, 1)
    expert_ids = jnp.arange(experts, dtype=jnp.int32)
    onehot = chosen[:, :, None, :] == expert_ids[None, None, :, None]
    named = jnp.sum(onehot.astype(jnp.float32), axis=1).astype(jnp.bfloat16)
    order = jnp.arange(tokens, dtype=jnp.int32)
    before = (order[:, None] < order[None, :]).astype(jnp.bfloat16)
    counted = lax.dot_general(
        named, before, (((2,), (0,)), ((), ())), preferred_element_type=jnp.float32
    )
    rank = jnp.sum(jnp.where(onehot, counted[:, None], 0.0), axis=2)
    place = (chosen ^ here).astype(jnp.float32) * slots + rank
    gates = gate_weights[:, 0].transpose(0, 2, 1).astype(jnp.float32)
    info = jnp.concatenate([place, gates], axis=0).reshape(2 * TICKS * TOPK, tokens)
    info_mirror = across(info, half)
    info_next = lax.ppermute(info, "section", [(s, (s + 1) % sections) for s in range(sections)])
    x0_mirror = across(layer_rows[0], half)

    def normed(t, values, given, base):
        return call_pack(pack_normed_kernel, half, slots, TOPK * t, base * slots, [given, values, norm_gain])

    def scaled(values, given, base):
        return call_pack(pack_scaled_kernel, half, slots, 0, base * slots, [given, values])

    scaled0 = deal(scaled(entering[0], info, 0))
    rows0 = deal(normed(0, layer_rows[0], info, 0))
    scaled0 += deal(scaled(grad_mirror, info_mirror, half))
    rows0 += deal(normed(0, x0_mirror, info_mirror, half))
    x1_mirror = across(layer_rows[1], half)

    pre_gate0, pre_up0 = pre_activations(rows0, gate_matrix, up_matrix)
    computed0 = expert_backward(scaled0, slots, pre_gate0, pre_up0, gate_matrix, up_matrix, down_matrix)
    returned0 = deal(computed0)
    rows1 = deal(normed(1, layer_rows[1], info, 0))
    rows1 += deal(normed(1, x1_mirror, info_mirror, half))

    flags = jnp.stack([section_here, sections - 1 - section_here]).astype(jnp.int32)
    relayed = call_combine(
        relay_kernel,
        returned0,
        [flags, info, info_next, layer_rows[0], entering[0], fresh[0], norm_gain],
        [token_rows] + slab_shapes(experts, slots, width),
    )
    result0 = relayed[0]
    outgoing = to_slabs(relayed[1:], experts, slots)
    scaled1 = [previous(outgoing[k], k) for k in range(experts)]
    arrived = previous(result0, 0)
    pre_gate1, pre_up1 = pre_activations(rows1, gate_matrix, up_matrix)
    computed1 = expert_backward(scaled1, slots, pre_gate1, pre_up1, gate_matrix, up_matrix, down_matrix)
    returned1 = deal(computed1)
    (out,) = call_combine(
        final_kernel,
        returned1,
        [flags, info, layer_rows[1], arrived, fresh[0], norm_gain, result0],
        [jax.ShapeDtypeStruct((TICKS, tokens, width), jnp.bfloat16)],
    )
    return out[:, None]


def solution(mesh):
    in_specs = (
        P(None, "section", "expert", None),
        P("section", "expert", None),
        P(None, "expert", None),
        P(None, "section", "expert", None),
        P(None, "section", "expert", None),
        P("section", None),
        P("section", "expert", None, None),
        P("section", "expert", None, None),
        P("section", "expert", None, None),
    )
    out_specs = P(None, "section", "expert", None)

    return jax.shard_map(local, mesh=mesh, in_specs=in_specs, out_specs=out_specs, check_vma=False)
```

time: 369 us -> 238 us (0.64)
  the two profiles are of different devices: /device:TPU:0 before, /device:TPU:12 now
where the time goes in v3:
time: 238 us; the launch traced here: 237 us
  waiting for transfers between devices  146 us (61%)
  starting transfers between devices  51.2 us (22%)
  Pallas kernels  26.1 us (11%)
  local copies, waits for them, and re-layouts  13.8 us (6%)
    ppermute x36, waiting for transfers between devices, across(): return lax.ppermute(value, 'expert', [(i, i ^ k) for i in range(experts)])  114 us
    ppermute x36, starting transfers between devices, across(): return lax.ppermute(value, 'expert', [(i, i ^ k) for i in range(experts)])  46.3 us
    ppermute x9, waiting for transfers between devices, previous(): return lax.ppermute(value, ('section', 'expert'), pairs)  29 us
    unnamed x42, local copies, waits for them, and re-layouts  12.4 us
    pallas_call x2, Pallas kernels, expert_backward(): pl.pallas_call(functools.partial(backward_kernel, piece(hidden, 256), pie...  10.5 us
    pallas_call x2, Pallas kernels, pre_activations(): pl.pallas_call(functools.partial(pre_kernel, piece(hidden, 256)), in_spec...  6.54 us
    ppermute x9, starting transfers between devices, previous(): return lax.ppermute(value, ('section', 'expert'), pairs)  4.95 us
  transfers between devices with their start and end apart: 46, of which 24 were waited for; matrix products, arithmetic and copies ran while one was open for 0% of the time, Pallas kernels for 10%

profile of v3, /device:TPU:12, one launch (start us, length us, event | category | flops | bytes accessed | tf_op | source)
XLA Modules:
  0.0 237.2 jit_solution(3714412128772731542)
XLA Ops:
  1.4 2.7 %collective-permute-start.11 = (bf16[128,2048]{1,0:T(8,128)(2,1)S(1)}, bf16[128,2048]{1,0:T(8,128)(2,1)S(1)}, u32[]{:S(2)}, u32[]{:S(2)}) collective-permute-start(bf16[128,2048]{1,0:T(8,128)(2,1)S(1)} %get-tuple-element.112.x_ref.refs_11_), channel_id=1, source_target_pairs={{0,4},{1,5},{2,6},{3,7},{4,0},{5,1},{6,2},{7,3},{8,12},{9,13},{10,... | collective-permute-start | bytes 1572872 | tf_op jit(solution)/shard_map/ppermute | solution.py:318
  10.1 38.9 %collective-permute-done.3.info_ref = f32[8,128]{1,0:T(8,128)S(1)} collective-permute-done((f32[8,128]{1,0:T(8,128)S(1)}, f32[8,128]{1,0:T(8,128)S(1)}, u32[]{:S(2)}, u32[]{:S(2)}) %collective-permute-start.3) | collective-permute-done | bytes 4128 | tf_op jit(solution)/shard_map/ppermute | solution.py:318
  58.8 5.3 %collective-permute-done.12.refs_5_ = bf16[48,2048]{1,0:T(8,128)(2,1)S(1)} collective-permute-done((bf16[48,2048]{1,0:T(8,128)(2,1)S(1)}, bf16[48,2048]{1,0:T(8,128)(2,1)S(1)}, u32[]{:S(2)}, u32[]{:S(2)}) %collective-permute-start.12) | collective-permute-done | bytes 196640 | tf_op jit(solution)/shard_map/ppermute | solution.py:318
  64.0 3.0 %collective-permute-start.6 = (bf16[48,2048]{1,0:T(8,128)(2,1)S(1)}, bf16[48,2048]{1,0:T(8,128)(2,1)S(1)}, u32[]{:S(2)}, u32[]{:S(2)}) collective-permute-start(bf16[48,2048]{1,0:T(8,128)(2,1)S(1)} %get-tuple-element.64), channel_id=1, source_target_pairs={{0,2},{1,3},{2,0},{3,1},{4,6},{5,7},{6,4},{7,5},{8,10},{9,11},{10,... | collective-permute-start | bytes 589832 | tf_op jit(solution)/shard_map/ppermute | solution.py:318
  77.4 4.9 %collective-permute-done.6.refs_6_ = bf16[48,2048]{1,0:T(8,128)(2,1)S(1)} collective-permute-done((bf16[48,2048]{1,0:T(8,128)(2,1)S(1)}, bf16[48,2048]{1,0:T(8,128)(2,1)S(1)}, u32[]{:S(2)}, u32[]{:S(2)}) %collective-permute-start.6) | collective-permute-done | bytes 196640 | tf_op jit(solution)/shard_map/ppermute | solution.py:318
  82.3 3.8 %collective-permute-done.7.refs_7_ = bf16[48,2048]{1,0:T(8,128)(2,1)S(1)} collective-permute-done((bf16[48,2048]{1,0:T(8,128)(2,1)S(1)}, bf16[48,2048]{1,0:T(8,128)(2,1)S(1)}, u32[]{:S(2)}, u32[]{:S(2)}) %collective-permute-start.7) | collective-permute-done | bytes 196640 | tf_op jit(solution)/shard_map/ppermute | solution.py:318
  87.9 5.6 %expert_backward.2 = (bf16[48,2048]{1,0:T(8,128)(2,1)S(1)}, bf16[48,2048]{1,0:T(8,128)(2,1)S(1)}, bf16[48,2048]{1,0:T(8,128)(2,1)S(1)}, bf16[48,2048]{1,0:T(8,12...) custom-call(bf16[48,2048]{1,0:T(8,128)(2,1)S(1)} %get-tuple-element., ...), custom_call_target="tpu_custom_call" | custom-call | flops 3623878656 | bytes 14942208 | tf_op jit(solution)/shard_map/expert_backward/pallas_call | solution.py:202
  94.5 3.0 %collective-permute-start.16 = (bf16[48,2048]{1,0:T(8,128)(2,1)S(1)}, bf16[48,2048]{1,0:T(8,128)(2,1)S(1)}, u32[]{:S(2)}, u32[]{:S(2)}) collective-permute-start(bf16[48,2048]{1,0:T(8,128)(2,1)S(1)} %get-tuple-element.78), channel_id=1, source_target_pairs={{0,2},{1,3},{2,0},{3,1},{4,6},{5,7},{6,4},{7,5},{8,10},{9,11},{10,... | collective-permute-start | bytes 589832 | tf_op jit(solution)/shard_map/ppermute | solution.py:318
  97.9 2.7 %collective-permute-done.22.refs_10_ = f32[8,128]{1,0:T(8,128)S(1)} collective-permute-done((f32[8,128]{1,0:T(8,128)S(1)}, f32[8,128]{1,0:T(8,128)S(1)}, u32[]{:S(2)}, u32[]{:S(2)}) %collective-permute-start.22) | collective-permute-done | bytes 4128 | tf_op jit(solution)/shard_map/ppermute | solution.py:347
  111.2 12.7 %collective-permute-done.18.refs_4_ = bf16[48,2048]{1,0:T(8,128)(2,1)S(1)} collective-permute-done((bf16[48,2048]{1,0:T(8,128)(2,1)S(1)}, bf16[48,2048]{1,0:T(8,128)(2,1)S(1)}, u32[]{:S(2)}, u32[]{:S(2)}) %collective-permute-start.18) | collective-permute-done | bytes 196640 | tf_op jit(solution)/shard_map/ppermute | solution.py:318
  128.2 3.4 %collective-permute-start.33 = (bf16[48,2048]{1,0:T(8,128)(2,1)}, bf16[48,2048]{1,0:T(8,128)(2,1)}, u32[]{:S(2)}, u32[]{:S(2)}) collective-permute-start(bf16[48,2048]{1,0:T(8,128)(2,1)} %get-tuple-element.95), channel_id=1, source_target_pairs={{0,3},{1,2},{2,1},{3,0},{4,7},{5,6},{6,5},{7,4},{8,11},{9,10},{10,... | collective-permute-start | bytes 589832 | tf_op jit(solution)/shard_map/ppermute | solution.py:318
  134.8 5.5 %collective-permute-done.21.refs_7_ = bf16[48,2048]{1,0:T(8,128)(2,1)} collective-permute-done((bf16[48,2048]{1,0:T(8,128)(2,1)}, bf16[48,2048]{1,0:T(8,128)(2,1)}, u32[]{:S(2)}, u32[]{:S(2)}) %collective-permute-start.21) | collective-permute-done | bytes 196640 | tf_op jit(solution)/shard_map/ppermute | solution.py:318
  143.6 3.0 %collective-permute-start.37 = (bf16[48,2048]{1,0:T(8,128)(2,1)}, bf16[48,2048]{1,0:T(8,128)(2,1)S(1)}, u32[]{:S(2)}, u32[]{:S(2)}) collective-permute-start(bf16[48,2048]{1,0:T(8,128)(2,1)} %copy-done.18), channel_id=1, source_target_pairs={{0,3},{1,2},{2,1},{3,0},{4,7},{5,6},{6,5},{7,4},{8,11},{9,10},{10,... | collective-permute-start | bytes 589832 | tf_op jit(solution)/shard_map/ppermute | solution.py:318
  147.6 3.2 %collective-permute-start.26 = (bf16[48,2048]{1,0:T(8,128)(2,1)S(1)}, bf16[48,2048]{1,0:T(8,128)(2,1)S(1)}, u32[]{:S(2)}, u32[]{:S(2)}) collective-permute-start(bf16[48,2048]{1,0:T(8,128)(2,1)S(1)} %get-tuple-element.87), channel_id=1, source_target_pairs={{0,27},{1,26},{2,25},{3,24},{4,31},{5,30},{6,29},{7,28},{8,3},{9,2... | collective-permute-start | bytes 589832 | tf_op jit(solution)/shard_map/ppermute | solution.py:329
  153.4 5.6 %collective-permute-done.24.refs_1_ = bf16[48,2048]{1,0:T(8,128)(2,1)S(1)} collective-permute-done((bf16[48,2048]{1,0:T(8,128)(2,1)S(1)}, bf16[48,2048]{1,0:T(8,128)(2,1)S(1)}, u32[]{:S(2)}, u32[]{:S(2)}) %collective-permute-start.24) | collective-permute-done | bytes 196640 | tf_op jit(solution)/shard_map/ppermute | solution.py:329
  164.6 3.9 %pre_activations.3 = (f32[384,768]{1,0:T(8,128)S(1)}, f32[384,768]{1,0:T(8,128)S(1)}) custom-call(bf16[48,2048]{1,0:T(8,128)(2,1)S(1)} %copy-done.15, bf16[48,2048]{1,0:T(8,128)(2,1)} %collective-permute-done.31.refs_1_, bf16[48,2048]{1,0:T(8,128)(2,1)} %collective-permute-done.32.refs_2_, bf16[48,2048]{1,0:T(8,128)(2,1)} %collective-permute-done.33.refs_3_, ...), custom_call_target="tpu_custom_call" | custom-call | flops 2415919104 | bytes 10223616 | tf_op jit(solution)/shard_map/pre_activations/pallas_call | solution.py:157
  168.9 8.0 %collective-permute-done.28.refs_5_ = bf16[48,2048]{1,0:T(8,128)(2,1)S(1)} collective-permute-done((bf16[48,2048]{1,0:T(8,128)(2,1)S(1)}, bf16[48,2048]{1,0:T(8,128)(2,1)S(1)}, u32[]{:S(2)}, u32[]{:S(2)}) %collective-permute-start.28) | collective-permute-done | bytes 196640 | tf_op jit(solution)/shard_map/ppermute | solution.py:329
  177.0 10.3 %collective-permute-done.29.refs_6_ = bf16[48,2048]{1,0:T(8,128)(2,1)S(1)} collective-permute-done((bf16[48,2048]{1,0:T(8,128)(2,1)S(1)}, bf16[48,2048]{1,0:T(8,128)(2,1)S(1)}, u32[]{:S(2)}, u32[]{:S(2)}) %collective-permute-start.29) | collective-permute-done | bytes 196640 | tf_op jit(solution)/shard_map/ppermute | solution.py:329
  187.3 3.2 %collective-permute-done.30.refs_7_ = bf16[48,2048]{1,0:T(8,128)(2,1)S(1)} collective-permute-done((bf16[48,2048]{1,0:T(8,128)(2,1)S(1)}, bf16[48,2048]{1,0:T(8,128)(2,1)S(1)}, u32[]{:S(2)}, u32[]{:S(2)}) %collective-permute-start.30) | collective-permute-done | bytes 196640 | tf_op jit(solution)/shard_map/ppermute | solution.py:329
  190.5 4.9 %expert_backward.3 = (bf16[48,2048]{1,0:T(8,128)(2,1)S(1)}, bf16[48,2048]{1,0:T(8,128)(2,1)S(1)}, bf16[48,2048]{1,0:T(8,128)(2,1)S(1)}, bf16[48,2048]{1,0:T(8,12...) custom-call(bf16[48,2048]{1,0:T(8,128)(2,1)S(1)} %collective-permute, ...), custom_call_target="tpu_custom_call" | custom-call | flops 3623878656 | bytes 14942208 | tf_op jit(solution)/shard_map/expert_backward/pallas_call | solution.py:202
  202.9 7.1 %collective-permute-done.39.refs_2_ = bf16[48,2048]{1,0:T(8,128)(2,1)S(1)} collective-permute-done((bf16[48,2048]{1,0:T(8,128)(2,1)S(1)}, bf16[48,2048]{1,0:T(8,128)(2,1)S(1)}, u32[]{:S(2)}, u32[]{:S(2)}) %collective-permute-start.39) | collective-permute-done | bytes 196640 | tf_op jit(solution)/shard_map/ppermute | solution.py:318
  214.2 12.2 %collective-permute-done.42.refs_5_ = bf16[48,2048]{1,0:T(8,128)(2,1)S(1)} collective-permute-done((bf16[48,2048]{1,0:T(8,128)(2,1)S(1)}, bf16[48,2048]{1,0:T(8,128)(2,1)S(1)}, u32[]{:S(2)}, u32[]{:S(2)}) %collective-permute-start.42) | collective-permute-done | bytes 196640 | tf_op jit(solution)/shard_map/ppermute | solution.py:318
  226.3 4.8 %collective-permute-done.43.refs_6_ = bf16[48,2048]{1,0:T(8,128)(2,1)S(1)} collective-permute-done((bf16[48,2048]{1,0:T(8,128)(2,1)S(1)}, bf16[48,2048]{1,0:T(8,128)(2,1)S(1)}, u32[]{:S(2)}, u32[]{:S(2)}) %collective-permute-start.43) | collective-permute-done | bytes 196640 | tf_op jit(solution)/shard_map/ppermute | solution.py:318
  231.1 3.8 %collective-permute-done.44.refs_7_ = bf16[48,2048]{1,0:T(8,128)(2,1)S(1)} collective-permute-done((bf16[48,2048]{1,0:T(8,128)(2,1)S(1)}, bf16[48,2048]{1,0:T(8,128)(2,1)S(1)}, u32[]{:S(2)}, u32[]{:S(2)}) %collective-permute-start.44) | collective-permute-done | bytes 196640 | tf_op jit(solution)/shard_map/ppermute | solution.py:318
  (130 shorter events, 75.4 us)
Async XLA Ops:
  1.4 49.0 %collective-permute-start.11 = (bf16[128,2048]{1,0:T(8,128)(2,1)S(1)}, bf16[128,2048]{1,0:T(8,128)(2,1)S(1)}, u32[]{:S(2)}, u32[]{:S(2)}) collective-permute-start(bf16[128,2048]{1,0:T(8,128)(2,1)S(1)} %get-tuple-element.112.x_ref.refs_11_), channel_id=1, source_target_pairs={{0,4},{1,5},{2,6},{3,7},{4,0},{5,1},{6,2},{7,3},{8,12},{9,13},{10,... | collective-permute-start | bytes 1572872 | tf_op jit(solution)/shard_map/ppermute | solution.py:318
  4.0 49.7 %collective-permute-start.4 = (bf16[128,2048]{1,0:T(8,128)(2,1)S(1)}, bf16[128,2048]{1,0:T(8,128)(2,1)S(1)}, u32[]{:S(2)}, u32[]{:S(2)}) collective-permute-start(bf16[128,2048]{1,0:T(8,128)(2,1)S(1)} %bitcast.30), channel_id=1, source_target_pairs={{0,4},{1,5},{2,6},{3,7},{4,0},{5,1},{6,2},{7,3},{8,12},{9,13},{10,... | collective-permute-start | bytes 1572872 | tf_op jit(solution)/shard_map/ppermute | solution.py:318
  5.2 46.2 %collective-permute-start.10 = (bf16[48,2048]{1,0:T(8,128)(2,1)S(1)}, bf16[48,2048]{1,0:T(8,128)(2,1)S(1)}, u32[]{:S(2)}, u32[]{:S(2)}) collective-permute-start(bf16[48,2048]{1,0:T(8,128)(2,1)S(1)} %get-tuple-element.69), channel_id=1, source_target_pairs={{0,3},{1,2},{2,1},{3,0},{4,7},{5,6},{6,5},{7,4},{8,11},{9,10},{10,... | collective-permute-start | bytes 589832 | tf_op jit(solution)/shard_map/ppermute | solution.py:318
  5.4 47.6 %collective-permute-start.8 = (bf16[48,2048]{1,0:T(8,128)(2,1)S(1)}, bf16[48,2048]{1,0:T(8,128)(2,1)S(1)}, u32[]{:S(2)}, u32[]{:S(2)}) collective-permute-start(bf16[48,2048]{1,0:T(8,128)(2,1)S(1)} %get-tuple-element.67), channel_id=1, source_target_pairs={{0,1},{1,0},{2,3},{3,2},{4,5},{5,4},{6,7},{7,6},{8,9},{9,8},{10,11... | collective-permute-start | bytes 589832 | tf_op jit(solution)/shard_map/ppermute | solution.py:318
  7.1 41.9 %collective-permute-start.3 = (f32[8,128]{1,0:T(8,128)S(1)}, f32[8,128]{1,0:T(8,128)S(1)}, u32[]{:S(2)}, u32[]{:S(2)}) collective-permute-start(f32[8,128]{1,0:T(8,128)S(1)} %bitcast.36), channel_id=1, source_target_pairs={{0,4},{1,5},{2,6},{3,7},{4,0},{5,1},{6,2},{7,3},{8,12},{9,13},{10,... | collective-permute-start | bytes 12296 | tf_op jit(solution)/shard_map/ppermute | solution.py:318
  58.0 19.4 %collective-permute-start.2 = (bf16[48,2048]{1,0:T(8,128)(2,1)S(1)}, bf16[48,2048]{1,0:T(8,128)(2,1)S(1)}, u32[]{:S(2)}, u32[]{:S(2)}) collective-permute-start(bf16[48,2048]{1,0:T(8,128)(2,1)S(1)} %get-tuple-element.61), channel_id=1, source_target_pairs={{0,3},{1,2},{2,1},{3,0},{4,7},{5,6},{6,5},{7,4},{8,11},{9,10},{10,... | collective-permute-start | bytes 589832 | tf_op jit(solution)/shard_map/ppermute | solution.py:318
  64.0 18.2 %collective-permute-start.6 = (bf16[48,2048]{1,0:T(8,128)(2,1)S(1)}, bf16[48,2048]{1,0:T(8,128)(2,1)S(1)}, u32[]{:S(2)}, u32[]{:S(2)}) collective-permute-start(bf16[48,2048]{1,0:T(8,128)(2,1)S(1)} %get-tuple-element.64), channel_id=1, source_target_pairs={{0,2},{1,3},{2,0},{3,1},{4,6},{5,7},{6,4},{7,5},{8,10},{9,11},{10,... | collective-permute-start | bytes 589832 | tf_op jit(solution)/shard_map/ppermute | solution.py:318
  67.1 19.0 %collective-permute-start.7 = (bf16[48,2048]{1,0:T(8,128)(2,1)S(1)}, bf16[48,2048]{1,0:T(8,128)(2,1)S(1)}, u32[]{:S(2)}, u32[]{:S(2)}) collective-permute-start(bf16[48,2048]{1,0:T(8,128)(2,1)S(1)} %get-tuple-element.65), channel_id=1, source_target_pairs={{0,3},{1,2},{2,1},{3,0},{4,7},{5,6},{6,5},{7,4},{8,11},{9,10},{10,... | collective-permute-start | bytes 589832 | tf_op jit(solution)/shard_map/ppermute | solution.py:318
  75.0 26.8 %collective-permute-start.34 = (bf16[128,2048]{1,0:T(8,128)(2,1)S(1)}, bf16[128,2048]{1,0:T(8,128)(2,1)S(1)}, u32[]{:S(2)}, u32[]{:S(2)}) collective-permute-start(bf16[128,2048]{1,0:T(8,128)(2,1)S(1)} %get-tuple-element.111.x_ref.refs_10_), channel_id=1, source_target_pairs={{0,4},{1,5},{2,6},{3,7},{4,0},{5,1},{6,2},{7,3},{8,12},{9,13},{10,... | collective-permute-start | bytes 1572872 | tf_op jit(solution)/shard_map/ppermute | solution.py:318
  100.5 23.5 %collective-permute-start.18 = (bf16[48,2048]{1,0:T(8,128)(2,1)S(1)}, bf16[48,2048]{1,0:T(8,128)(2,1)S(1)}, u32[]{:S(2)}, u32[]{:S(2)}) collective-permute-start(bf16[48,2048]{1,0:T(8,128)(2,1)S(1)} %get-tuple-element.80), channel_id=1, source_target_pairs={{0,4},{1,5},{2,6},{3,7},{4,0},{5,1},{6,2},{7,3},{8,12},{9,13},{10,... | collective-permute-start | bytes 589832 | tf_op jit(solution)/shard_map/ppermute | solution.py:318
  101.8 26.4 %collective-permute-start.19 = (bf16[48,2048]{1,0:T(8,128)(2,1)S(1)}, bf16[48,2048]{1,0:T(8,128)(2,1)S(1)}, u32[]{:S(2)}, u32[]{:S(2)}) collective-permute-start(bf16[48,2048]{1,0:T(8,128)(2,1)S(1)} %get-tuple-element.81), channel_id=1, source_target_pairs={{0,5},{1,4},{2,7},{3,6},{4,1},{5,0},{6,3},{7,2},{8,13},{9,12},{10,... | collective-permute-start | bytes 589832 | tf_op jit(solution)/shard_map/ppermute | solution.py:318
  103.8 29.7 %collective-permute-start.20 = (bf16[48,2048]{1,0:T(8,128)(2,1)S(1)}, bf16[48,2048]{1,0:T(8,128)(2,1)S(1)}, u32[]{:S(2)}, u32[]{:S(2)}) collective-permute-start(bf16[48,2048]{1,0:T(8,128)(2,1)S(1)} %get-tuple-element.82), channel_id=1, source_target_pairs={{0,6},{1,7},{2,4},{3,5},{4,2},{5,3},{6,0},{7,1},{8,14},{9,15},{10,... | collective-permute-start | bytes 589832 | tf_op jit(solution)/shard_map/ppermute | solution.py:318
  106.7 33.6 %collective-permute-start.21 = (bf16[48,2048]{1,0:T(8,128)(2,1)}, bf16[48,2048]{1,0:T(8,128)(2,1)}, u32[]{:S(2)}, u32[]{:S(2)}) collective-permute-start(bf16[48,2048]{1,0:T(8,128)(2,1)} %get-tuple-element.83), channel_id=1, source_target_pairs={{0,7},{1,6},{2,5},{3,4},{4,3},{5,2},{6,1},{7,0},{8,15},{9,14},{10,... | collective-permute-start | bytes 589832 | tf_op jit(solution)/shard_map/ppermute | solution.py:318
  110.3 33.3 %collective-permute-start.31 = (bf16[48,2048]{1,0:T(8,128)(2,1)}, bf16[48,2048]{1,0:T(8,128)(2,1)}, u32[]{:S(2)}, u32[]{:S(2)}) collective-permute-start(bf16[48,2048]{1,0:T(8,128)(2,1)} %get-tuple-element.93), channel_id=1, source_target_pairs={{0,1},{1,0},{2,3},{3,2},{4,5},{5,4},{6,7},{7,6},{8,9},{9,8},{10,11... | collective-permute-start | bytes 589832 | tf_op jit(solution)/shard_map/ppermute | solution.py:318
  124.0 22.6 %collective-permute-start.32 = (bf16[48,2048]{1,0:T(8,128)(2,1)}, bf16[48,2048]{1,0:T(8,128)(2,1)}, u32[]{:S(2)}, u32[]{:S(2)}) collective-permute-start(bf16[48,2048]{1,0:T(8,128)(2,1)} %get-tuple-element.94), channel_id=1, source_target_pairs={{0,2},{1,3},{2,0},{3,1},{4,6},{5,7},{6,4},{7,5},{8,10},{9,11},{10,... | collective-permute-start | bytes 589832 | tf_op jit(solution)/shard_map/ppermute | solution.py:318
  128.2 18.4 %collective-permute-start.33 = (bf16[48,2048]{1,0:T(8,128)(2,1)}, bf16[48,2048]{1,0:T(8,128)(2,1)}, u32[]{:S(2)}, u32[]{:S(2)}) collective-permute-start(bf16[48,2048]{1,0:T(8,128)(2,1)} %get-tuple-element.95), channel_id=1, source_target_pairs={{0,3},{1,2},{2,1},{3,0},{4,7},{5,6},{6,5},{7,4},{8,11},{9,10},{10,... | collective-permute-start | bytes 589832 | tf_op jit(solution)/shard_map/ppermute | solution.py:318
  147.6 20.9 %collective-permute-start.26 = (bf16[48,2048]{1,0:T(8,128)(2,1)S(1)}, bf16[48,2048]{1,0:T(8,128)(2,1)S(1)}, u32[]{:S(2)}, u32[]{:S(2)}) collective-permute-start(bf16[48,2048]{1,0:T(8,128)(2,1)S(1)} %get-tuple-element.87), channel_id=1, source_target_pairs={{0,27},{1,26},{2,25},{3,24},{4,31},{5,30},{6,29},{7,28},{8,3},{9,2... | collective-permute-start | bytes 589832 | tf_op jit(solution)/shard_map/ppermute | solution.py:329
  153.1 23.9 %collective-permute-start.28 = (bf16[48,2048]{1,0:T(8,128)(2,1)S(1)}, bf16[48,2048]{1,0:T(8,128)(2,1)S(1)}, u32[]{:S(2)}, u32[]{:S(2)}) collective-permute-start(bf16[48,2048]{1,0:T(8,128)(2,1)S(1)} %get-tuple-element.89), channel_id=1, source_target_pairs={{0,29},{1,28},{2,31},{3,30},{4,25},{5,24},{6,27},{7,26},{8,5},{9,4... | collective-permute-start | bytes 589832 | tf_op jit(solution)/shard_map/ppermute | solution.py:329
  159.0 28.3 %collective-permute-start.29 = (bf16[48,2048]{1,0:T(8,128)(2,1)S(1)}, bf16[48,2048]{1,0:T(8,128)(2,1)S(1)}, u32[]{:S(2)}, u32[]{:S(2)}) collective-permute-start(bf16[48,2048]{1,0:T(8,128)(2,1)S(1)} %get-tuple-element.90), channel_id=1, source_target_pairs={{0,30},{1,31},{2,28},{3,29},{4,26},{5,27},{6,24},{7,25},{8,6},{9,7... | collective-permute-start | bytes 589832 | tf_op jit(solution)/shard_map/ppermute | solution.py:329
  160.8 29.7 %collective-permute-start.30 = (bf16[48,2048]{1,0:T(8,128)(2,1)S(1)}, bf16[48,2048]{1,0:T(8,128)(2,1)S(1)}, u32[]{:S(2)}, u32[]{:S(2)}) collective-permute-start(bf16[48,2048]{1,0:T(8,128)(2,1)S(1)} %get-tuple-element.91), channel_id=1, source_target_pairs={{0,31},{1,30},{2,29},{3,28},{4,27},{5,26},{6,25},{7,24},{8,7},{9,6... | collective-permute-start | bytes 589832 | tf_op jit(solution)/shard_map/ppermute | solution.py:329
  168.5 66.3 %collective-permute-start.45 = (bf16[128,2048]{1,0:T(8,128)(2,1)S(1)}, bf16[128,2048]{1,0:T(8,128)(2,1)S(1)}, u32[]{:S(2)}, u32[]{:S(2)}) collective-permute-start(bf16[128,2048]{1,0:T(8,128)(2,1)S(1)} %get-tuple-element.110.refs_14_), channel_id=1, source_target_pairs={{0,24},{1,25},{2,26},{3,27},{4,28},{5,29},{6,30},{7,31},{8,0},{9,1... | collective-permute-start | bytes 1572872 | tf_op jit(solution)/shard_map/ppermute | solution.py:329
  202.5 23.8 %collective-permute-start.42 = (bf16[48,2048]{1,0:T(8,128)(2,1)S(1)}, bf16[48,2048]{1,0:T(8,128)(2,1)S(1)}, u32[]{:S(2)}, u32[]{:S(2)}) collective-permute-start(bf16[48,2048]{1,0:T(8,128)(2,1)S(1)} %get-tuple-element.107), channel_id=1, source_target_pairs={{0,5},{1,4},{2,7},{3,6},{4,1},{5,0},{6,3},{7,2},{8,13},{9,12},{10,... | collective-permute-start | bytes 589832 | tf_op jit(solution)/shard_map/ppermute | solution.py:318
  210.0 21.1 %collective-permute-start.43 = (bf16[48,2048]{1,0:T(8,128)(2,1)S(1)}, bf16[48,2048]{1,0:T(8,128)(2,1)S(1)}, u32[]{:S(2)}, u32[]{:S(2)}) collective-permute-start(bf16[48,2048]{1,0:T(8,128)(2,1)S(1)} %get-tuple-element.108), channel_id=1, source_target_pairs={{0,6},{1,7},{2,4},{3,5},{4,2},{5,3},{6,0},{7,1},{8,14},{9,15},{10,... | collective-permute-start | bytes 589832 | tf_op jit(solution)/shard_map/ppermute | solution.py:318
  212.2 22.7 %collective-permute-start.44 = (bf16[48,2048]{1,0:T(8,128)(2,1)S(1)}, bf16[48,2048]{1,0:T(8,128)(2,1)S(1)}, u32[]{:S(2)}, u32[]{:S(2)}) collective-permute-start(bf16[48,2048]{1,0:T(8,128)(2,1)S(1)} %get-tuple-element.109), channel_id=1, source_target_pairs={{0,7},{1,6},{2,5},{3,4},{4,3},{5,2},{6,1},{7,0},{8,15},{9,14},{10,... | collective-permute-start | bytes 589832 | tf_op jit(solution)/shard_map/ppermute | solution.py:318
  (43 other events, 453.2 us)

commit v4 on v3

--- a/solution.py
+++ b/solution.py
@@ -170,21 +170,42 @@
     )(*slabs, resident(gate_matrix), resident(up_matrix))
 
 
-def backward_kernel(part, column, count_in, *refs):
-    slabs, refs = refs[:count_in], refs[count_in:]
-    pre_gate_ref, pre_up_ref, down_ref, gate_ref, up_ref, *outs = refs
-    *outs, rows_ref, gate_grad, up_grad = outs
+def hidden_kernel(part, *refs):
+    *slabs, down_ref, hidden_ref, rows_ref = refs
     gather_slabs(slabs, rows_ref)
-    for start in range(0, gate_ref.shape[1], part):
-        columns = slice(start, start + part)
-        hidden_grad = contract_last(rows_ref[...], down_ref[columns, :])
-        pre_gate = pre_gate_ref[:, columns]
-        sigmoid = 1.0 / (1.0 + jnp.exp(-pre_gate))
-        both = hidden_grad * sigmoid
-        gate_grad[:, columns] = (
-            both * pre_up_ref[:, columns] * (1.0 + pre_gate * (1.0 - sigmoid))
-        ).astype(jnp.bfloat16)
-        up_grad[:, columns] = (both * pre_gate).astype(jnp.bfloat16)
+    for start in range(0, down_ref.shape[0], part):
+        columns = slice(start, start + part)
+        hidden_ref[:, columns] = contract_last(rows_ref[...], down_ref[columns, :])
+
+
+def hidden_gradient(slabs, down_matrix):
+    slabs = from_slabs(slabs)
+    count, width = sum(s.shape[0] for s in slabs), slabs[0].shape[1]
+    hidden = down_matrix.shape[0]
+    return pl.pallas_call(
+        functools.partial(hidden_kernel, piece(hidden, 256)),
+        in_specs=[VMEM_WHOLE] * (len(slabs) + 1),
+        out_specs=VMEM_WHOLE,
+        out_shape=jax.ShapeDtypeStruct((count, hidden), jnp.float32),
+        scratch_shapes=[pltpu.VMEM((count, width), jnp.bfloat16)],
+        compiler_params=params(16),
+        cost_estimate=pl.CostEstimate(
+            flops=2 * count * width * hidden,
+            bytes_accessed=2 * width * hidden + 2 * count * width + 4 * count * hidden,
+            transcendentals=0,
+        ),
+        name="hidden_gradient",
+    )(*slabs, resident(down_matrix))
+
+
+def store_grads(pre_gate, pre_up, hidden_grad, gate_grad, up_grad, columns):
+    sigmoid = 1.0 / (1.0 + jnp.exp(-pre_gate))
+    both = hidden_grad * sigmoid
+    gate_grad[:, columns] = (both * pre_up * (1.0 + pre_gate * (1.0 - sigmoid))).astype(jnp.bfloat16)
+    up_grad[:, columns] = (both * pre_gate).astype(jnp.bfloat16)
+
+
+def store_rows(gate_grad, up_grad, gate_ref, up_ref, outs, column):
     for start in range(0, gate_ref.shape[0], column):
         chosen = slice(start, start + column)
         total = contract_last(gate_grad[...], gate_ref[chosen, :]) + contract_last(
@@ -193,18 +214,47 @@
         store_slabs(total, outs, chosen)
 
 
-def expert_backward(slabs, slots, pre_gate, pre_up, gate_matrix, up_matrix, down_matrix):
-    number = len(slabs)
+def gradient_last_kernel(part, column, count_in, *refs):
+    slabs, refs = refs[:count_in], refs[count_in:]
+    pre_gate_ref, pre_up_ref, down_ref, gate_ref, up_ref, *outs = refs
+    *outs, rows_ref, gate_grad, up_grad = outs
+    gather_slabs(slabs, rows_ref)
+    for start in range(0, gate_ref.shape[1], part):
+        columns = slice(start, start + part)
+        hidden_grad = contract_last(rows_ref[...], down_ref[columns, :])
+        store_grads(
+            pre_gate_ref[:, columns], pre_up_ref[:, columns], hidden_grad, gate_grad, up_grad, columns
+        )
+    store_rows(gate_grad, up_grad, gate_ref, up_ref, outs, column)
+
+
+def normed_last_kernel(part, column, count_in, *refs):
+    slabs, refs = refs[:count_in], refs[count_in:]
+    pre_gate_ref, pre_up_ref, hidden_ref, gate_ref, up_ref, *outs = refs
+    *outs, rows_ref, gate_grad, up_grad = outs
+    gather_slabs(slabs, rows_ref)
+    for start in range(0, gate_ref.shape[1], part):
+        columns = slice(start, start + part)
+        far_gate = jnp.dot(rows_ref[...], gate_ref[:, columns], preferred_element_type=jnp.float32)
+        far_up = jnp.dot(rows_ref[...], up_ref[:, columns], preferred_element_type=jnp.float32)
+        pre_gate = jnp.concatenate([pre_gate_ref[:, columns], far_gate], axis=0)
+        pre_up = jnp.concatenate([pre_up_ref[:, columns], far_up], axis=0)
+        store_grads(pre_gate, pre_up, hidden_ref[:, columns], gate_grad, up_grad, columns)
+    store_rows(gate_grad, up_grad, gate_ref, up_ref, outs, column)
+
+
+def call_backward(kernel, slabs, number, slots, given, matrices):
     slabs = from_slabs(slabs)
-    count, width = sum(s.shape[0] for s in slabs), slabs[0].shape[1]
-    hidden = gate_matrix.shape[1]
+    count, width = number * slots, slabs[0].shape[1]
+    gathered = sum(s.shape[0] for s in slabs)
+    hidden = matrices[-1].shape[1]
     shapes = slab_shapes(number, slots, width)
     outs = pl.pallas_call(
-        functools.partial(backward_kernel, piece(hidden, 256), piece(width, 256), len(slabs)),
-        in_specs=[VMEM_WHOLE] * (len(slabs) + 5),
+        functools.partial(kernel, piece(hidden, 256), piece(width, 256), len(slabs)),
+        in_specs=[VMEM_WHOLE] * (len(slabs) + len(given) + len(matrices)),
         out_specs=[VMEM_WHOLE] * len(shapes),
         out_shape=shapes,
-        scratch_shapes=[pltpu.VMEM((count, width), jnp.bfloat16)]
+        scratch_shapes=[pltpu.VMEM((gathered, width), jnp.bfloat16)]
         + [pltpu.VMEM((count, hidden), jnp.bfloat16)] * 2,
         compiler_params=params(16),
         cost_estimate=pl.CostEstimate(
@@ -213,7 +263,7 @@
             transcendentals=count * hidden,
         ),
         name="expert_backward",
-    )(*slabs, pre_gate, pre_up, resident(down_matrix), resident(gate_matrix), resident(up_matrix))
+    )(*slabs, *given, *[resident(m) for m in matrices])
     return to_slabs(outs, number, slots)
 
 
@@ -359,9 +409,16 @@
     rows0 += deal(normed(0, x0_mirror, info_mirror, half))
     x1_mirror = across(layer_rows[1], half)
 
-    pre_gate0, pre_up0 = pre_activations(rows0, gate_matrix, up_matrix)
-    computed0 = expert_backward(scaled0, slots, pre_gate0, pre_up0, gate_matrix, up_matrix, down_matrix)
-    returned0 = deal(computed0)
+    def deal_all(slabs):
+        near = deal(slabs[:half])
+        return near + [across(slabs[k], k) for k in range(half, experts)]
+
+    given = [*pre_activations(rows0[:half], gate_matrix, up_matrix)]
+    given += [hidden_gradient(scaled0, down_matrix)]
+    computed0 = call_backward(
+        normed_last_kernel, rows0[half:], experts, slots, given, [gate_matrix, up_matrix]
+    )
+    returned0 = deal_all(computed0)
     rows1 = deal(normed(1, layer_rows[1], info, 0))
     rows1 += deal(normed(1, x1_mirror, info_mirror, half))
 
@@ -374,11 +431,14 @@
     )
     result0 = relayed[0]
     outgoing = to_slabs(relayed[1:], experts, slots)
-    scaled1 = [previous(outgoing[k], k) for k in range(experts)]
+    scaled1 = [previous(outgoing[k], k) for k in range(half)]
+    scaled1 += [previous(outgoing[k], k) for k in range(half, experts)]
     arrived = previous(result0, 0)
-    pre_gate1, pre_up1 = pre_activations(rows1, gate_matrix, up_matrix)
-    computed1 = expert_backward(scaled1, slots, pre_gate1, pre_up1, gate_matrix, up_matrix, down_matrix)
-    returned1 = deal(computed1)
+    given = [*pre_activations(rows1, gate_matrix, up_matrix)]
+    computed1 = call_backward(
+        gradient_last_kernel, scaled1, experts, slots, given, [down_matrix, gate_matrix, up_matrix]
+    )
+    returned1 = deal_all(computed1)
     (out,) = call_combine(
         final_kernel,
         returned1,

time: 238 us -> 234 us (0.983)
  the two profiles are of different devices: /device:TPU:12 before, /device:TPU:0 now
where the time goes in v4:
time: 234 us; the launch traced here: 230 us
  waiting for transfers between devices  103 us (44%)
  starting transfers between devices  85.3 us (36%)
  Pallas kernels  25.2 us (11%)
  local copies, waits for them, and re-layouts  13.4 us (6%)
  other arithmetic  2.84 us (1%)
    ppermute x36, waiting for transfers between devices, across(): return lax.ppermute(value, 'expert', [(i, i ^ k) for i in range(experts)])  86.6 us
    ppermute x36, starting transfers between devices, across(): return lax.ppermute(value, 'expert', [(i, i ^ k) for i in range(experts)])  75.3 us
    ppermute x9, waiting for transfers between devices, previous(): return lax.ppermute(value, ('section', 'expert'), pairs)  15.7 us
    unnamed x40, local copies, waits for them, and re-layouts  12.1 us
    ppermute x9, starting transfers between devices, previous(): return lax.ppermute(value, ('section', 'expert'), pairs)  10.1 us
    pallas_call x2, Pallas kernels, call_backward(): pl.pallas_call(functools.partial(kernel, piece(hidden, 256), piece(width,...  9.57 us
    pallas_call x2, Pallas kernels, pre_activations(): pl.pallas_call(functools.partial(pre_kernel, piece(hidden, 256)), in_spec...  5.33 us
  transfers between devices with their start and end apart: 46, of which 19 were waited for; matrix products, arithmetic and copies ran while one was open for 2% of the time, Pallas kernels for 10%

profile of v4, /device:TPU:0, one launch (start us, length us, event | category | flops | bytes accessed | tf_op | source)
XLA Modules:
  0.0 230.1 jit_solution(17947258516643501365)
XLA Ops:
  0.0 4.1 %collective-permute-start.11 = (bf16[128,2048]{1,0:T(8,128)(2,1)}, bf16[128,2048]{1,0:T(8,128)(2,1)S(1)}, u32[]{:S(2)}, u32[]{:S(2)}) collective-permute-start(bf16[128,2048]{1,0:T(8,128)(2,1)} %bitcast.40), channel_id=1, source_target_pairs={{0,4},{1,5},{2,6},{3,7},{4,0},{5,1},{6,2},{7,3},{8,12},{9,13},{10,... | collective-permute-start | bytes 1572872 | tf_op jit(solution)/shard_map/ppermute | solution.py:368
  8.4 2.9 %collective-permute-start = (f32[8,128]{1,0:T(8,128)S(1)}, f32[8,128]{1,0:T(8,128)S(1)}, u32[]{:S(2)}, u32[]{:S(2)}) collective-permute-start(f32[8,128]{1,0:T(8,128)S(1)} %bitcast.45), channel_id=1, source_target_pairs={{0,4},{1,5},{2,6},{3,7},{4,0},{5,1},{6,2},{7,3},{8,12},{9,13},{10,... | collective-permute-start | bytes 12296 | tf_op jit(solution)/shard_map/ppermute | solution.py:368
  15.8 34.3 %collective-permute-done.info_ref = f32[8,128]{1,0:T(8,128)S(1)} collective-permute-done((f32[8,128]{1,0:T(8,128)S(1)}, f32[8,128]{1,0:T(8,128)S(1)}, u32[]{:S(2)}, u32[]{:S(2)}) %collective-permute-start) | collective-permute-done | bytes 4128 | tf_op jit(solution)/shard_map/ppermute | solution.py:368
  60.1 3.7 %collective-permute-start.14 = (bf16[48,2048]{1,0:T(8,128)(2,1)S(1)}, bf16[48,2048]{1,0:T(8,128)(2,1)S(1)}, u32[]{:S(2)}, u32[]{:S(2)}) collective-permute-start(bf16[48,2048]{1,0:T(8,128)(2,1)S(1)} %get-tuple-element.75), channel_id=1, source_target_pairs={{0,3},{1,2},{2,1},{3,0},{4,7},{5,6},{6,5},{7,4},{8,11},{9,10},{10,... | collective-permute-start | bytes 589832 | tf_op jit(solution)/shard_map/ppermute | solution.py:368
  76.2 3.1 %collective-permute-start.34 = (bf16[128,2048]{1,0:T(8,128)(2,1)S(1)}, bf16[128,2048]{1,0:T(8,128)(2,1)S(1)}, u32[]{:S(2)}, u32[]{:S(2)}) collective-permute-start(bf16[128,2048]{1,0:T(8,128)(2,1)S(1)} %get-tuple-element.111.x_ref.refs_10_), channel_id=1, source_target_pairs={{0,4},{1,5},{2,6},{3,7},{4,0},{5,1},{6,2},{7,3},{8,12},{9,13},{10,... | collective-permute-start | bytes 1572872 | tf_op jit(solution)/shard_map/ppermute | solution.py:368
  80.8 6.7 %collective-permute-done.3.refs_2_ = bf16[48,2048]{1,0:T(8,128)(2,1)S(1)} collective-permute-done((bf16[48,2048]{1,0:T(8,128)(2,1)S(1)}, bf16[48,2048]{1,0:T(8,128)(2,1)S(1)}, u32[]{:S(2)}, u32[]{:S(2)}) %collective-permute-start.3) | collective-permute-done | bytes 196640 | tf_op jit(solution)/shard_map/ppermute | solution.py:368
  87.5 3.0 %collective-permute-done.4.refs_3_ = bf16[48,2048]{1,0:T(8,128)(2,1)S(1)} collective-permute-done((bf16[48,2048]{1,0:T(8,128)(2,1)S(1)}, bf16[48,2048]{1,0:T(8,128)(2,1)S(1)}, u32[]{:S(2)}, u32[]{:S(2)}) %collective-permute-start.4) | collective-permute-done | bytes 196640 | tf_op jit(solution)/shard_map/ppermute | solution.py:368
  90.5 4.6 %expert_backward.2 = (bf16[48,2048]{1,0:T(8,128)(2,1)S(1)}, bf16[48,2048]{1,0:T(8,128)(2,1)S(1)}, bf16[48,2048]{1,0:T(8,128)(2,1)S(1)}, bf16[48,2048]{1,0:T(8,12...) custom-call(bf16[48,2048]{1,0:T(8,128)(2,1)S(1)} %get-tuple-element., ...), custom_call_target="tpu_custom_call" | custom-call | flops 3623878656 | bytes 14942208 | tf_op jit(solution)/shard_map/expert_backward/pallas_call | solution.py:252
  106.5 5.0 %collective-permute-start.21 = (bf16[48,2048]{1,0:T(8,128)(2,1)}, bf16[48,2048]{1,0:T(8,128)(2,1)}, u32[]{:S(2)}, u32[]{:S(2)}) collective-permute-start(bf16[48,2048]{1,0:T(8,128)(2,1)} %get-tuple-element.83), channel_id=1, source_target_pairs={{0,7},{1,6},{2,5},{3,4},{4,3},{5,2},{6,1},{7,0},{8,15},{9,14},{10,... | collective-permute-start | bytes 589832 | tf_op jit(solution)/shard_map/ppermute | solution.py:368
  115.4 9.5 %collective-permute-done.18.refs_4_ = bf16[48,2048]{1,0:T(8,128)(2,1)S(1)} collective-permute-done((bf16[48,2048]{1,0:T(8,128)(2,1)S(1)}, bf16[48,2048]{1,0:T(8,128)(2,1)S(1)}, u32[]{:S(2)}, u32[]{:S(2)}) %collective-permute-start.18) | collective-permute-done | bytes 196640 | tf_op jit(solution)/shard_map/ppermute | solution.py:368
  124.9 4.6 %collective-permute-done.19.refs_5_ = bf16[48,2048]{1,0:T(8,128)(2,1)S(1)} collective-permute-done((bf16[48,2048]{1,0:T(8,128)(2,1)S(1)}, bf16[48,2048]{1,0:T(8,128)(2,1)S(1)}, u32[]{:S(2)}, u32[]{:S(2)}) %collective-permute-start.19) | collective-permute-done | bytes 196640 | tf_op jit(solution)/shard_map/ppermute | solution.py:368
  130.7 10.5 %collective-permute-start.36 = (bf16[48,2048]{1,0:T(8,128)(2,1)}, bf16[48,2048]{1,0:T(8,128)(2,1)S(1)}, u32[]{:S(2)}, u32[]{:S(2)}) collective-permute-start(bf16[48,2048]{1,0:T(8,128)(2,1)} %copy-done.19), channel_id=1, source_target_pairs={{0,2},{1,3},{2,0},{3,1},{4,6},{5,7},{6,4},{7,5},{8,10},{9,11},{10,... | collective-permute-start | bytes 589832 | tf_op jit(solution)/shard_map/ppermute | solution.py:368
  148.7 4.5 %collective-permute-done.37.refs_7_ = bf16[48,2048]{1,0:T(8,128)(2,1)S(1)} collective-permute-done((bf16[48,2048]{1,0:T(8,128)(2,1)}, bf16[48,2048]{1,0:T(8,128)(2,1)S(1)}, u32[]{:S(2)}, u32[]{:S(2)}) %collective-permute-start.37) | collective-permute-done | bytes 196640 | tf_op jit(solution)/shard_map/ppermute | solution.py:368
  155.9 5.3 %collective-permute-start.30 = (bf16[48,2048]{1,0:T(8,128)(2,1)S(1)}, bf16[48,2048]{1,0:T(8,128)(2,1)S(1)}, u32[]{:S(2)}, u32[]{:S(2)}) collective-permute-start(bf16[48,2048]{1,0:T(8,128)(2,1)S(1)} %get-tuple-element.91), channel_id=1, source_target_pairs={{0,31},{1,30},{2,29},{3,28},{4,27},{5,26},{6,25},{7,24},{8,7},{9,6... | collective-permute-start | bytes 589832 | tf_op jit(solution)/shard_map/ppermute | solution.py:379
  165.0 3.9 %pre_activations.3 = (f32[384,768]{1,0:T(8,128)S(1)}, f32[384,768]{1,0:T(8,128)S(1)}) custom-call(bf16[48,2048]{1,0:T(8,128)(2,1)S(1)} %copy-done.15, bf16[48,2048]{1,0:T(8,128)(2,1)} %collective-permute-done.31.refs_1_, bf16[48,2048]{1,0:T(8,128)(2,1)} %collective-permute-done.32.refs_2_, bf16[48,2048]{1,0:T(8,128)(2,1)} %collective-permute-done.33.refs_3_, ...), custom_call_target="tpu_custom_call" | custom-call | flops 2415919104 | bytes 10223616 | tf_op jit(solution)/shard_map/pre_activations/pallas_call | solution.py:157
  169.0 9.2 %collective-permute-done.27.refs_4_ = bf16[48,2048]{1,0:T(8,128)(2,1)S(1)} collective-permute-done((bf16[48,2048]{1,0:T(8,128)(2,1)S(1)}, bf16[48,2048]{1,0:T(8,128)(2,1)S(1)}, u32[]{:S(2)}, u32[]{:S(2)}) %collective-permute-start.27) | collective-permute-done | bytes 196640 | tf_op jit(solution)/shard_map/ppermute | solution.py:379
  178.2 4.2 %collective-permute-done.28.refs_5_ = bf16[48,2048]{1,0:T(8,128)(2,1)S(1)} collective-permute-done((bf16[48,2048]{1,0:T(8,128)(2,1)S(1)}, bf16[48,2048]{1,0:T(8,128)(2,1)S(1)}, u32[]{:S(2)}, u32[]{:S(2)}) %collective-permute-start.28) | collective-permute-done | bytes 196640 | tf_op jit(solution)/shard_map/ppermute | solution.py:379
  182.5 4.9 %expert_backward.3 = (bf16[48,2048]{1,0:T(8,128)(2,1)S(1)}, bf16[48,2048]{1,0:T(8,128)(2,1)S(1)}, bf16[48,2048]{1,0:T(8,128)(2,1)S(1)}, bf16[48,2048]{1,0:T(8,12...) custom-call(bf16[48,2048]{1,0:T(8,128)(2,1)S(1)} %collective-permute, ...), custom_call_target="tpu_custom_call" | custom-call | flops 3623878656 | bytes 14942208 | tf_op jit(solution)/shard_map/expert_backward/pallas_call | solution.py:252
  189.0 8.3 %collective-permute-start.39 = (bf16[48,2048]{1,0:T(8,128)(2,1)S(1)}, bf16[48,2048]{1,0:T(8,128)(2,1)S(1)}, u32[]{:S(2)}, u32[]{:S(2)}) collective-permute-start(bf16[48,2048]{1,0:T(8,128)(2,1)S(1)} %get-tuple-element.104), channel_id=1, source_target_pairs={{0,2},{1,3},{2,0},{3,1},{4,6},{5,7},{6,4},{7,5},{8,10},{9,11},{10,... | collective-permute-start | bytes 589832 | tf_op jit(solution)/shard_map/ppermute | solution.py:368
  197.2 2.8 %collective-permute-start.41 = (bf16[48,2048]{1,0:T(8,128)(2,1)S(1)}, bf16[48,2048]{1,0:T(8,128)(2,1)S(1)}, u32[]{:S(2)}, u32[]{:S(2)}) collective-permute-start(bf16[48,2048]{1,0:T(8,128)(2,1)S(1)} %get-tuple-element.106), channel_id=1, source_target_pairs={{0,4},{1,5},{2,6},{3,7},{4,0},{5,1},{6,2},{7,3},{8,12},{9,13},{10,... | collective-permute-start | bytes 589832 | tf_op jit(solution)/shard_map/ppermute | solution.py:368
  200.0 4.7 %collective-permute-start.42 = (bf16[48,2048]{1,0:T(8,128)(2,1)S(1)}, bf16[48,2048]{1,0:T(8,128)(2,1)S(1)}, u32[]{:S(2)}, u32[]{:S(2)}) collective-permute-start(bf16[48,2048]{1,0:T(8,128)(2,1)S(1)} %get-tuple-element.107), channel_id=1, source_target_pairs={{0,5},{1,4},{2,7},{3,6},{4,1},{5,0},{6,3},{7,2},{8,13},{9,12},{10,... | collective-permute-start | bytes 589832 | tf_op jit(solution)/shard_map/ppermute | solution.py:368
  204.7 4.2 %collective-permute-done.39.refs_2_ = bf16[48,2048]{1,0:T(8,128)(2,1)S(1)} collective-permute-done((bf16[48,2048]{1,0:T(8,128)(2,1)S(1)}, bf16[48,2048]{1,0:T(8,128)(2,1)S(1)}, u32[]{:S(2)}, u32[]{:S(2)}) %collective-permute-start.39) | collective-permute-done | bytes 196640 | tf_op jit(solution)/shard_map/ppermute | solution.py:368
  213.5 9.2 %collective-permute-done.41.refs_4_ = bf16[48,2048]{1,0:T(8,128)(2,1)S(1)} collective-permute-done((bf16[48,2048]{1,0:T(8,128)(2,1)S(1)}, bf16[48,2048]{1,0:T(8,128)(2,1)S(1)}, u32[]{:S(2)}, u32[]{:S(2)}) %collective-permute-start.41) | collective-permute-done | bytes 196640 | tf_op jit(solution)/shard_map/ppermute | solution.py:368
  222.7 5.1 %collective-permute-done.42.refs_5_ = bf16[48,2048]{1,0:T(8,128)(2,1)S(1)} collective-permute-done((bf16[48,2048]{1,0:T(8,128)(2,1)S(1)}, bf16[48,2048]{1,0:T(8,128)(2,1)S(1)}, u32[]{:S(2)}, u32[]{:S(2)}) %collective-permute-start.42) | collective-permute-done | bytes 196640 | tf_op jit(solution)/shard_map/ppermute | solution.py:368
  (129 shorter events, 71.4 us)
Async XLA Ops:
  0.0 52.1 %collective-permute-start.11 = (bf16[128,2048]{1,0:T(8,128)(2,1)}, bf16[128,2048]{1,0:T(8,128)(2,1)S(1)}, u32[]{:S(2)}, u32[]{:S(2)}) collective-permute-start(bf16[128,2048]{1,0:T(8,128)(2,1)} %bitcast.40), channel_id=1, source_target_pairs={{0,4},{1,5},{2,6},{3,7},{4,0},{5,1},{6,2},{7,3},{8,12},{9,13},{10,... | collective-permute-start | bytes 1572872 | tf_op jit(solution)/shard_map/ppermute | solution.py:368
  5.4 54.8 %collective-permute-start.1 = (bf16[128,2048]{1,0:T(8,128)(2,1)S(1)}, bf16[128,2048]{1,0:T(8,128)(2,1)S(1)}, u32[]{:S(2)}, u32[]{:S(2)}) collective-permute-start(bf16[128,2048]{1,0:T(8,128)(2,1)S(1)} %get-tuple-element.112.x_ref.refs_11_), channel_id=1, source_target_pairs={{0,4},{1,5},{2,6},{3,7},{4,0},{5,1},{6,2},{7,3},{8,12},{9,13},{10,... | collective-permute-start | bytes 1572872 | tf_op jit(solution)/shard_map/ppermute | solution.py:368
  8.4 41.7 %collective-permute-start = (f32[8,128]{1,0:T(8,128)S(1)}, f32[8,128]{1,0:T(8,128)S(1)}, u32[]{:S(2)}, u32[]{:S(2)}) collective-permute-start(f32[8,128]{1,0:T(8,128)S(1)} %bitcast.45), channel_id=1, source_target_pairs={{0,4},{1,5},{2,6},{3,7},{4,0},{5,1},{6,2},{7,3},{8,12},{9,13},{10,... | collective-permute-start | bytes 12296 | tf_op jit(solution)/shard_map/ppermute | solution.py:368
  12.7 41.4 %collective-permute-start.10 = (bf16[48,2048]{1,0:T(8,128)(2,1)S(1)}, bf16[48,2048]{1,0:T(8,128)(2,1)S(1)}, u32[]{:S(2)}, u32[]{:S(2)}) collective-permute-start(bf16[48,2048]{1,0:T(8,128)(2,1)S(1)} %get-tuple-element.71), channel_id=1, source_target_pairs={{0,3},{1,2},{2,1},{3,0},{4,7},{5,6},{6,5},{7,4},{8,11},{9,10},{10,... | collective-permute-start | bytes 589832 | tf_op jit(solution)/shard_map/ppermute | solution.py:368
  15.3 40.2 %collective-permute-start.8 = (bf16[48,2048]{1,0:T(8,128)(2,1)S(1)}, bf16[48,2048]{1,0:T(8,128)(2,1)S(1)}, u32[]{:S(2)}, u32[]{:S(2)}) collective-permute-start(bf16[48,2048]{1,0:T(8,128)(2,1)S(1)} %get-tuple-element.69), channel_id=1, source_target_pairs={{0,1},{1,0},{2,3},{3,2},{4,5},{5,4},{6,7},{7,6},{8,9},{9,8},{10,11... | collective-permute-start | bytes 589832 | tf_op jit(solution)/shard_map/ppermute | solution.py:368
  60.1 19.2 %collective-permute-start.14 = (bf16[48,2048]{1,0:T(8,128)(2,1)S(1)}, bf16[48,2048]{1,0:T(8,128)(2,1)S(1)}, u32[]{:S(2)}, u32[]{:S(2)}) collective-permute-start(bf16[48,2048]{1,0:T(8,128)(2,1)S(1)} %get-tuple-element.75), channel_id=1, source_target_pairs={{0,3},{1,2},{2,1},{3,0},{4,7},{5,6},{6,5},{7,4},{8,11},{9,10},{10,... | collective-permute-start | bytes 589832 | tf_op jit(solution)/shard_map/ppermute | solution.py:368
  66.2 21.3 %collective-permute-start.3 = (bf16[48,2048]{1,0:T(8,128)(2,1)S(1)}, bf16[48,2048]{1,0:T(8,128)(2,1)S(1)}, u32[]{:S(2)}, u32[]{:S(2)}) collective-permute-start(bf16[48,2048]{1,0:T(8,128)(2,1)S(1)} %get-tuple-element.60), channel_id=1, source_target_pairs={{0,2},{1,3},{2,0},{3,1},{4,6},{5,7},{6,4},{7,5},{8,10},{9,11},{10,... | collective-permute-start | bytes 589832 | tf_op jit(solution)/shard_map/ppermute | solution.py:368
  68.2 22.2 %collective-permute-start.4 = (bf16[48,2048]{1,0:T(8,128)(2,1)S(1)}, bf16[48,2048]{1,0:T(8,128)(2,1)S(1)}, u32[]{:S(2)}, u32[]{:S(2)}) collective-permute-start(bf16[48,2048]{1,0:T(8,128)(2,1)S(1)} %get-tuple-element.61), channel_id=1, source_target_pairs={{0,3},{1,2},{2,1},{3,0},{4,7},{5,6},{6,5},{7,4},{8,11},{9,10},{10,... | collective-permute-start | bytes 589832 | tf_op jit(solution)/shard_map/ppermute | solution.py:368
  76.2 24.2 %collective-permute-start.34 = (bf16[128,2048]{1,0:T(8,128)(2,1)S(1)}, bf16[128,2048]{1,0:T(8,128)(2,1)S(1)}, u32[]{:S(2)}, u32[]{:S(2)}) collective-permute-start(bf16[128,2048]{1,0:T(8,128)(2,1)S(1)} %get-tuple-element.111.x_ref.refs_10_), channel_id=1, source_target_pairs={{0,4},{1,5},{2,6},{3,7},{4,0},{5,1},{6,2},{7,3},{8,12},{9,13},{10,... | collective-permute-start | bytes 1572872 | tf_op jit(solution)/shard_map/ppermute | solution.py:368
  99.3 25.6 %collective-permute-start.18 = (bf16[48,2048]{1,0:T(8,128)(2,1)S(1)}, bf16[48,2048]{1,0:T(8,128)(2,1)S(1)}, u32[]{:S(2)}, u32[]{:S(2)}) collective-permute-start(bf16[48,2048]{1,0:T(8,128)(2,1)S(1)} %get-tuple-element.80), channel_id=1, source_target_pairs={{0,4},{1,5},{2,6},{3,7},{4,0},{5,1},{6,2},{7,3},{8,12},{9,13},{10,... | collective-permute-start | bytes 589832 | tf_op jit(solution)/shard_map/ppermute | solution.py:368
  100.4 29.2 %collective-permute-start.19 = (bf16[48,2048]{1,0:T(8,128)(2,1)S(1)}, bf16[48,2048]{1,0:T(8,128)(2,1)S(1)}, u32[]{:S(2)}, u32[]{:S(2)}) collective-permute-start(bf16[48,2048]{1,0:T(8,128)(2,1)S(1)} %get-tuple-element.81), channel_id=1, source_target_pairs={{0,5},{1,4},{2,7},{3,6},{4,1},{5,0},{6,3},{7,2},{8,13},{9,12},{10,... | collective-permute-start | bytes 589832 | tf_op jit(solution)/shard_map/ppermute | solution.py:368
  102.5 27.0 %collective-permute-start.20 = (bf16[48,2048]{1,0:T(8,128)(2,1)S(1)}, bf16[48,2048]{1,0:T(8,128)(2,1)S(1)}, u32[]{:S(2)}, u32[]{:S(2)}) collective-permute-start(bf16[48,2048]{1,0:T(8,128)(2,1)S(1)} %get-tuple-element.82), channel_id=1, source_target_pairs={{0,6},{1,7},{2,4},{3,5},{4,2},{5,3},{6,0},{7,1},{8,14},{9,15},{10,... | collective-permute-start | bytes 589832 | tf_op jit(solution)/shard_map/ppermute | solution.py:368
  106.5 24.2 %collective-permute-start.21 = (bf16[48,2048]{1,0:T(8,128)(2,1)}, bf16[48,2048]{1,0:T(8,128)(2,1)}, u32[]{:S(2)}, u32[]{:S(2)}) collective-permute-start(bf16[48,2048]{1,0:T(8,128)(2,1)} %get-tuple-element.83), channel_id=1, source_target_pairs={{0,7},{1,6},{2,5},{3,4},{4,3},{5,2},{6,1},{7,0},{8,15},{9,14},{10,... | collective-permute-start | bytes 589832 | tf_op jit(solution)/shard_map/ppermute | solution.py:368
  114.9 28.6 %collective-permute-start.31 = (bf16[48,2048]{1,0:T(8,128)(2,1)}, bf16[48,2048]{1,0:T(8,128)(2,1)}, u32[]{:S(2)}, u32[]{:S(2)}) collective-permute-start(bf16[48,2048]{1,0:T(8,128)(2,1)} %get-tuple-element.93), channel_id=1, source_target_pairs={{0,1},{1,0},{2,3},{3,2},{4,5},{5,4},{6,7},{7,6},{8,9},{9,8},{10,11... | collective-permute-start | bytes 589832 | tf_op jit(solution)/shard_map/ppermute | solution.py:368
  124.9 19.5 %collective-permute-start.32 = (bf16[48,2048]{1,0:T(8,128)(2,1)}, bf16[48,2048]{1,0:T(8,128)(2,1)}, u32[]{:S(2)}, u32[]{:S(2)}) collective-permute-start(bf16[48,2048]{1,0:T(8,128)(2,1)} %get-tuple-element.94), channel_id=1, source_target_pairs={{0,2},{1,3},{2,0},{3,1},{4,6},{5,7},{6,4},{7,5},{8,10},{9,11},{10,... | collective-permute-start | bytes 589832 | tf_op jit(solution)/shard_map/ppermute | solution.py:368
  147.3 21.7 %collective-permute-start.26 = (bf16[48,2048]{1,0:T(8,128)(2,1)S(1)}, bf16[48,2048]{1,0:T(8,128)(2,1)S(1)}, u32[]{:S(2)}, u32[]{:S(2)}) collective-permute-start(bf16[48,2048]{1,0:T(8,128)(2,1)S(1)} %get-tuple-element.87), channel_id=1, source_target_pairs={{0,27},{1,26},{2,25},{3,24},{4,31},{5,30},{6,29},{7,28},{8,3},{9,2... | collective-permute-start | bytes 589832 | tf_op jit(solution)/shard_map/ppermute | solution.py:379
  153.2 25.0 %collective-permute-start.27 = (bf16[48,2048]{1,0:T(8,128)(2,1)S(1)}, bf16[48,2048]{1,0:T(8,128)(2,1)S(1)}, u32[]{:S(2)}, u32[]{:S(2)}) collective-permute-start(bf16[48,2048]{1,0:T(8,128)(2,1)S(1)} %get-tuple-element.88), channel_id=1, source_target_pairs={{0,28},{1,29},{2,30},{3,31},{4,24},{5,25},{6,26},{7,27},{8,4},{9,5... | collective-permute-start | bytes 589832 | tf_op jit(solution)/shard_map/ppermute | solution.py:379
  153.2 29.2 %collective-permute-start.28 = (bf16[48,2048]{1,0:T(8,128)(2,1)S(1)}, bf16[48,2048]{1,0:T(8,128)(2,1)S(1)}, u32[]{:S(2)}, u32[]{:S(2)}) collective-permute-start(bf16[48,2048]{1,0:T(8,128)(2,1)S(1)} %get-tuple-element.89), channel_id=1, source_target_pairs={{0,29},{1,28},{2,31},{3,30},{4,25},{5,24},{6,27},{7,26},{8,5},{9,4... | collective-permute-start | bytes 589832 | tf_op jit(solution)/shard_map/ppermute | solution.py:379
  155.9 26.6 %collective-permute-start.29 = (bf16[48,2048]{1,0:T(8,128)(2,1)S(1)}, bf16[48,2048]{1,0:T(8,128)(2,1)S(1)}, u32[]{:S(2)}, u32[]{:S(2)}) collective-permute-start(bf16[48,2048]{1,0:T(8,128)(2,1)S(1)} %get-tuple-element.90), channel_id=1, source_target_pairs={{0,30},{1,31},{2,28},{3,29},{4,26},{5,27},{6,24},{7,25},{8,6},{9,7... | collective-permute-start | bytes 589832 | tf_op jit(solution)/shard_map/ppermute | solution.py:379
  155.9 26.6 %collective-permute-start.30 = (bf16[48,2048]{1,0:T(8,128)(2,1)S(1)}, bf16[48,2048]{1,0:T(8,128)(2,1)S(1)}, u32[]{:S(2)}, u32[]{:S(2)}) collective-permute-start(bf16[48,2048]{1,0:T(8,128)(2,1)S(1)} %get-tuple-element.91), channel_id=1, source_target_pairs={{0,31},{1,30},{2,29},{3,28},{4,27},{5,26},{6,25},{7,24},{8,7},{9,6... | collective-permute-start | bytes 589832 | tf_op jit(solution)/shard_map/ppermute | solution.py:379
  169.0 58.9 %collective-permute-start.45 = (bf16[128,2048]{1,0:T(8,128)(2,1)S(1)}, bf16[128,2048]{1,0:T(8,128)(2,1)S(1)}, u32[]{:S(2)}, u32[]{:S(2)}) collective-permute-start(bf16[128,2048]{1,0:T(8,128)(2,1)S(1)} %get-tuple-element.110.refs_14_), channel_id=1, source_target_pairs={{0,24},{1,25},{2,26},{3,27},{4,28},{5,29},{6,30},{7,31},{8,0},{9,1... | collective-permute-start | bytes 1572872 | tf_op jit(solution)/shard_map/ppermute | solution.py:379
  189.0 19.9 %collective-permute-start.39 = (bf16[48,2048]{1,0:T(8,128)(2,1)S(1)}, bf16[48,2048]{1,0:T(8,128)(2,1)S(1)}, u32[]{:S(2)}, u32[]{:S(2)}) collective-permute-start(bf16[48,2048]{1,0:T(8,128)(2,1)S(1)} %get-tuple-element.104), channel_id=1, source_target_pairs={{0,2},{1,3},{2,0},{3,1},{4,6},{5,7},{6,4},{7,5},{8,10},{9,11},{10,... | collective-permute-start | bytes 589832 | tf_op jit(solution)/shard_map/ppermute | solution.py:368
  197.2 25.5 %collective-permute-start.41 = (bf16[48,2048]{1,0:T(8,128)(2,1)S(1)}, bf16[48,2048]{1,0:T(8,128)(2,1)S(1)}, u32[]{:S(2)}, u32[]{:S(2)}) collective-permute-start(bf16[48,2048]{1,0:T(8,128)(2,1)S(1)} %get-tuple-element.106), channel_id=1, source_target_pairs={{0,4},{1,5},{2,6},{3,7},{4,0},{5,1},{6,2},{7,3},{8,12},{9,13},{10,... | collective-permute-start | bytes 589832 | tf_op jit(solution)/shard_map/ppermute | solution.py:368
  200.0 27.8 %collective-permute-start.42 = (bf16[48,2048]{1,0:T(8,128)(2,1)S(1)}, bf16[48,2048]{1,0:T(8,128)(2,1)S(1)}, u32[]{:S(2)}, u32[]{:S(2)}) collective-permute-start(bf16[48,2048]{1,0:T(8,128)(2,1)S(1)} %get-tuple-element.107), channel_id=1, source_target_pairs={{0,5},{1,4},{2,7},{3,6},{4,1},{5,0},{6,3},{7,2},{8,13},{9,12},{10,... | collective-permute-start | bytes 589832 | tf_op jit(solution)/shard_map/ppermute | solution.py:368
  (42 other events, 546.4 us)

commit v5 on v4

--- a/solution.py
+++ b/solution.py
@@ -411,7 +411,10 @@
 
     def deal_all(slabs):
         near = deal(slabs[:half])
-        return near + [across(slabs[k], k) for k in range(half, experts)]
+        far = []
+        for k in range(half, experts):
+            far.append(across(slabs[k], k))
+        return near + far
 
     given = [*pre_activations(rows0[:half], gate_matrix, up_matrix)]
     given += [hidden_gradient(scaled0, down_matrix)]
@@ -432,7 +435,8 @@
     result0 = relayed[0]
     outgoing = to_slabs(relayed[1:], experts, slots)
     scaled1 = [previous(outgoing[k], k) for k in range(half)]
-    scaled1 += [previous(outgoing[k], k) for k in range(half, experts)]
+    for k in range(half, experts):
+        scaled1.append(previous(outgoing[k], k))
     arrived = previous(result0, 0)
     given = [*pre_activations(rows1, gate_matrix, up_matrix)]
     computed1 = call_backward(

time: 234 us -> 234 us (level)
  no operation moved by 1% of the time
where the time goes in v5:
time: 234 us; the launch traced here: 230 us
  waiting for transfers between devices  103 us (44%)
  starting transfers between devices  85.3 us (36%)
  Pallas kernels  25.2 us (11%)
  local copies, waits for them, and re-layouts  13.4 us (6%)
  other arithmetic  2.84 us (1%)
    ppermute x36, waiting for transfers between devices, across(): return lax.ppermute(value, 'expert', [(i, i ^ k) for i in range(experts)])  86.6 us
    ppermute x36, starting transfers between devices, across(): return lax.ppermute(value, 'expert', [(i, i ^ k) for i in range(experts)])  75.3 us
    ppermute x9, waiting for transfers between devices, previous(): return lax.ppermute(value, ('section', 'expert'), pairs)  15.7 us
    unnamed x40, local copies, waits for them, and re-layouts  12.1 us
    ppermute x9, starting transfers between devices, previous(): return lax.ppermute(value, ('section', 'expert'), pairs)  10.1 us
    pallas_call x2, Pallas kernels, call_backward(): pl.pallas_call(functools.partial(kernel, piece(hidden, 256), piece(width,...  9.57 us
    pallas_call x2, Pallas kernels, pre_activations(): pl.pallas_call(functools.partial(pre_kernel, piece(hidden, 256)), in_spec...  5.33 us
  transfers between devices with their start and end apart: 46, of which 19 were waited for; matrix products, arithmetic and copies ran while one was open for 2% of the time, Pallas kernels for 10%

profile of v5, /device:TPU:0, one launch (start us, length us, event | category | flops | bytes accessed | tf_op | source)
XLA Modules:
  0.0 230.1 jit_solution(17947258516643501365)
XLA Ops:
  0.0 4.1 %collective-permute-start.11 = (bf16[128,2048]{1,0:T(8,128)(2,1)}, bf16[128,2048]{1,0:T(8,128)(2,1)S(1)}, u32[]{:S(2)}, u32[]{:S(2)}) collective-permute-start(bf16[128,2048]{1,0:T(8,128)(2,1)} %bitcast.40), channel_id=1, source_target_pairs={{0,4},{1,5},{2,6},{3,7},{4,0},{5,1},{6,2},{7,3},{8,12},{9,13},{10,... | collective-permute-start | bytes 1572872 | tf_op jit(solution)/shard_map/ppermute | solution.py:368
  8.4 2.9 %collective-permute-start = (f32[8,128]{1,0:T(8,128)S(1)}, f32[8,128]{1,0:T(8,128)S(1)}, u32[]{:S(2)}, u32[]{:S(2)}) collective-permute-start(f32[8,128]{1,0:T(8,128)S(1)} %bitcast.45), channel_id=1, source_target_pairs={{0,4},{1,5},{2,6},{3,7},{4,0},{5,1},{6,2},{7,3},{8,12},{9,13},{10,... | collective-permute-start | bytes 12296 | tf_op jit(solution)/shard_map/ppermute | solution.py:368
  15.8 34.3 %collective-permute-done.info_ref = f32[8,128]{1,0:T(8,128)S(1)} collective-permute-done((f32[8,128]{1,0:T(8,128)S(1)}, f32[8,128]{1,0:T(8,128)S(1)}, u32[]{:S(2)}, u32[]{:S(2)}) %collective-permute-start) | collective-permute-done | bytes 4128 | tf_op jit(solution)/shard_map/ppermute | solution.py:368
  60.1 3.7 %collective-permute-start.14 = (bf16[48,2048]{1,0:T(8,128)(2,1)S(1)}, bf16[48,2048]{1,0:T(8,128)(2,1)S(1)}, u32[]{:S(2)}, u32[]{:S(2)}) collective-permute-start(bf16[48,2048]{1,0:T(8,128)(2,1)S(1)} %get-tuple-element.75), channel_id=1, source_target_pairs={{0,3},{1,2},{2,1},{3,0},{4,7},{5,6},{6,5},{7,4},{8,11},{9,10},{10,... | collective-permute-start | bytes 589832 | tf_op jit(solution)/shard_map/ppermute | solution.py:368
  76.2 3.1 %collective-permute-start.34 = (bf16[128,2048]{1,0:T(8,128)(2,1)S(1)}, bf16[128,2048]{1,0:T(8,128)(2,1)S(1)}, u32[]{:S(2)}, u32[]{:S(2)}) collective-permute-start(bf16[128,2048]{1,0:T(8,128)(2,1)S(1)} %get-tuple-element.111.x_ref.refs_10_), channel_id=1, source_target_pairs={{0,4},{1,5},{2,6},{3,7},{4,0},{5,1},{6,2},{7,3},{8,12},{9,13},{10,... | collective-permute-start | bytes 1572872 | tf_op jit(solution)/shard_map/ppermute | solution.py:368
  80.8 6.7 %collective-permute-done.3.refs_2_ = bf16[48,2048]{1,0:T(8,128)(2,1)S(1)} collective-permute-done((bf16[48,2048]{1,0:T(8,128)(2,1)S(1)}, bf16[48,2048]{1,0:T(8,128)(2,1)S(1)}, u32[]{:S(2)}, u32[]{:S(2)}) %collective-permute-start.3) | collective-permute-done | bytes 196640 | tf_op jit(solution)/shard_map/ppermute | solution.py:368
  87.5 3.0 %collective-permute-done.4.refs_3_ = bf16[48,2048]{1,0:T(8,128)(2,1)S(1)} collective-permute-done((bf16[48,2048]{1,0:T(8,128)(2,1)S(1)}, bf16[48,2048]{1,0:T(8,128)(2,1)S(1)}, u32[]{:S(2)}, u32[]{:S(2)}) %collective-permute-start.4) | collective-permute-done | bytes 196640 | tf_op jit(solution)/shard_map/ppermute | solution.py:368
  90.5 4.6 %expert_backward.2 = (bf16[48,2048]{1,0:T(8,128)(2,1)S(1)}, bf16[48,2048]{1,0:T(8,128)(2,1)S(1)}, bf16[48,2048]{1,0:T(8,128)(2,1)S(1)}, bf16[48,2048]{1,0:T(8,12...) custom-call(bf16[48,2048]{1,0:T(8,128)(2,1)S(1)} %get-tuple-element., ...), custom_call_target="tpu_custom_call" | custom-call | flops 3623878656 | bytes 14942208 | tf_op jit(solution)/shard_map/expert_backward/pallas_call | solution.py:252
  106.5 5.0 %collective-permute-start.21 = (bf16[48,2048]{1,0:T(8,128)(2,1)}, bf16[48,2048]{1,0:T(8,128)(2,1)}, u32[]{:S(2)}, u32[]{:S(2)}) collective-permute-start(bf16[48,2048]{1,0:T(8,128)(2,1)} %get-tuple-element.83), channel_id=1, source_target_pairs={{0,7},{1,6},{2,5},{3,4},{4,3},{5,2},{6,1},{7,0},{8,15},{9,14},{10,... | collective-permute-start | bytes 589832 | tf_op jit(solution)/shard_map/ppermute | solution.py:368
  115.4 9.5 %collective-permute-done.18.refs_4_ = bf16[48,2048]{1,0:T(8,128)(2,1)S(1)} collective-permute-done((bf16[48,2048]{1,0:T(8,128)(2,1)S(1)}, bf16[48,2048]{1,0:T(8,128)(2,1)S(1)}, u32[]{:S(2)}, u32[]{:S(2)}) %collective-permute-start.18) | collective-permute-done | bytes 196640 | tf_op jit(solution)/shard_map/ppermute | solution.py:368
  124.9 4.6 %collective-permute-done.19.refs_5_ = bf16[48,2048]{1,0:T(8,128)(2,1)S(1)} collective-permute-done((bf16[48,2048]{1,0:T(8,128)(2,1)S(1)}, bf16[48,2048]{1,0:T(8,128)(2,1)S(1)}, u32[]{:S(2)}, u32[]{:S(2)}) %collective-permute-start.19) | collective-permute-done | bytes 196640 | tf_op jit(solution)/shard_map/ppermute | solution.py:368
  130.7 10.5 %collective-permute-start.36 = (bf16[48,2048]{1,0:T(8,128)(2,1)}, bf16[48,2048]{1,0:T(8,128)(2,1)S(1)}, u32[]{:S(2)}, u32[]{:S(2)}) collective-permute-start(bf16[48,2048]{1,0:T(8,128)(2,1)} %copy-done.19), channel_id=1, source_target_pairs={{0,2},{1,3},{2,0},{3,1},{4,6},{5,7},{6,4},{7,5},{8,10},{9,11},{10,... | collective-permute-start | bytes 589832 | tf_op jit(solution)/shard_map/ppermute | solution.py:368
  148.7 4.5 %collective-permute-done.37.refs_7_ = bf16[48,2048]{1,0:T(8,128)(2,1)S(1)} collective-permute-done((bf16[48,2048]{1,0:T(8,128)(2,1)}, bf16[48,2048]{1,0:T(8,128)(2,1)S(1)}, u32[]{:S(2)}, u32[]{:S(2)}) %collective-permute-start.37) | collective-permute-done | bytes 196640 | tf_op jit(solution)/shard_map/ppermute | solution.py:368
  155.9 5.3 %collective-permute-start.30 = (bf16[48,2048]{1,0:T(8,128)(2,1)S(1)}, bf16[48,2048]{1,0:T(8,128)(2,1)S(1)}, u32[]{:S(2)}, u32[]{:S(2)}) collective-permute-start(bf16[48,2048]{1,0:T(8,128)(2,1)S(1)} %get-tuple-element.91), channel_id=1, source_target_pairs={{0,31},{1,30},{2,29},{3,28},{4,27},{5,26},{6,25},{7,24},{8,7},{9,6... | collective-permute-start | bytes 589832 | tf_op jit(solution)/shard_map/ppermute | solution.py:379
  165.0 3.9 %pre_activations.3 = (f32[384,768]{1,0:T(8,128)S(1)}, f32[384,768]{1,0:T(8,128)S(1)}) custom-call(bf16[48,2048]{1,0:T(8,128)(2,1)S(1)} %copy-done.15, bf16[48,2048]{1,0:T(8,128)(2,1)} %collective-permute-done.31.refs_1_, bf16[48,2048]{1,0:T(8,128)(2,1)} %collective-permute-done.32.refs_2_, bf16[48,2048]{1,0:T(8,128)(2,1)} %collective-permute-done.33.refs_3_, ...), custom_call_target="tpu_custom_call" | custom-call | flops 2415919104 | bytes 10223616 | tf_op jit(solution)/shard_map/pre_activations/pallas_call | solution.py:157
  169.0 9.2 %collective-permute-done.27.refs_4_ = bf16[48,2048]{1,0:T(8,128)(2,1)S(1)} collective-permute-done((bf16[48,2048]{1,0:T(8,128)(2,1)S(1)}, bf16[48,2048]{1,0:T(8,128)(2,1)S(1)}, u32[]{:S(2)}, u32[]{:S(2)}) %collective-permute-start.27) | collective-permute-done | bytes 196640 | tf_op jit(solution)/shard_map/ppermute | solution.py:379
  178.2 4.2 %collective-permute-done.28.refs_5_ = bf16[48,2048]{1,0:T(8,128)(2,1)S(1)} collective-permute-done((bf16[48,2048]{1,0:T(8,128)(2,1)S(1)}, bf16[48,2048]{1,0:T(8,128)(2,1)S(1)}, u32[]{:S(2)}, u32[]{:S(2)}) %collective-permute-start.28) | collective-permute-done | bytes 196640 | tf_op jit(solution)/shard_map/ppermute | solution.py:379
  182.5 4.9 %expert_backward.3 = (bf16[48,2048]{1,0:T(8,128)(2,1)S(1)}, bf16[48,2048]{1,0:T(8,128)(2,1)S(1)}, bf16[48,2048]{1,0:T(8,128)(2,1)S(1)}, bf16[48,2048]{1,0:T(8,12...) custom-call(bf16[48,2048]{1,0:T(8,128)(2,1)S(1)} %collective-permute, ...), custom_call_target="tpu_custom_call" | custom-call | flops 3623878656 | bytes 14942208 | tf_op jit(solution)/shard_map/expert_backward/pallas_call | solution.py:252
  189.0 8.3 %collective-permute-start.39 = (bf16[48,2048]{1,0:T(8,128)(2,1)S(1)}, bf16[48,2048]{1,0:T(8,128)(2,1)S(1)}, u32[]{:S(2)}, u32[]{:S(2)}) collective-permute-start(bf16[48,2048]{1,0:T(8,128)(2,1)S(1)} %get-tuple-element.104), channel_id=1, source_target_pairs={{0,2},{1,3},{2,0},{3,1},{4,6},{5,7},{6,4},{7,5},{8,10},{9,11},{10,... | collective-permute-start | bytes 589832 | tf_op jit(solution)/shard_map/ppermute | solution.py:368
  197.2 2.8 %collective-permute-start.41 = (bf16[48,2048]{1,0:T(8,128)(2,1)S(1)}, bf16[48,2048]{1,0:T(8,128)(2,1)S(1)}, u32[]{:S(2)}, u32[]{:S(2)}) collective-permute-start(bf16[48,2048]{1,0:T(8,128)(2,1)S(1)} %get-tuple-element.106), channel_id=1, source_target_pairs={{0,4},{1,5},{2,6},{3,7},{4,0},{5,1},{6,2},{7,3},{8,12},{9,13},{10,... | collective-permute-start | bytes 589832 | tf_op jit(solution)/shard_map/ppermute | solution.py:368
  200.0 4.7 %collective-permute-start.42 = (bf16[48,2048]{1,0:T(8,128)(2,1)S(1)}, bf16[48,2048]{1,0:T(8,128)(2,1)S(1)}, u32[]{:S(2)}, u32[]{:S(2)}) collective-permute-start(bf16[48,2048]{1,0:T(8,128)(2,1)S(1)} %get-tuple-element.107), channel_id=1, source_target_pairs={{0,5},{1,4},{2,7},{3,6},{4,1},{5,0},{6,3},{7,2},{8,13},{9,12},{10,... | collective-permute-start | bytes 589832 | tf_op jit(solution)/shard_map/ppermute | solution.py:368
  204.7 4.2 %collective-permute-done.39.refs_2_ = bf16[48,2048]{1,0:T(8,128)(2,1)S(1)} collective-permute-done((bf16[48,2048]{1,0:T(8,128)(2,1)S(1)}, bf16[48,2048]{1,0:T(8,128)(2,1)S(1)}, u32[]{:S(2)}, u32[]{:S(2)}) %collective-permute-start.39) | collective-permute-done | bytes 196640 | tf_op jit(solution)/shard_map/ppermute | solution.py:368
  213.5 9.2 %collective-permute-done.41.refs_4_ = bf16[48,2048]{1,0:T(8,128)(2,1)S(1)} collective-permute-done((bf16[48,2048]{1,0:T(8,128)(2,1)S(1)}, bf16[48,2048]{1,0:T(8,128)(2,1)S(1)}, u32[]{:S(2)}, u32[]{:S(2)}) %collective-permute-start.41) | collective-permute-done | bytes 196640 | tf_op jit(solution)/shard_map/ppermute | solution.py:368
  222.7 5.1 %collective-permute-done.42.refs_5_ = bf16[48,2048]{1,0:T(8,128)(2,1)S(1)} collective-permute-done((bf16[48,2048]{1,0:T(8,128)(2,1)S(1)}, bf16[48,2048]{1,0:T(8,128)(2,1)S(1)}, u32[]{:S(2)}, u32[]{:S(2)}) %collective-permute-start.42) | collective-permute-done | bytes 196640 | tf_op jit(solution)/shard_map/ppermute | solution.py:368
  (129 shorter events, 71.4 us)
Async XLA Ops:
  0.0 52.1 %collective-permute-start.11 = (bf16[128,2048]{1,0:T(8,128)(2,1)}, bf16[128,2048]{1,0:T(8,128)(2,1)S(1)}, u32[]{:S(2)}, u32[]{:S(2)}) collective-permute-start(bf16[128,2048]{1,0:T(8,128)(2,1)} %bitcast.40), channel_id=1, source_target_pairs={{0,4},{1,5},{2,6},{3,7},{4,0},{5,1},{6,2},{7,3},{8,12},{9,13},{10,... | collective-permute-start | bytes 1572872 | tf_op jit(solution)/shard_map/ppermute | solution.py:368
  5.4 54.8 %collective-permute-start.1 = (bf16[128,2048]{1,0:T(8,128)(2,1)S(1)}, bf16[128,2048]{1,0:T(8,128)(2,1)S(1)}, u32[]{:S(2)}, u32[]{:S(2)}) collective-permute-start(bf16[128,2048]{1,0:T(8,128)(2,1)S(1)} %get-tuple-element.112.x_ref.refs_11_), channel_id=1, source_target_pairs={{0,4},{1,5},{2,6},{3,7},{4,0},{5,1},{6,2},{7,3},{8,12},{9,13},{10,... | collective-permute-start | bytes 1572872 | tf_op jit(solution)/shard_map/ppermute | solution.py:368
  8.4 41.7 %collective-permute-start = (f32[8,128]{1,0:T(8,128)S(1)}, f32[8,128]{1,0:T(8,128)S(1)}, u32[]{:S(2)}, u32[]{:S(2)}) collective-permute-start(f32[8,128]{1,0:T(8,128)S(1)} %bitcast.45), channel_id=1, source_target_pairs={{0,4},{1,5},{2,6},{3,7},{4,0},{5,1},{6,2},{7,3},{8,12},{9,13},{10,... | collective-permute-start | bytes 12296 | tf_op jit(solution)/shard_map/ppermute | solution.py:368
  12.7 41.4 %collective-permute-start.10 = (bf16[48,2048]{1,0:T(8,128)(2,1)S(1)}, bf16[48,2048]{1,0:T(8,128)(2,1)S(1)}, u32[]{:S(2)}, u32[]{:S(2)}) collective-permute-start(bf16[48,2048]{1,0:T(8,128)(2,1)S(1)} %get-tuple-element.71), channel_id=1, source_target_pairs={{0,3},{1,2},{2,1},{3,0},{4,7},{5,6},{6,5},{7,4},{8,11},{9,10},{10,... | collective-permute-start | bytes 589832 | tf_op jit(solution)/shard_map/ppermute | solution.py:368
  15.3 40.2 %collective-permute-start.8 = (bf16[48,2048]{1,0:T(8,128)(2,1)S(1)}, bf16[48,2048]{1,0:T(8,128)(2,1)S(1)}, u32[]{:S(2)}, u32[]{:S(2)}) collective-permute-start(bf16[48,2048]{1,0:T(8,128)(2,1)S(1)} %get-tuple-element.69), channel_id=1, source_target_pairs={{0,1},{1,0},{2,3},{3,2},{4,5},{5,4},{6,7},{7,6},{8,9},{9,8},{10,11... | collective-permute-start | bytes 589832 | tf_op jit(solution)/shard_map/ppermute | solution.py:368
  60.1 19.2 %collective-permute-start.14 = (bf16[48,2048]{1,0:T(8,128)(2,1)S(1)}, bf16[48,2048]{1,0:T(8,128)(2,1)S(1)}, u32[]{:S(2)}, u32[]{:S(2)}) collective-permute-start(bf16[48,2048]{1,0:T(8,128)(2,1)S(1)} %get-tuple-element.75), channel_id=1, source_target_pairs={{0,3},{1,2},{2,1},{3,0},{4,7},{5,6},{6,5},{7,4},{8,11},{9,10},{10,... | collective-permute-start | bytes 589832 | tf_op jit(solution)/shard_map/ppermute | solution.py:368
  66.2 21.3 %collective-permute-start.3 = (bf16[48,2048]{1,0:T(8,128)(2,1)S(1)}, bf16[48,2048]{1,0:T(8,128)(2,1)S(1)}, u32[]{:S(2)}, u32[]{:S(2)}) collective-permute-start(bf16[48,2048]{1,0:T(8,128)(2,1)S(1)} %get-tuple-element.60), channel_id=1, source_target_pairs={{0,2},{1,3},{2,0},{3,1},{4,6},{5,7},{6,4},{7,5},{8,10},{9,11},{10,... | collective-permute-start | bytes 589832 | tf_op jit(solution)/shard_map/ppermute | solution.py:368
  68.2 22.2 %collective-permute-start.4 = (bf16[48,2048]{1,0:T(8,128)(2,1)S(1)}, bf16[48,2048]{1,0:T(8,128)(2,1)S(1)}, u32[]{:S(2)}, u32[]{:S(2)}) collective-permute-start(bf16[48,2048]{1,0:T(8,128)(2,1)S(1)} %get-tuple-element.61), channel_id=1, source_target_pairs={{0,3},{1,2},{2,1},{3,0},{4,7},{5,6},{6,5},{7,4},{8,11},{9,10},{10,... | collective-permute-start | bytes 589832 | tf_op jit(solution)/shard_map/ppermute | solution.py:368
  76.2 24.2 %collective-permute-start.34 = (bf16[128,2048]{1,0:T(8,128)(2,1)S(1)}, bf16[128,2048]{1,0:T(8,128)(2,1)S(1)}, u32[]{:S(2)}, u32[]{:S(2)}) collective-permute-start(bf16[128,2048]{1,0:T(8,128)(2,1)S(1)} %get-tuple-element.111.x_ref.refs_10_), channel_id=1, source_target_pairs={{0,4},{1,5},{2,6},{3,7},{4,0},{5,1},{6,2},{7,3},{8,12},{9,13},{10,... | collective-permute-start | bytes 1572872 | tf_op jit(solution)/shard_map/ppermute | solution.py:368
  99.3 25.6 %collective-permute-start.18 = (bf16[48,2048]{1,0:T(8,128)(2,1)S(1)}, bf16[48,2048]{1,0:T(8,128)(2,1)S(1)}, u32[]{:S(2)}, u32[]{:S(2)}) collective-permute-start(bf16[48,2048]{1,0:T(8,128)(2,1)S(1)} %get-tuple-element.80), channel_id=1, source_target_pairs={{0,4},{1,5},{2,6},{3,7},{4,0},{5,1},{6,2},{7,3},{8,12},{9,13},{10,... | collective-permute-start | bytes 589832 | tf_op jit(solution)/shard_map/ppermute | solution.py:368
  100.4 29.2 %collective-permute-start.19 = (bf16[48,2048]{1,0:T(8,128)(2,1)S(1)}, bf16[48,2048]{1,0:T(8,128)(2,1)S(1)}, u32[]{:S(2)}, u32[]{:S(2)}) collective-permute-start(bf16[48,2048]{1,0:T(8,128)(2,1)S(1)} %get-tuple-element.81), channel_id=1, source_target_pairs={{0,5},{1,4},{2,7},{3,6},{4,1},{5,0},{6,3},{7,2},{8,13},{9,12},{10,... | collective-permute-start | bytes 589832 | tf_op jit(solution)/shard_map/ppermute | solution.py:368
  102.5 27.0 %collective-permute-start.20 = (bf16[48,2048]{1,0:T(8,128)(2,1)S(1)}, bf16[48,2048]{1,0:T(8,128)(2,1)S(1)}, u32[]{:S(2)}, u32[]{:S(2)}) collective-permute-start(bf16[48,2048]{1,0:T(8,128)(2,1)S(1)} %get-tuple-element.82), channel_id=1, source_target_pairs={{0,6},{1,7},{2,4},{3,5},{4,2},{5,3},{6,0},{7,1},{8,14},{9,15},{10,... | collective-permute-start | bytes 589832 | tf_op jit(solution)/shard_map/ppermute | solution.py:368
  106.5 24.2 %collective-permute-start.21 = (bf16[48,2048]{1,0:T(8,128)(2,1)}, bf16[48,2048]{1,0:T(8,128)(2,1)}, u32[]{:S(2)}, u32[]{:S(2)}) collective-permute-start(bf16[48,2048]{1,0:T(8,128)(2,1)} %get-tuple-element.83), channel_id=1, source_target_pairs={{0,7},{1,6},{2,5},{3,4},{4,3},{5,2},{6,1},{7,0},{8,15},{9,14},{10,... | collective-permute-start | bytes 589832 | tf_op jit(solution)/shard_map/ppermute | solution.py:368
  114.9 28.6 %collective-permute-start.31 = (bf16[48,2048]{1,0:T(8,128)(2,1)}, bf16[48,2048]{1,0:T(8,128)(2,1)}, u32[]{:S(2)}, u32[]{:S(2)}) collective-permute-start(bf16[48,2048]{1,0:T(8,128)(2,1)} %get-tuple-element.93), channel_id=1, source_target_pairs={{0,1},{1,0},{2,3},{3,2},{4,5},{5,4},{6,7},{7,6},{8,9},{9,8},{10,11... | collective-permute-start | bytes 589832 | tf_op jit(solution)/shard_map/ppermute | solution.py:368
  124.9 19.5 %collective-permute-start.32 = (bf16[48,2048]{1,0:T(8,128)(2,1)}, bf16[48,2048]{1,0:T(8,128)(2,1)}, u32[]{:S(2)}, u32[]{:S(2)}) collective-permute-start(bf16[48,2048]{1,0:T(8,128)(2,1)} %get-tuple-element.94), channel_id=1, source_target_pairs={{0,2},{1,3},{2,0},{3,1},{4,6},{5,7},{6,4},{7,5},{8,10},{9,11},{10,... | collective-permute-start | bytes 589832 | tf_op jit(solution)/shard_map/ppermute | solution.py:368
  147.3 21.7 %collective-permute-start.26 = (bf16[48,2048]{1,0:T(8,128)(2,1)S(1)}, bf16[48,2048]{1,0:T(8,128)(2,1)S(1)}, u32[]{:S(2)}, u32[]{:S(2)}) collective-permute-start(bf16[48,2048]{1,0:T(8,128)(2,1)S(1)} %get-tuple-element.87), channel_id=1, source_target_pairs={{0,27},{1,26},{2,25},{3,24},{4,31},{5,30},{6,29},{7,28},{8,3},{9,2... | collective-permute-start | bytes 589832 | tf_op jit(solution)/shard_map/ppermute | solution.py:379
  153.2 25.0 %collective-permute-start.27 = (bf16[48,2048]{1,0:T(8,128)(2,1)S(1)}, bf16[48,2048]{1,0:T(8,128)(2,1)S(1)}, u32[]{:S(2)}, u32[]{:S(2)}) collective-permute-start(bf16[48,2048]{1,0:T(8,128)(2,1)S(1)} %get-tuple-element.88), channel_id=1, source_target_pairs={{0,28},{1,29},{2,30},{3,31},{4,24},{5,25},{6,26},{7,27},{8,4},{9,5... | collective-permute-start | bytes 589832 | tf_op jit(solution)/shard_map/ppermute | solution.py:379
  153.2 29.2 %collective-permute-start.28 = (bf16[48,2048]{1,0:T(8,128)(2,1)S(1)}, bf16[48,2048]{1,0:T(8,128)(2,1)S(1)}, u32[]{:S(2)}, u32[]{:S(2)}) collective-permute-start(bf16[48,2048]{1,0:T(8,128)(2,1)S(1)} %get-tuple-element.89), channel_id=1, source_target_pairs={{0,29},{1,28},{2,31},{3,30},{4,25},{5,24},{6,27},{7,26},{8,5},{9,4... | collective-permute-start | bytes 589832 | tf_op jit(solution)/shard_map/ppermute | solution.py:379
  155.9 26.6 %collective-permute-start.29 = (bf16[48,2048]{1,0:T(8,128)(2,1)S(1)}, bf16[48,2048]{1,0:T(8,128)(2,1)S(1)}, u32[]{:S(2)}, u32[]{:S(2)}) collective-permute-start(bf16[48,2048]{1,0:T(8,128)(2,1)S(1)} %get-tuple-element.90), channel_id=1, source_target_pairs={{0,30},{1,31},{2,28},{3,29},{4,26},{5,27},{6,24},{7,25},{8,6},{9,7... | collective-permute-start | bytes 589832 | tf_op jit(solution)/shard_map/ppermute | solution.py:379
  155.9 26.6 %collective-permute-start.30 = (bf16[48,2048]{1,0:T(8,128)(2,1)S(1)}, bf16[48,2048]{1,0:T(8,128)(2,1)S(1)}, u32[]{:S(2)}, u32[]{:S(2)}) collective-permute-start(bf16[48,2048]{1,0:T(8,128)(2,1)S(1)} %get-tuple-element.91), channel_id=1, source_target_pairs={{0,31},{1,30},{2,29},{3,28},{4,27},{5,26},{6,25},{7,24},{8,7},{9,6... | collective-permute-start | bytes 589832 | tf_op jit(solution)/shard_map/ppermute | solution.py:379
  169.0 58.9 %collective-permute-start.45 = (bf16[128,2048]{1,0:T(8,128)(2,1)S(1)}, bf16[128,2048]{1,0:T(8,128)(2,1)S(1)}, u32[]{:S(2)}, u32[]{:S(2)}) collective-permute-start(bf16[128,2048]{1,0:T(8,128)(2,1)S(1)} %get-tuple-element.110.refs_14_), channel_id=1, source_target_pairs={{0,24},{1,25},{2,26},{3,27},{4,28},{5,29},{6,30},{7,31},{8,0},{9,1... | collective-permute-start | bytes 1572872 | tf_op jit(solution)/shard_map/ppermute | solution.py:379
  189.0 19.9 %collective-permute-start.39 = (bf16[48,2048]{1,0:T(8,128)(2,1)S(1)}, bf16[48,2048]{1,0:T(8,128)(2,1)S(1)}, u32[]{:S(2)}, u32[]{:S(2)}) collective-permute-start(bf16[48,2048]{1,0:T(8,128)(2,1)S(1)} %get-tuple-element.104), channel_id=1, source_target_pairs={{0,2},{1,3},{2,0},{3,1},{4,6},{5,7},{6,4},{7,5},{8,10},{9,11},{10,... | collective-permute-start | bytes 589832 | tf_op jit(solution)/shard_map/ppermute | solution.py:368
  197.2 25.5 %collective-permute-start.41 = (bf16[48,2048]{1,0:T(8,128)(2,1)S(1)}, bf16[48,2048]{1,0:T(8,128)(2,1)S(1)}, u32[]{:S(2)}, u32[]{:S(2)}) collective-permute-start(bf16[48,2048]{1,0:T(8,128)(2,1)S(1)} %get-tuple-element.106), channel_id=1, source_target_pairs={{0,4},{1,5},{2,6},{3,7},{4,0},{5,1},{6,2},{7,3},{8,12},{9,13},{10,... | collective-permute-start | bytes 589832 | tf_op jit(solution)/shard_map/ppermute | solution.py:368
  200.0 27.8 %collective-permute-start.42 = (bf16[48,2048]{1,0:T(8,128)(2,1)S(1)}, bf16[48,2048]{1,0:T(8,128)(2,1)S(1)}, u32[]{:S(2)}, u32[]{:S(2)}) collective-permute-start(bf16[48,2048]{1,0:T(8,128)(2,1)S(1)} %get-tuple-element.107), channel_id=1, source_target_pairs={{0,5},{1,4},{2,7},{3,6},{4,1},{5,0},{6,3},{7,2},{8,13},{9,12},{10,... | collective-permute-start | bytes 589832 | tf_op jit(solution)/shard_map/ppermute | solution.py:368
  (42 other events, 546.4 us)
